TPU v7x, 128 devices: a whole 4x4x4 slice. The times are simulated.
128 devices in a mesh: samples: 8 (over y, x_hi), space: 16 (over x_lo, z, core).
Axes of the slice: x: 4 (x_hi: 2, x_lo: 2; x = x_hi * 2 + x_lo), y: 4, z: 4, core: 2. Of those that a mesh axis runs over, the one named last changes fastest.
Arguments:
- target: bfloat16 [8, 16384, 8192], P(None, 'samples', 'space'), may hold values from 0 to 1
- a_factor: bfloat16 [16384, 256], P(('samples', 'space')), may hold values from -3 to 3
- b_factor: bfloat16 [8192, 256], P(('space', 'samples')), may hold values from -3 to 3
- c_factor: bfloat16 [8, 256], replicated, may hold values from -3 to 3
Outputs:
- grad_a: float32 [16384, 256], P(('samples', 'space'))
- grad_b: float32 [8192, 256], P(('space', 'samples'))
- grad_c: float32 [8, 256], replicated
All inputs are finite; a program needn't handle non-finite values.
Results may differ from a plain program's by a relative error of at most 0.002.
Values may be sent and summed in bfloat16 or wider, within the bound.
No kernel may reach another device: no remote copies, remote signals or barrier semaphores. Data moves between devices by JAX's collectives and lax.ppermute only.
A program may use at most 128 MiB of HBM per device.

v0:
```python
import jax
import jax.numpy as jnp
from jax import lax
from jax.sharding import PartitionSpec as P


def on_device(target, a_factor, b_factor, c_factor):
    a_full = lax.all_gather(a_factor, "space", axis=0, tiled=True)
    b_full = lax.all_gather(b_factor, "samples", axis=0, tiled=True)
    c_wide = c_factor.astype(jnp.float32)
    scaled = (c_wide[:, None, :] * a_full.astype(jnp.float32)[None]).astype(jnp.bfloat16)
    model = jnp.einsum("kir,jr->kij", scaled, b_full, preferred_element_type=jnp.float32)
    derivative = (jax.nn.sigmoid(model) - target.astype(jnp.float32)).astype(jnp.bfloat16)
    weighted = jnp.einsum("kij,ir->kjr", derivative, a_full, preferred_element_type=jnp.float32)
    b_part = jnp.sum(weighted * c_wide[:, None, :], axis=0)
    c_part = jnp.sum(weighted * b_full.astype(jnp.float32)[None], axis=1)
    own_a = a_factor.shape[0]
    own_b = b_factor.shape[0]
    inner = jnp.einsum("kij,jr->kir", derivative, b_full, preferred_element_type=jnp.float32)
    whole_a = lax.psum(jnp.sum(inner * c_wide[:, None, :], axis=0), "space")
    grad_a = lax.dynamic_slice_in_dim(whole_a, lax.axis_index("space") * own_a, own_a, 0)
    whole_b = lax.psum(b_part, "samples")
    grad_b = lax.dynamic_slice_in_dim(whole_b, lax.axis_index("samples") * own_b, own_b, 0)
    grad_c = lax.psum(c_part, ("samples", "space"))
    return (grad_a, grad_b, grad_c)


def solution(mesh):
    return jax.shard_map(
        on_device,
        mesh=mesh,
        in_specs=(
            P(None, "samples", "space"),
            P(("samples", "space"), None),
            P(("space", "samples"), None),
            P(),
        ),
        out_specs=(P(("samples", "space"), None), P(("space", "samples"), None), P()),
        check_vma=False,
    )
```

profile of v0, /device:TPU:0, one launch (start us, length us, event | category | flops | bytes accessed | tf_op | source)
XLA Modules:
  0.0 294.4 jit_solution(3848630474228114266)
XLA Ops:
  7.2 0.0 all-gather.2.cloned.1.call-start
  7.2 0.7 all-gather.2.cloned.1.call-update
  7.9 0.0 all-reduce.5.cloned.1.call-start
  7.9 0.7 convert_element_type.18
  8.6 35.8 %all_gather.7 = bf16[512,256]{1,0:T(8,128)(2,1)S(1)} all-gather(bf16[64,256]{1,0:T(8,128)(2,1)} %param.6), channel_id=1, replica_groups=mesh['samples'=8,'space'=16] {'samples'}, dimensions={0}, use_global_device_ids=true | all-gather | bytes 294912 | tf_op jit(solution)/shard_map/all_gather | solution.py:9
  44.4 0.4 all-gather.2.cloned.1.call-done
  44.8 1.4 convert_element_type.19
  46.2 0.0 copy-start
  46.2 17.1 %subtract_convert_fusion = bf16[8,2048,512]{2,1,0:T(8,128)(2,1)} fusion(bf16[8,2048,512]{2,1,0:T(8,128)(2,1)} %param.4, f32[2048,256]{1,0:T(8,128)S(1)} %convert_element_type.19, f32[8,256]{1,0:T(8,128)S(1)} %convert_element_type.18, bf16[512,256]{1,0:T(8,128)(2,1)S(1)} %all_gather.7), kind=kOutput, calls=%fused_computation | convolution fusion | flops 4353687552 | bytes 35921920 | tf_op jit(solution)/shard_map/kir,jr->kij/dot_general | solution.py:12
  63.3 0.0 copy-done
  63.3 11.7 %multiply_reduce_fusion.1 = (f32[8,256]{1,0:T(8,128)S(1)}, f32[512,256]{1,0:T(8,128)}) fusion(f32[512,256]{1,0:T(8,128)S(1)} %convert_element_type.23, f32[8,256]{1,0:T(8,128)S(1)} %convert_element_type.18, bf16[8,2048,512]{2,1,0:T(8,128)(2,1)} %subtract_convert_fusion, bf16[2048,256]{1,0:T(8,128)(2,1)S(1)} %copy-done), kind=kOutput, calls=%fused_computation.5 | convolution fusion | flops 4299028480 | bytes 18890752 | tf_op jit(solution)/shard_map/kij,ir->kjr/dot_general | solution.py:14
  75.0 0.0 all-reduce.5.cloned.1.call-update
  75.0 0.2 all-reduce.3.cloned.1.call-start
  75.3 11.8 %multiply_reduce_fusion = f32[2048,256]{1,0:T(8,128)} fusion(f32[8,256]{1,0:T(8,128)S(1)} %convert_element_type.18, bf16[8,2048,512]{2,1,0:T(8,128)(2,1)} %subtract_convert_fusion, bf16[512,256]{1,0:T(8,128)(2,1)S(1)} %all_gather.7), kind=kOutput, calls=%fused_computation.1 | convolution fusion | flops 4302831616 | bytes 19144704 | tf_op jit(solution)/shard_map/kij,jr->kir/dot_general | solution.py:19
  87.1 0.0 all-reduce.3.cloned.1.call-update
  87.1 67.6 %psum.23 = f32[8,256]{1,0:T(8,128)} all-reduce(f32[8,256]{1,0:T(8,128)S(1)} %get-tuple-element.3), channel_id=1, replica_groups=mesh['samples'=8,'space'=16] {'samples','space'}, use_global_device_ids=true, to_apply=%region_5.0 | all-reduce | flops 2048 | bytes 16384 | tf_op jit(solution)/shard_map/psum | solution.py:24
  154.7 8.0 %all-reduce.5.cloned.1.call-done = f32[512,256]{1,0:T(8,128)} async-done(((f32[512,256]{1,0:T(8,128)}), f32[512,256]{1,0:T(8,128)}) %all-reduce.5.cloned.1.call-update) | async-done | bytes 524304 | tf_op jit(solution)/shard_map/psum | solution.py:22
  162.7 1.5 constant_dynamic-slice_fusion
  164.2 122.2 %all-reduce.3.cloned.1.call-done = f32[2048,256]{1,0:T(8,128)} async-done(((f32[2048,256]{1,0:T(8,128)}), f32[2048,256]{1,0:T(8,128)}) %all-reduce.3.cloned.1.call-update) | async-done | bytes 2097168 | tf_op jit(solution)/shard_map/psum | solution.py:20
  286.3 1.6 constant_dynamic-slice_fusion.1
  (1 shorter events, 0.0 us)
Async XLA Ops:
  7.2 37.7 %all-gather.2.cloned.1.call-start = ((), (), s32[]{:S(2)}) async-start(), calls=%async_computation | async-start | bytes 1114112 | tf_op jit(solution)/shard_map/all_gather | solution.py:8
  7.9 154.8 %all-reduce.5.cloned.1.call-start = ((), (), s32[]{:S(2)}) async-start(), calls=%async_computation.2 | async-start | bytes 1048576 | tf_op jit(solution)/shard_map/psum | solution.py:22
  46.2 17.1 %copy-start = (bf16[2048,256]{1,0:T(8,128)(2,1)S(1)}, bf16[2048,256]{1,0:T(8,128)(2,1)}, u32[]{:S(2)}) copy-start(bf16[2048,256]{1,0:T(8,128)(2,1)} %all-gather.2.cloned.1.call-done) | copy-start | bytes 3145732
  75.0 211.3 %all-reduce.3.cloned.1.call-start = ((), (), s32[]{:S(2)}) async-start(), calls=%async_computation.1 | async-start | bytes 4194304 | tf_op jit(solution)/shard_map/psum | solution.py:20
Sparse Core Ops, SparseCore 0:
  9.7 35.0 all-gather.1
  75.2 87.4 all-reduce.4
  165.4 120.9 all-reduce.2
where the time goes:
time: 295 us; the launch traced here: 294 us
  waiting for transfers between devices  131 us (44%)
  blocking collectives  103 us (35%)
  matrix products  40.6 us (14%)
  between operations  13.8 us (5%)
  local copies, waits for them, and re-layouts  3.04 us (1%)
    psum x1, waiting for transfers between devices, on_device(): whole_a = lax.psum(jnp.sum(inner * c_wide[:, None, :], axis=0), 'space')  122 us
    psum x1, blocking collectives, on_device(): grad_c = lax.psum(c_part, ('samples', 'space'))  67.6 us
    all_gather x1, blocking collectives, on_device(): b_full = lax.all_gather(b_factor, 'samples', axis=0, tiled=True)  35.8 us
    dot_general x1, matrix products, on_device(): jnp.einsum('kir,jr->kij', scaled, b_full, preferred_element_type=jnp.floa...  17.1 us
    dot_general x1, matrix products, on_device(): jnp.einsum('kij,jr->kir', derivative, b_full, preferred_element_type=jnp....  11.8 us
    dot_general x1, matrix products, on_device(): jnp.einsum('kij,ir->kjr', derivative, a_full, preferred_element_type=jnp....  11.7 us
    psum x1, waiting for transfers between devices, on_device(): whole_b = lax.psum(b_part, 'samples')  8.01 us
  transfers between devices with their start and end apart: 3, of which 3 were waited for; matrix products, arithmetic and copies ran while one was open for 5% of the time, Pallas kernels for 0%

commit v1 on v0

v1 whole, which is shorter than its diff:
```python
import jax
import jax.numpy as jnp
from jax import lax
from jax.experimental import pallas as pl
from jax.experimental.pallas import tpu as pltpu
from jax.sharding import PartitionSpec as P

F32 = jnp.float32
BF16 = jnp.bfloat16
K, R = 8, 256
SHARD = 128
NJ = 512
XL, Z, CORE = 2, 4, 2

SPACE = range(XL * Z * CORE)
SAME_CORE = [[2 * g + c for g in range(XL * Z)] for c in range(CORE)]
TO_CORE = [(p, p ^ 1) for p in SPACE]
TO_XL = [(p, p ^ 8) for p in SPACE]


def from_z(d):
    return [((p & 9) | ((((p >> 1) + d) % 4) << 1), p) for p in SPACE]


def dot_last(x, y):
    return lax.dot_general(x, y, (((1,), (1,)), ((), ())), preferred_element_type=F32)


def dot(x, y):
    return jnp.dot(x, y, preferred_element_type=F32)


def body(table, t0, t1, t2, t3, a_ref, b_ref, ch_ref, cht_ref, bt_ref, same_ref, other_ref, gb_ref, gc_ref, w_ref):
    step = pl.program_id(0)
    rows = a_ref[0]
    wide = rows.astype(F32)
    rows_t = rows.T
    b = b_ref[...]
    grad = jnp.zeros((4 * SHARD, R), F32)
    for k in range(K):
        ck = ch_ref[k : k + 1, :]
        half = dot_last((wide * ck).astype(BF16), b)
        t = jnp.concatenate([r[k, 0] for r in (t0, t1, t2, t3)], axis=0).astype(F32)
        d2 = ((jnp.tanh(half) + 1.0) - (t + t)).astype(BF16)
        grad = grad + dot(d2, b) * ck
        part = dot(rows_t, d2)
        w_ref[k] = jnp.where(step > 0, w_ref[k], 0.0) + part

    xl = table[16]
    for dx in range(2):
        at = lax.bitwise_xor(xl, dx)
        same_ref[at, 0] = grad[dx * SHARD : (dx + 1) * SHARD]
        other_ref[at, 0] = grad[(2 + dx) * SHARD : (3 + dx) * SHARD]

    @pl.when(step == pl.num_programs(0) - 1)
    def _():
        total = jnp.zeros((R, NJ), F32)
        lane = lax.broadcasted_iota(jnp.int32, (R, 128), 1)
        sums = jnp.zeros((R, 128), F32)
        bt = bt_ref[...].astype(F32)
        for k in range(K):
            wk = w_ref[k]
            total = total + wk * cht_ref[:, k : k + 1]
            s = jnp.sum(wk * bt, axis=1, keepdims=True) * 0.5
            sums = jnp.where(lane == k, s, sums)
        gb_ref[...] = total.T
        gc_ref[...] = sums.T[:K]


def local(table, target, a_all, b_full, c_half):
    def tile(q):
        return pl.BlockSpec((K, 1, SHARD, NJ), lambda s, tab: (0, tab[s * 4 + q], 0, 0))

    def whole(*shape):
        return pl.BlockSpec(shape, lambda s, tab: (0,) * len(shape))

    out = pl.BlockSpec((XL, 1, SHARD, R), lambda s, tab: (0, tab[17 + s], 0, 0))
    return pl.pallas_call(
        body,
        grid_spec=pltpu.PrefetchScalarGridSpec(
            num_scalar_prefetch=1,
            grid=(Z,),
            in_specs=[tile(0), tile(1), tile(2), tile(3),
                      pl.BlockSpec((1, 4 * SHARD, R), lambda s, tab: (s, 0, 0)),
                      whole(NJ, R), whole(K, R), whole(R, K), whole(R, NJ)],
            out_specs=[out, out, whole(NJ, R), whole(K, R)],
            scratch_shapes=[pltpu.VMEM((K, R, NJ), F32)],
        ),
        out_shape=[jax.ShapeDtypeStruct((XL, Z, SHARD, R), F32)] * 2
        + [jax.ShapeDtypeStruct((NJ, R), F32), jax.ShapeDtypeStruct((K, R), F32)],
        compiler_params=pltpu.CompilerParams(vmem_limit_bytes=56 << 20),
        cost_estimate=pl.CostEstimate(flops=12_900_000_000, bytes_accessed=22_000_000, transcendentals=8_400_000),
        name="fused",
    )(table, target, target, target, target, a_all, b_full, c_half, c_half.T, b_full.T)


def on_device(target, a_factor, b_factor, c_factor):
    p = lax.axis_index("space")
    xl, z, core = p >> 3, (p >> 1) & 3, p & 1
    b_full = lax.all_to_all(jnp.broadcast_to(b_factor[None], (8, 64, R)), "samples", 0, 0).reshape(NJ, R)
    a_x = lax.ppermute(a_factor, "space", TO_XL)
    pair = jnp.concatenate([a_factor, a_x], axis=0)
    mine = [pair] + [lax.ppermute(pair, "space", from_z(d)) for d in (1, 2, 3)]
    theirs = [lax.ppermute(m, "space", TO_CORE) for m in mine]
    a_all = jnp.stack([jnp.concatenate([m, t], axis=0) for m, t in zip(mine, theirs)])
    dz, dc, dx = jnp.meshgrid(jnp.arange(4), jnp.arange(2), jnp.arange(2), indexing="ij")
    slots = ((xl ^ dx) * 8 + ((z + dz) & 3) * 2 + (core ^ dc)).reshape(16)
    table = jnp.concatenate([slots, xl[None], (z + jnp.arange(4)) & 3]).astype(jnp.int32)
    c_half = c_factor.astype(F32) * 0.5
    same, other, gb, gc = local(table, target.reshape(K, 16, SHARD, NJ), a_all, b_full, c_half)

    first = jnp.concatenate([gb.reshape(8, 64, R), jnp.broadcast_to(gc[None], (8, K, R))], axis=1)
    first = jnp.sum(lax.all_to_all(first, "samples", 0, 0), axis=0)
    grad_b, gc = first[:64], first[64:]
    gc = gc + lax.ppermute(gc, "space", TO_CORE)
    same = (same + lax.ppermute(other, "space", TO_CORE)).reshape(8, SHARD, R)
    second = jnp.concatenate([same, jnp.broadcast_to(gc[None], (8, K, R))], axis=1)
    second = jnp.sum(lax.all_to_all(second, "space", 0, 0, axis_index_groups=SAME_CORE), axis=0)
    return second[:SHARD], grad_b, second[SHARD:]


def solution(mesh):
    return jax.shard_map(
        on_device,
        mesh=mesh,
        in_specs=(
            P(None, "samples", "space"),
            P(("samples", "space"), None),
            P(("space", "samples"), None),
            P(),
        ),
        out_specs=(P(("samples", "space"), None), P(("space", "samples"), None), P()),
        check_vma=False,
    )
```

time: 295 us -> 93.1 us (0.32)
  waiting for transfers between devices: 131 us -> 19.7 us
  blocking collectives: 103 us -> 19.6 us
  matrix products: 40.6 us -> 0 us
  Pallas kernels: 0 us -> 20.1 us
  starting transfers between devices: 0.3 us -> 19.4 us
  between operations: 13.8 us -> 0.78 us
  local copies, waits for them, and re-layouts: 3.04 us -> 7.33 us
    psum x2 -> x0, waiting for transfers between devices: 130 us -> none  [the longest x1 122 us: on_device(): whole_a = lax.psum(jnp.sum(inner * c_wide[:, None, :], axis=0), 'space')]
    psum x1 -> x0, blocking collectives: 67.6 us -> none  [on_device(): grad_c = lax.psum(c_part, ('samples', 'space'))]
    dot_general x3 -> x0, matrix products: 40.6 us -> none  [the longest x1 17.1 us: on_device(): jnp.einsum('kir,jr->kij', scaled, b_full, preferred_element_type=jnp.floa...]
    all_gather x1 -> x0, blocking collectives: 35.8 us -> none  [on_device(): b_full = lax.all_gather(b_factor, 'samples', axis=0, tiled=True)]
    pallas_call x0 -> x1, Pallas kernels: none -> 20.1 us  [local(): pl.pallas_call(body, grid_spec=pltpu.PrefetchScalarGridSpec(num_scalar_pr...]
    all_to_all x0 -> x1, blocking collectives: none -> 19.6 us  [on_device(): first = jnp.sum(lax.all_to_all(first, 'samples', 0, 0), axis=0)]
    all_to_all x0 -> x2, waiting for transfers between devices: none -> 15.4 us  [the longest x1 15.4 us: on_device(): lax.all_to_all(second, 'space', 0, 0, axis_index_groups=SAME_CORE)]
    all_to_all x0 -> x2, starting transfers between devices: none -> 10.2 us  [the longest x1 6.64 us: on_device(): lax.all_to_all(jnp.broadcast_to(b_factor[None], (8, 64, R)), 'samples', 0...]
  transfers between devices with their start and end apart: 3 -> 12, of which waited for: 3 -> 5; matrix products, arithmetic and copies ran while one was open for 5% -> 9% of each run, Pallas kernels for 0% -> 0%
where the time goes in v1:
time: 93.1 us; the launch traced here: 91.9 us
  Pallas kernels  20.1 us (22%)
  waiting for transfers between devices  19.7 us (21%)
  blocking collectives  19.6 us (21%)
  starting transfers between devices  19.4 us (21%)
  local copies, waits for them, and re-layouts  7.33 us (8%)
  other arithmetic  4.95 us (5%)
    pallas_call x1, Pallas kernels, local(): pl.pallas_call(body, grid_spec=pltpu.PrefetchScalarGridSpec(num_scalar_pr...  20.1 us
    all_to_all x1, blocking collectives, on_device(): first = jnp.sum(lax.all_to_all(first, 'samples', 0, 0), axis=0)  19.6 us
    all_to_all x1, waiting for transfers between devices, on_device(): lax.all_to_all(second, 'space', 0, 0, axis_index_groups=SAME_CORE)  15.4 us
    all_to_all x1, starting transfers between devices, on_device(): lax.all_to_all(jnp.broadcast_to(b_factor[None], (8, 64, R)), 'samples', 0...  6.64 us
    ppermute x3, starting transfers between devices, on_device(): mine = [pair] + [lax.ppermute(pair, 'space', from_z(d)) for d in (1, 2, 3)]  6.59 us
    all_to_all x1, starting transfers between devices, on_device(): lax.all_to_all(second, 'space', 0, 0, axis_index_groups=SAME_CORE)  3.56 us
    ppermute x3, waiting for transfers between devices, on_device(): mine = [pair] + [lax.ppermute(pair, 'space', from_z(d)) for d in (1, 2, 3)]  3.05 us
  transfers between devices with their start and end apart: 12, of which 5 were waited for; matrix products, arithmetic and copies ran while one was open for 9% of the time, Pallas kernels for 0%

profile of v1, /device:TPU:0, one launch (start us, length us, event | category | flops | bytes accessed | tf_op | source)
XLA Modules:
  0.0 91.9 jit_solution(10904321217716549487)
XLA Ops:
  0.6 0.0 copy-start.2
  0.6 1.7 %collective-permute-start = (bf16[128,256]{1,0:T(8,128)(2,1)}, bf16[128,256]{1,0:T(8,128)(2,1)S(1)}, u32[]{:S(2)}, u32[]{:S(2)}) collective-permute-start(bf16[128,256]{1,0:T(8,128)(2,1)} %param.5), channel_id=1, source_target_pairs={{0,8},{1,9},{2,10},{3,11},{4,12},{5,13},{6,14},{7,15},{8,0},{9,1},... | collective-permute-start | bytes 196616 | tf_op jit(solution)/shard_map/ppermute | solution.py:101
  2.3 1.5 %broadcast_in_dim.34 = bf16[8,64,256]{2,1,0:T(8,128)(2,1)} broadcast(bf16[64,256]{1,0:T(8,128)(2,1)} %param.6), dimensions={1,2} | broadcast | bytes 294912 | tf_op jit(solution)/shard_map/broadcast_in_dim | solution.py:100
  3.8 6.6 %all-to-all-start = ((bf16[8,64,256]{2,1,0:T(8,128)(2,1)}), bf16[8,64,256]{2,1,0:T(8,128)(2,1)S(1)}, u32[]{:S(2)}, u32[]{:S(2)}) async-start(bf16[8,64,256]{2,1,0:T(8,128)(2,1)} %broadcast_in_dim.34), calls=%async_computation | async-start | bytes 524288 | tf_op jit(solution)/shard_map/all_to_all | solution.py:100
  10.4 0.8 constant_dynamic-update-slice_fusion.1
  11.3 0.8 copy.14
  12.0 0.7 fusion
  12.7 0.0 collective-permute-done
  12.7 2.0 %collective-permute-start.6 = (bf16[256,256]{1,0:T(8,128)(2,1)S(1)}, bf16[256,256]{1,0:T(8,128)(2,1)S(1)}, u32[]{:S(2)}, u32[]{:S(2)}) collective-permute-start(bf16[256,256]{1,0:T(8,128)(2,1)S(1)} %constant_dynamic-update-slice_fusion), channel_id=1, source_target_pairs={{6,0},{7,1},{0,2},{1,3},{2,4},{3,5},{4,6},{5,7},{14,8},{15,9},{8,1... | collective-permute-start | bytes 393224 | tf_op jit(solution)/shard_map/ppermute | solution.py:103
  14.7 0.1 add_add_fusion
  14.8 3.6 %collective-permute-start.4 = (bf16[256,256]{1,0:T(8,128)(2,1)S(1)}, bf16[256,256]{1,0:T(8,128)(2,1)S(1)}, u32[]{:S(2)}, u32[]{:S(2)}) collective-permute-start(bf16[256,256]{1,0:T(8,128)(2,1)S(1)} %constant_dynamic-update-slice_fusion), channel_id=1, source_target_pairs={{4,0},{5,1},{6,2},{7,3},{0,4},{1,5},{2,6},{3,7},{12,8},{13,9},{14,... | collective-permute-start | bytes 393224 | tf_op jit(solution)/shard_map/ppermute | solution.py:103
  18.4 1.0 %collective-permute-start.2 = (bf16[256,256]{1,0:T(8,128)(2,1)S(1)}, bf16[256,256]{1,0:T(8,128)(2,1)S(1)}, u32[]{:S(2)}, u32[]{:S(2)}) collective-permute-start(bf16[256,256]{1,0:T(8,128)(2,1)S(1)} %constant_dynamic-update-slice_fusion), channel_id=1, source_target_pairs={{2,0},{3,1},{4,2},{5,3},{6,4},{7,5},{0,6},{1,7},{10,8},{11,9},{12,... | collective-permute-start | bytes 393224 | tf_op jit(solution)/shard_map/ppermute | solution.py:103
  19.4 0.0 collective-permute-start.1
  19.4 0.1 add.31
  19.5 0.9 collective-permute-done.6
  20.4 0.0 collective-permute-start.7
  20.4 0.6 pad_add_fusion.table
  21.0 0.7 copy.17.ch_ref
  21.6 2.2 %collective-permute-done.4 = bf16[256,256]{1,0:T(8,128)(2,1)S(1)} collective-permute-done((bf16[256,256]{1,0:T(8,128)(2,1)S(1)}, bf16[256,256]{1,0:T(8,128)(2,1)S(1)}, u32[]{:S(2)}, u32[]{:S(2)}) %collective-permute-start.4) | collective-permute-done | bytes 131104 | tf_op jit(solution)/shard_map/ppermute | solution.py:103
  23.8 0.0 collective-permute-start.5
  23.8 0.0 collective-permute-done.2
  23.8 0.5 collective-permute-start.3
  24.3 0.0 collective-permute-done.1
  24.3 0.0 copy-done.2
  24.3 0.0 all-to-all-done
  24.3 0.0 copy-start
  24.3 0.8 copy.16
  25.2 0.0 collective-permute-done.7
  25.2 0.0 collective-permute-done.5
  25.2 0.1 collective-permute-done.3
  25.3 1.1 %pad_maximum_fusion.1.a_ref = bf16[4,512,256]{2,1,0:T(8,128)(2,1)} fusion(bf16[1,512,256]{2,1,0:T(8,128)(2,1)S(1)} %maximum_bitcast_fusion.3, bf16[1,512,256]{2,1,0:T(8,128)(2,1)S(1)} %maximum_bitcast_fusion.2, bf16[1,512,256]{2,1,0:T(8,128)(2,1)S(1)} %maximum_bitcast_fusion.1, bf16[1,512,256]{2,1,0:T(8,128)(2,1)S(1)} %maximum_bitcast_fusion), kind=kLoop, calls=%fused_computation.1 | loop fusion | flops 1572864 | bytes 2097152 | tf_op jit(solution)/shard_map/stack | solution.py:105
  26.5 0.0 copy-done
  26.5 20.1 %fused.1 = (f32[2,4,128,256]{3,2,1,0:T(8,128)}, f32[2,4,128,256]{3,2,1,0:T(8,128)}, f32[512,256]{1,0:T(8,128)}, f32[8,256]{1,0:T(8,128)}) custom-call(s32[21]{0:T(128)} %pad_add_fusion.table, bf16[8,16,128,512]{3,2,1,0:T(8,128)(2,1)} %bitcast.16, bf16[8,16,128,512]{3,2,1,0:T(8,128)(2,1)} %bitcast.17, bf16[8,16,128,512]{3,2,1,0:T(8,128)(2,1)} %bitcast.18, ...), custom_call_target="tpu_custom_call" | custom-call | flops 12899999744 | bytes 22000000 | tf_op jit(solution)/shard_map/fused/pallas_call | solution.py:78
  46.5 0.4 collective-permute-start.8
  46.9 0.7 broadcast_in_dim.35
  47.6 1.1 %pad_maximum_fusion.2 = f32[8,72,256]{2,1,0:T(8,128)S(1)} fusion(f32[8,8,256]{2,1,0:T(8,128)S(1)} %broadcast_in_dim.35, f32[8,64,256]{2,1,0:T(8,128)} %bitcast.24), kind=kLoop, calls=%fused_computation.2 | loop fusion | flops 147456 | bytes 1179648 | tf_op jit(solution)/shard_map/concatenate | solution.py:112
  48.7 0.0 copy-start.1
  48.7 19.6 %all_to_all.15 = f32[8,72,256]{2,1,0:T(8,128)S(1)} all-to-all(f32[8,72,256]{2,1,0:T(8,128)S(1)} %pad_maximum_fusion.2), channel_id=1, replica_groups=mesh['samples'=8,'space'=16] {'samples'}, dimensions={0} | all-to-all | bytes 1179648 | tf_op jit(solution)/shard_map/all_to_all | solution.py:113
  68.4 0.1 collective-permute-start.9
  68.5 1.2 %collective-permute-done.9 = f32[8,256]{1,0:T(8,128)S(1)} collective-permute-done((f32[8,256]{1,0:T(8,128)S(1)}, f32[8,256]{1,0:T(8,128)S(1)}, u32[]{:S(2)}, u32[]{:S(2)}) %collective-permute-start.9) | collective-permute-done | bytes 8224 | tf_op jit(solution)/shard_map/ppermute | solution.py:115
  69.7 0.0 collective-permute-done.8
  69.7 0.0 copy-done.1
  69.7 0.1 add.32
  69.8 1.1 %pad_maximum_fusion = f32[8,136,256]{2,1,0:T(8,128)} fusion(f32[8,8,256]{2,1,0:T(8,128)S(1)} %broadcast_in_dim.36, f32[8,128,256]{2,1,0:T(8,128)S(1)} %bitcast.20), kind=kLoop, calls=%fused_computation | loop fusion | flops 278528 | bytes 2228224 | tf_op jit(solution)/shard_map/concatenate | solution.py:117
  70.9 3.6 %all-to-all-start.2 = ((f32[8,136,256]{2,1,0:T(8,128)}), f32[8,136,256]{2,1,0:T(8,128)S(1)}, u32[]{:S(2)}, u32[]{:S(2)}) async-start(f32[8,136,256]{2,1,0:T(8,128)} %pad_maximum_fusion), calls=%async_computation.2 | async-start | bytes 2228224 | tf_op jit(solution)/shard_map/all_to_all | solution.py:118
  74.5 0.6 slice.18
  75.1 15.4 %all-to-all-done.2 = f32[8,136,256]{2,1,0:T(8,128)S(1)} async-done(((f32[8,136,256]{2,1,0:T(8,128)}), f32[8,136,256]{2,1,0:T(8,128)S(1)}, u32[]{:S(2)}, u32[]{:S(2)}) %all-to-all-start.2) | async-done | bytes 1114144 | tf_op jit(solution)/shard_map/all_to_all | solution.py:118
  90.5 0.1 reduce_sum.19
  90.6 0.6 slice.19
  91.2 0.7 slice.17
  (12 shorter events, 0.1 us)
Async XLA Ops:
  0.6 23.7 %copy-start.2 = (bf16[128,256]{1,0:T(8,128)(2,1)S(1)}, bf16[128,256]{1,0:T(8,128)(2,1)}, u32[]{:S(2)}) copy-start(bf16[128,256]{1,0:T(8,128)(2,1)} %param.5) | copy-start | bytes 196612
  0.6 12.1 %collective-permute-start = (bf16[128,256]{1,0:T(8,128)(2,1)}, bf16[128,256]{1,0:T(8,128)(2,1)S(1)}, u32[]{:S(2)}, u32[]{:S(2)}) collective-permute-start(bf16[128,256]{1,0:T(8,128)(2,1)} %param.5), channel_id=1, source_target_pairs={{0,8},{1,9},{2,10},{3,11},{4,12},{5,13},{6,14},{7,15},{8,0},{9,1},... | collective-permute-start | bytes 196616 | tf_op jit(solution)/shard_map/ppermute | solution.py:101
  3.8 20.5 %all-to-all-start = ((bf16[8,64,256]{2,1,0:T(8,128)(2,1)}), bf16[8,64,256]{2,1,0:T(8,128)(2,1)S(1)}, u32[]{:S(2)}, u32[]{:S(2)}) async-start(bf16[8,64,256]{2,1,0:T(8,128)(2,1)} %broadcast_in_dim.34), calls=%async_computation | async-start | bytes 524288 | tf_op jit(solution)/shard_map/all_to_all | solution.py:100
  12.7 7.6 %collective-permute-start.6 = (bf16[256,256]{1,0:T(8,128)(2,1)S(1)}, bf16[256,256]{1,0:T(8,128)(2,1)S(1)}, u32[]{:S(2)}, u32[]{:S(2)}) collective-permute-start(bf16[256,256]{1,0:T(8,128)(2,1)S(1)} %constant_dynamic-update-slice_fusion), channel_id=1, source_target_pairs={{6,0},{7,1},{0,2},{1,3},{2,4},{3,5},{4,6},{5,7},{14,8},{15,9},{8,1... | collective-permute-start | bytes 393224 | tf_op jit(solution)/shard_map/ppermute | solution.py:103
  14.8 9.0 %collective-permute-start.4 = (bf16[256,256]{1,0:T(8,128)(2,1)S(1)}, bf16[256,256]{1,0:T(8,128)(2,1)S(1)}, u32[]{:S(2)}, u32[]{:S(2)}) collective-permute-start(bf16[256,256]{1,0:T(8,128)(2,1)S(1)} %constant_dynamic-update-slice_fusion), channel_id=1, source_target_pairs={{4,0},{5,1},{6,2},{7,3},{0,4},{1,5},{2,6},{3,7},{12,8},{13,9},{14,... | collective-permute-start | bytes 393224 | tf_op jit(solution)/shard_map/ppermute | solution.py:103
  18.4 5.4 %collective-permute-start.2 = (bf16[256,256]{1,0:T(8,128)(2,1)S(1)}, bf16[256,256]{1,0:T(8,128)(2,1)S(1)}, u32[]{:S(2)}, u32[]{:S(2)}) collective-permute-start(bf16[256,256]{1,0:T(8,128)(2,1)S(1)} %constant_dynamic-update-slice_fusion), channel_id=1, source_target_pairs={{2,0},{3,1},{4,2},{5,3},{6,4},{7,5},{0,6},{1,7},{10,8},{11,9},{12,... | collective-permute-start | bytes 393224 | tf_op jit(solution)/shard_map/ppermute | solution.py:103
  19.4 4.9 %collective-permute-start.1 = (bf16[256,256]{1,0:T(8,128)(2,1)S(1)}, bf16[256,256]{1,0:T(8,128)(2,1)S(1)}, u32[]{:S(2)}, u32[]{:S(2)}) collective-permute-start(bf16[256,256]{1,0:T(8,128)(2,1)S(1)} %constant_dynamic-update-slice_fusion), channel_id=1, source_target_pairs={{0,1},{1,0},{2,3},{3,2},{4,5},{5,4},{6,7},{7,6},{8,9},{9,8},{10,11... | collective-permute-start | bytes 393224 | tf_op jit(solution)/shard_map/ppermute | solution.py:104
  20.4 4.8 %collective-permute-start.7 = (bf16[256,256]{1,0:T(8,128)(2,1)S(1)}, bf16[256,256]{1,0:T(8,128)(2,1)S(1)}, u32[]{:S(2)}, u32[]{:S(2)}) collective-permute-start(bf16[256,256]{1,0:T(8,128)(2,1)S(1)} %collective-permute-done.6), channel_id=1, source_target_pairs={{0,1},{1,0},{2,3},{3,2},{4,5},{5,4},{6,7},{7,6},{8,9},{9,8},{10,11... | collective-permute-start | bytes 393224 | tf_op jit(solution)/shard_map/ppermute | solution.py:104
  23.8 1.4 %collective-permute-start.5 = (bf16[256,256]{1,0:T(8,128)(2,1)S(1)}, bf16[256,256]{1,0:T(8,128)(2,1)S(1)}, u32[]{:S(2)}, u32[]{:S(2)}) collective-permute-start(bf16[256,256]{1,0:T(8,128)(2,1)S(1)} %collective-permute-done.4), channel_id=1, source_target_pairs={{0,1},{1,0},{2,3},{3,2},{4,5},{5,4},{6,7},{7,6},{8,9},{9,8},{10,11... | collective-permute-start | bytes 393224 | tf_op jit(solution)/shard_map/ppermute | solution.py:104
  23.8 1.5 %collective-permute-start.3 = (bf16[256,256]{1,0:T(8,128)(2,1)S(1)}, bf16[256,256]{1,0:T(8,128)(2,1)S(1)}, u32[]{:S(2)}, u32[]{:S(2)}) collective-permute-start(bf16[256,256]{1,0:T(8,128)(2,1)S(1)} %collective-permute-done.2), channel_id=1, source_target_pairs={{0,1},{1,0},{2,3},{3,2},{4,5},{5,4},{6,7},{7,6},{8,9},{9,8},{10,11... | collective-permute-start | bytes 393224 | tf_op jit(solution)/shard_map/ppermute | solution.py:104
  24.3 2.1 %copy-start = (bf16[8,64,256]{2,1,0:T(8,128)(2,1)}, bf16[8,64,256]{2,1,0:T(8,128)(2,1)S(1)}, u32[]{:S(2)}) copy-start(bf16[8,64,256]{2,1,0:T(8,128)(2,1)S(1)} %all-to-all-done) | copy-start | bytes 786436
  46.5 23.1 %collective-permute-start.8 = (f32[2,4,128,256]{3,2,1,0:T(8,128)}, f32[2,4,128,256]{3,2,1,0:T(8,128)S(1)}, u32[]{:S(2)}, u32[]{:S(2)}) collective-permute-start(f32[2,4,128,256]{3,2,1,0:T(8,128)} %get-tuple-element.8), channel_id=1, source_target_pairs={{0,1},{1,0},{2,3},{3,2},{4,5},{5,4},{6,7},{7,6},{8,9},{9,8},{10,11... | collective-permute-start | bytes 3145736 | tf_op jit(solution)/shard_map/ppermute | solution.py:116
  48.7 20.9 %copy-start.1 = (f32[2,4,128,256]{3,2,1,0:T(8,128)S(1)}, f32[2,4,128,256]{3,2,1,0:T(8,128)}, u32[]{:S(2)}) copy-start(f32[2,4,128,256]{3,2,1,0:T(8,128)} %get-tuple-element.7) | copy-start | bytes 3145732
  68.4 1.3 %collective-permute-start.9 = (f32[8,256]{1,0:T(8,128)S(1)}, f32[8,256]{1,0:T(8,128)S(1)}, u32[]{:S(2)}, u32[]{:S(2)}) collective-permute-start(f32[8,256]{1,0:T(8,128)S(1)} %slice.16), channel_id=1, source_target_pairs={{0,1},{1,0},{2,3},{3,2},{4,5},{5,4},{6,7},{7,6},{8,9},{9,8},{10,11... | collective-permute-start | bytes 24584 | tf_op jit(solution)/shard_map/ppermute | solution.py:115
  70.9 19.6 %all-to-all-start.2 = ((f32[8,136,256]{2,1,0:T(8,128)}), f32[8,136,256]{2,1,0:T(8,128)S(1)}, u32[]{:S(2)}, u32[]{:S(2)}) async-start(f32[8,136,256]{2,1,0:T(8,128)} %pad_maximum_fusion), calls=%async_computation.2 | async-start | bytes 2228224 | tf_op jit(solution)/shard_map/all_to_all | solution.py:118

commit v2 on v1

v2 whole, which is shorter than its diff:
```python
import functools

import jax
import jax.numpy as jnp
from jax import lax
from jax.experimental import pallas as pl
from jax.experimental.pallas import tpu as pltpu
from jax.sharding import PartitionSpec as P

F32 = jnp.float32
BF16 = jnp.bfloat16
K, R = 8, 256
SHARD = 128
NB, NJ = 64, 512
XL, Z, CORE = 2, 4, 2
PEERS = 8

SPACE = range(XL * Z * CORE)
SAME_CORE = [[2 * g + c for g in range(XL * Z)] for c in range(CORE)]
TO_CORE = [(p, p ^ 1) for p in SPACE]
TO_XL = [(p, p ^ 8) for p in SPACE]


def from_z(d):
    return [((p & 9) | ((((p >> 1) + d) % 4) << 1), p) for p in SPACE]


def dot_last(x, y):
    return lax.dot_general(x, y, (((1,), (1,)), ((), ())), preferred_element_type=F32)


def add_up(x):
    return jnp.sum(x.astype(F32), axis=0)


def dot(x, y):
    return jnp.dot(x, y, preferred_element_type=F32)


def split(x):
    high = x.astype(BF16)
    return high, (x - high.astype(F32)).astype(BF16)


KH = 2


def body(last, place, t0, t1, t2, t3, *refs):
    n = 2 * (3 if last else 1)
    pieces, refs = refs[:n], refs[n:]
    b_any, c_ref, refs = refs[0], refs[1], refs[2:]
    if last:
        gb_in, gc_in, refs = refs[0], refs[1], refs[2:]
    same_ref, other_ref, *outs, w_ref, a_ref, b_ref, ch_ref, sems = refs
    step, part = pl.program_id(0), pl.program_id(1)

    def arrive(s, half):
        return pltpu.make_async_copy(pieces[2 * s + half], a_ref.at[s, pl.ds(half * 2 * SHARD, 2 * SHARD)], sems.at[2 * s + half])

    b_copy = pltpu.make_async_copy(b_any, b_ref, sems.at[n])

    @pl.when((step == 0) & (part == 0))
    def _():
        for s in range(n // 2):
            for half in range(2):
                arrive(s, half).start()
        b_copy.start()
        ch_ref[...] = c_ref[...].astype(F32) * 0.5
        for s in range(n // 2):
            for half in range(2):
                arrive(s, half).wait()
        b_copy.wait()

    rows = a_ref[step]
    wide = rows.astype(F32)
    rows_t = rows.T
    b = b_ref[...]
    grad = jnp.zeros((4 * SHARD, R), F32)
    for kk in range(K // KH):
        k = part * (K // KH) + kk
        ck = ch_ref[pl.ds(k, 1), :]
        half = dot_last((wide * ck).astype(BF16), b)
        t = jnp.concatenate([r[kk, 0] for r in (t0, t1, t2, t3)], axis=0).astype(F32)
        d2 = ((jnp.tanh(half) + 1.0) - (t + t)).astype(BF16)
        grad = grad + dot(d2, b) * ck
        w_ref[k] = jnp.where(step > 0, w_ref[k], 0.0) + dot(rows_t, d2)

    xl = place[0] >> 3
    for dx in range(2):
        at = lax.bitwise_xor(xl, dx)
        for slot, ref in ((dx, same_ref), (2 + dx, other_ref)):
            mine = grad[slot * SHARD : (slot + 1) * SHARD]
            ref[at, 0] = jnp.where(part > 0, ref[at, 0], 0.0) + mine

    @pl.when((step == pl.num_programs(0) - 1) & (part == KH - 1))
    def _():
        c_half = ch_ref[...]
        total = gb_in[...] if last else jnp.zeros((R, NJ), F32)
        lane = lax.broadcasted_iota(jnp.int32, (R, 128), 1)
        sums = jnp.zeros((R, 128), F32)
        bt = b_ref[...].T.astype(F32)
        c_t = jnp.concatenate([c_half, jnp.zeros((128 - K, R), F32)], axis=0).T
        for k in range(K):
            wk = w_ref[k]
            total = total + wk * c_t[:, k : k + 1]
            s = jnp.sum(wk * bt, axis=1, keepdims=True) * 0.5
            sums = jnp.where(lane == k, s, sums)
        if not last:
            outs[0][...] = total
            outs[1][...] = sums
            return
        grad_b = total.T.astype(BF16)
        high, low = split((sums + gc_in[...]).T[:K])
        for peer in range(PEERS):
            outs[0][peer, :NB] = grad_b[peer * NB : (peer + 1) * NB]
            outs[0][peer, NB:] = jnp.concatenate([high, low], axis=0)


def local(place, target, pieces, b_full, c_factor, *before):
    last = bool(before)
    steps, shift = (3, 1) if last else (1, 0)

    def tile(q):
        dc, dx = q // 2, q % 2

        def index(s, h, place):
            p = place[0]
            z = (lax.shift_right_logical(p, 1) + s + shift) & 3
            return h, ((p & 8) ^ (8 * dx)) + z * 2 + ((p & 1) ^ dc), 0, 0

        return pl.BlockSpec((K // KH, 1, SHARD, NJ), index)

    def whole(*shape):
        return pl.BlockSpec(shape, lambda s, h, place: (0,) * len(shape))

    anywhere = pl.BlockSpec(memory_space=pl.ANY)
    if last:
        out = pl.BlockSpec((XL, 1, SHARD, R), lambda s, h, place: (0, (lax.shift_right_logical(place[0], 1) + s + 1) & 3, 0, 0))
        after = [whole(PEERS, NB + 2 * K, R)]
        after_shape = [jax.ShapeDtypeStruct((PEERS, NB + 2 * K, R), BF16)]
        inputs = [whole(R, NJ), whole(R, 128)]
    else:
        out = pl.BlockSpec((XL, 1, SHARD, R), lambda s, h, place: (0, lax.shift_right_logical(place[0], 1) & 3, 0, 0))
        after = [whole(R, NJ), whole(R, 128)]
        after_shape = [jax.ShapeDtypeStruct((R, NJ), F32), jax.ShapeDtypeStruct((R, 128), F32)]
        inputs = []
    carried = [anywhere, anywhere] if last else []
    n = 2 * steps
    return pl.pallas_call(
        functools.partial(body if not last else skip_carried, last),
        grid_spec=pltpu.PrefetchScalarGridSpec(
            num_scalar_prefetch=1,
            grid=(steps, KH),
            in_specs=[tile(q) for q in range(4)] + [anywhere] * n + [anywhere, whole(K, R)] + inputs + carried,
            out_specs=[out, out] + after,
            scratch_shapes=[
                pltpu.VMEM((K, R, NJ), F32),
                pltpu.VMEM((steps, 4 * SHARD, R), BF16),
                pltpu.VMEM((NJ, R), BF16),
                pltpu.VMEM((K, R), F32),
                pltpu.SemaphoreType.DMA((n + 1,)),
            ],
        ),
        out_shape=[jax.ShapeDtypeStruct((XL, Z, SHARD, R), F32)] * 2 + after_shape,
        input_output_aliases={1 + 4 + n + 2 + 2: 0, 1 + 4 + n + 2 + 3: 1} if last else {},
        compiler_params=pltpu.CompilerParams(vmem_limit_bytes=46 << 20),
        cost_estimate=pl.CostEstimate(flops=3_230_000_000 * steps, bytes_accessed=5_500_000 * steps, transcendentals=2_100_000 * steps),
        name="rest" if last else "begin",
    )(place, target, target, target, target, *pieces, b_full, c_factor, *before)


def skip_carried(last, *refs):
    n = 1 + 4 + 6 + 2 + 2
    body(last, *refs[:n], *refs[n + 2 :])


def on_device(target, a_factor, b_factor, c_factor):
    place = lax.axis_index("space").astype(jnp.int32).reshape(1)
    b_full = lax.all_to_all(jnp.broadcast_to(b_factor[None], (PEERS, NB, R)), "samples", 0, 0).reshape(NJ, R)
    a_x = lax.ppermute(a_factor, "space", TO_XL)
    pair = jnp.concatenate([a_factor, a_x], axis=0)
    mine = [lax.ppermute(pair, "space", from_z(d)) if d else pair for d in range(Z)]
    target = target.reshape(K, 16, SHARD, NJ)
    same, other, gb, gc = local(place, target, [pair, lax.ppermute(pair, "space", TO_CORE)], b_full, c_factor)
    *mine, gc = lax.optimization_barrier((*mine[1:], gc))
    pieces = []
    for m in mine:
        pieces += [m, lax.ppermute(m, "space", TO_CORE)]
    same, other, first = local(place, target, pieces, b_full, c_factor, gb, gc, same, other)

    arrived = lax.ppermute(other, "space", TO_CORE)
    first = add_up(lax.all_to_all(first, "samples", 0, 0))
    grad_b, c_sum = first[:NB], first[NB : NB + K] + first[NB + K :]
    high, low = split(c_sum + lax.ppermute(c_sum, "space", TO_CORE))
    tail = jnp.broadcast_to(jnp.concatenate([high, low], axis=0)[None], (PEERS, 2 * K, R))
    second = (same + arrived).astype(BF16).reshape(PEERS, SHARD, R)
    second = lax.all_to_all(jnp.concatenate([second, tail], axis=1), "space", 0, 0, axis_index_groups=SAME_CORE)
    second = add_up(second)
    return second[:SHARD], grad_b, second[SHARD : SHARD + K] + second[SHARD + K :]


def solution(mesh):
    return jax.shard_map(
        on_device,
        mesh=mesh,
        in_specs=(
            P(None, "samples", "space"),
            P(("samples", "space"), None),
            P(("space", "samples"), None),
            P(),
        ),
        out_specs=(P(("samples", "space"), None), P(("space", "samples"), None), P()),
        check_vma=False,
    )
```

time: 93.1 us -> 79.9 us (0.86)
  waiting for transfers between devices: 19.7 us -> 13.6 us
  blocking collectives: 19.6 us -> 15.8 us
  Pallas kernels: 20.1 us -> 23.6 us
  other arithmetic: 4.95 us -> 1.8 us
  local copies, waits for them, and re-layouts: 7.33 us -> 4.31 us
    all_to_all x2, waiting for transfers between devices: 15.4 us -> 11.2 us  [the longest x1 9.93 us: on_device(): lax.all_to_all(jnp.concatenate([second, tail], axis=1), 'space', 0, 0, ax...]
    all_to_all x1, blocking collectives: 19.6 us -> 15.8 us  [on_device(): first = add_up(lax.all_to_all(first, 'samples', 0, 0))]
    pallas_call x1 -> x2, Pallas kernels: 20.1 us -> 23.6 us  [local(): pl.pallas_call(functools.partial(body if not last else skip_carried, last...]
    concatenate x3 -> x2, other arithmetic: 2.75 us -> 0.86 us  [the longest x1 0.85 us: on_device(): jnp.concatenate([second, tail], axis=1)]
    ppermute x9, waiting for transfers between devices: 4.29 us -> 2.43 us  [the longest x3 1.25 us: on_device(): pieces += [m, lax.ppermute(m, 'space', TO_CORE)]]
    another operation x5 -> x0, other arithmetic: 1.19 us -> none  [on_device(): jnp.stack([jnp.concatenate([m, t], axis=0) for m, t in zip(mine, theirs)])]
    broadcast_in_dim x3 -> x2, local copies, waits for them, and re-layouts: 2.19 us -> 1.48 us  [the longest x1 1.47 us: on_device(): jnp.broadcast_to(b_factor[None], (PEERS, NB, R))]
    slice x4 -> x2, local copies, waits for them, and re-layouts: 1.9 us -> 1.3 us  [the longest x1 0.66 us: on_device(): second[:SHARD]]
  transfers between devices with their start and end apart: 12 -> 12, of which waited for: 5 -> 6; matrix products, arithmetic and copies ran while one was open for 9% -> 4% of each run, Pallas kernels for 0% -> 9%
where the time goes in v2:
time: 79.9 us; the launch traced here: 79.5 us
  Pallas kernels  23.6 us (30%)
  starting transfers between devices  19.5 us (24%)
  blocking collectives  15.8 us (20%)
  waiting for transfers between devices  13.6 us (17%)
  local copies, waits for them, and re-layouts  4.31 us (5%)
  other arithmetic  1.8 us (2%)
    pallas_call x2, Pallas kernels, local(): pl.pallas_call(functools.partial(body if not last else skip_carried, last...  23.6 us
    all_to_all x1, blocking collectives, on_device(): first = add_up(lax.all_to_all(first, 'samples', 0, 0))  15.8 us
    all_to_all x1, waiting for transfers between devices, on_device(): lax.all_to_all(jnp.concatenate([second, tail], axis=1), 'space', 0, 0, ax...  9.93 us
    all_to_all x1, starting transfers between devices, on_device(): lax.all_to_all(jnp.broadcast_to(b_factor[None], (PEERS, NB, R)), 'samples...  6.64 us
    ppermute x3, starting transfers between devices, on_device(): lax.ppermute(pair, 'space', from_z(d))  6.58 us
    all_to_all x1, starting transfers between devices, on_device(): lax.all_to_all(jnp.concatenate([second, tail], axis=1), 'space', 0, 0, ax...  3.54 us
    ppermute x1, starting transfers between devices, on_device(): a_x = lax.ppermute(a_factor, 'space', TO_XL)  1.65 us
  transfers between devices with their start and end apart: 12, of which 6 were waited for; matrix products, arithmetic and copies ran while one was open for 4% of the time, Pallas kernels for 9%

profile of v2, /device:TPU:0, one launch (start us, length us, event | category | flops | bytes accessed | tf_op | source)
XLA Modules:
  0.0 79.5 jit_solution(18168195307085605126)
XLA Ops:
  0.6 1.7 %collective-permute-start = (bf16[128,256]{1,0:T(8,128)(2,1)}, bf16[128,256]{1,0:T(8,128)(2,1)S(1)}, u32[]{:S(2)}, u32[]{:S(2)}) collective-permute-start(bf16[128,256]{1,0:T(8,128)(2,1)} %param.5), channel_id=1, source_target_pairs={{0,8},{1,9},{2,10},{3,11},{4,12},{5,13},{6,14},{7,15},{8,0},{9,1},... | collective-permute-start | bytes 196616 | tf_op jit(solution)/shard_map/ppermute | solution.py:180
  2.3 1.5 %broadcast_in_dim.4 = bf16[8,64,256]{2,1,0:T(8,128)(2,1)} broadcast(bf16[64,256]{1,0:T(8,128)(2,1)} %param.6), dimensions={1,2} | broadcast | bytes 294912 | tf_op jit(solution)/shard_map/broadcast_in_dim | solution.py:179
  3.8 6.6 %all-to-all-start = ((bf16[8,64,256]{2,1,0:T(8,128)(2,1)}), bf16[8,64,256]{2,1,0:T(8,128)(2,1)S(1)}, u32[]{:S(2)}, u32[]{:S(2)}) async-start(bf16[8,64,256]{2,1,0:T(8,128)(2,1)} %broadcast_in_dim.4), calls=%async_computation | async-start | bytes 524288 | tf_op jit(solution)/shard_map/all_to_all | solution.py:179
  10.4 0.8 %constant_dynamic-update-slice_fusion.1 = bf16[256,256]{1,0:T(8,128)(2,1)S(1)} fusion(bf16[128,256]{1,0:T(8,128)(2,1)} %param.5), kind=kLoop, calls=%fused_computation.9 | loop fusion | bytes 131072
  11.2 0.0 collective-permute-done
  11.2 0.1 collective-permute-start.4
  11.3 2.0 %collective-permute-start.3 = (bf16[256,256]{1,0:T(8,128)(2,1)S(1)}, bf16[256,256]{1,0:T(8,128)(2,1)S(1)}, u32[]{:S(2)}, u32[]{:S(2)}) collective-permute-start(bf16[256,256]{1,0:T(8,128)(2,1)S(1)} %constant_dynamic-update-slice_fusion.refs_0_), channel_id=1, source_target_pairs={{6,0},{7,1},{0,2},{1,3},{2,4},{3,5},{4,6},{5,7},{14,8},{15,9},{8,1... | collective-permute-start | bytes 393224 | tf_op jit(solution)/shard_map/ppermute | solution.py:182
  13.3 3.6 %collective-permute-start.2 = (bf16[256,256]{1,0:T(8,128)(2,1)S(1)}, bf16[256,256]{1,0:T(8,128)(2,1)S(1)}, u32[]{:S(2)}, u32[]{:S(2)}) collective-permute-start(bf16[256,256]{1,0:T(8,128)(2,1)S(1)} %constant_dynamic-update-slice_fusion.refs_0_), channel_id=1, source_target_pairs={{4,0},{5,1},{6,2},{7,3},{0,4},{1,5},{2,6},{3,7},{12,8},{13,9},{14,... | collective-permute-start | bytes 393224 | tf_op jit(solution)/shard_map/ppermute | solution.py:182
  16.9 1.0 %collective-permute-start.1 = (bf16[256,256]{1,0:T(8,128)(2,1)S(1)}, bf16[256,256]{1,0:T(8,128)(2,1)S(1)}, u32[]{:S(2)}, u32[]{:S(2)}) collective-permute-start(bf16[256,256]{1,0:T(8,128)(2,1)S(1)} %constant_dynamic-update-slice_fusion.refs_0_), channel_id=1, source_target_pairs={{2,0},{3,1},{4,2},{5,3},{6,4},{7,5},{0,6},{1,7},{10,8},{11,9},{12,... | collective-permute-start | bytes 393224 | tf_op jit(solution)/shard_map/ppermute | solution.py:182
  17.9 0.0 collective-permute-done.4.refs_1_
  17.9 1.3 %all-to-all-done = bf16[8,64,256]{2,1,0:T(8,128)(2,1)S(1)} async-done(((bf16[8,64,256]{2,1,0:T(8,128)(2,1)}), bf16[8,64,256]{2,1,0:T(8,128)(2,1)S(1)}, u32[]{:S(2)}, u32[]{:S(2)}) %all-to-all-start) | async-done | bytes 262176 | tf_op jit(solution)/shard_map/all_to_all | solution.py:179
  19.2 0.0 copy-start
  19.2 0.7 copy-done
  19.9 0.0 copy-start.1
  19.9 7.2 %begin.1 = (f32[2,4,128,256]{3,2,1,0:T(8,128)S(1)}, f32[2,4,128,256]{3,2,1,0:T(8,128)S(1)}, f32[256,512]{1,0:T(8,128)S(1)}, f32[256,128]{1,0:T(8,128)S(1)}) custom-call(s32[1]{0:T(128)} %bitcast.place.refs_0_, bf16[8,16,128,512]{3,2,1,0:T(8,128)(2,1)} %bitcast.6, bf16[8,16,128,512]{3,2,1,0:T(8,128)(2,1)} %bitcast.7, bf16[8,16,128,512]{3,2,1,0:T(8,128)(2,1)} %bitcast.8, ...), custom_call_target="tpu_custom_call" | custom-call | flops 3230000128 | bytes 5500000 | tf_op jit(solution)/shard_map/begin/pallas_call | solution.py:149
  27.0 0.0 collective-permute-done.3.refs_9_
  27.0 0.0 collective-permute-done.2.refs_7_
  27.1 0.0 collective-permute-done.1.refs_5_
  27.1 0.1 collective-permute-start.5
  27.2 0.5 collective-permute-start.6
  27.7 0.1 collective-permute-start.7
  27.7 0.7 collective-permute-done.5.refs_6_
  28.5 0.2 collective-permute-done.6.refs_8_
  28.7 0.3 collective-permute-done.7.refs_10_
  29.0 0.0 copy-done.1
  29.0 16.5 %rest.1 = (f32[2,4,128,256]{3,2,1,0:T(8,128)S(1)}, f32[2,4,128,256]{3,2,1,0:T(8,128)S(1)}, bf16[8,80,256]{2,1,0:T(8,128)(2,1)S(1)}) custom-call(s32[1]{0:T(128)} %bitcast.place.refs_0_, bf16[8,16,128,512]{3,2,1,0:T(8,128)(2,1)} %bitcast.10, bf16[8,16,128,512]{3,2,1,0:T(8,128)(2,1)} %bitcast.11, ...), custom_call_target="tpu_custom_call", output_to_operand_aliasing={{0}: (15, {}), {1}: (16, {})} | custom-call | flops 9690000384 | bytes 16500000 | tf_op jit(solution)/shard_map/rest/pallas_call | solution.py:149
  45.5 0.3 collective-permute-start.8
  45.8 15.8 %all_to_all.15 = bf16[8,80,256]{2,1,0:T(8,128)(2,1)S(1)} all-to-all(bf16[8,80,256]{2,1,0:T(8,128)(2,1)S(1)} %get-tuple-element.24), channel_id=1, replica_groups=mesh['samples'=8,'space'=16] {'samples'}, dimensions={0} | all-to-all | bytes 655360 | tf_op jit(solution)/shard_map/all_to_all | solution.py:192
  61.7 0.1 collective-permute-start.9
  61.8 1.2 %collective-permute-done.9 = f32[8,256]{1,0:T(8,128)S(1)} collective-permute-done((f32[8,256]{1,0:T(8,128)S(1)}, f32[8,256]{1,0:T(8,128)S(1)}, u32[]{:S(2)}, u32[]{:S(2)}) %collective-permute-start.9) | collective-permute-done | bytes 8224 | tf_op jit(solution)/shard_map/ppermute | solution.py:194
  62.9 0.0 collective-permute-done.8
  62.9 0.2 add_convert_fusion
  63.2 0.9 %pad_maximum_fusion = bf16[8,144,256]{2,1,0:T(8,128)(2,1)} fusion(bf16[8,16,256]{2,1,0:T(8,128)(2,1)S(1)} %broadcast_in_dim.5, bf16[8,128,256]{2,1,0:T(8,128)(2,1)S(1)} %bitcast.14), kind=kLoop, calls=%fused_computation.3 | loop fusion | flops 1179648 | bytes 1179648 | tf_op jit(solution)/shard_map/concatenate | solution.py:197
  64.0 3.5 %all-to-all-start.2 = ((bf16[8,144,256]{2,1,0:T(8,128)(2,1)}), bf16[8,144,256]{2,1,0:T(8,128)(2,1)S(1)}, u32[]{:S(2)}, u32[]{:S(2)}) async-start(bf16[8,144,256]{2,1,0:T(8,128)(2,1)} %pad_maximum_fusion), calls=%async_computation.2 | async-start | bytes 1179648 | tf_op jit(solution)/shard_map/all_to_all | solution.py:197
  67.6 0.6 slice.27
  68.2 9.9 %all-to-all-done.2 = bf16[8,144,256]{2,1,0:T(8,128)(2,1)S(1)} async-done(((bf16[8,144,256]{2,1,0:T(8,128)(2,1)}), bf16[8,144,256]{2,1,0:T(8,128)(2,1)S(1)}, u32[]{:S(2)}, u32[]{:S(2)}) %all-to-all-start.2) | async-done | bytes 589856 | tf_op jit(solution)/shard_map/all_to_all | solution.py:197
  78.1 0.1 convert_reduce_fusion
  78.2 0.6 slice_add_fusion
  78.8 0.7 slice.26
  (6 shorter events, 0.1 us)
Async XLA Ops:
  0.6 10.6 %collective-permute-start = (bf16[128,256]{1,0:T(8,128)(2,1)}, bf16[128,256]{1,0:T(8,128)(2,1)S(1)}, u32[]{:S(2)}, u32[]{:S(2)}) collective-permute-start(bf16[128,256]{1,0:T(8,128)(2,1)} %param.5), channel_id=1, source_target_pairs={{0,8},{1,9},{2,10},{3,11},{4,12},{5,13},{6,14},{7,15},{8,0},{9,1},... | collective-permute-start | bytes 196616 | tf_op jit(solution)/shard_map/ppermute | solution.py:180
  3.8 15.4 %all-to-all-start = ((bf16[8,64,256]{2,1,0:T(8,128)(2,1)}), bf16[8,64,256]{2,1,0:T(8,128)(2,1)S(1)}, u32[]{:S(2)}, u32[]{:S(2)}) async-start(bf16[8,64,256]{2,1,0:T(8,128)(2,1)} %broadcast_in_dim.4), calls=%async_computation | async-start | bytes 524288 | tf_op jit(solution)/shard_map/all_to_all | solution.py:179
  11.2 6.7 %collective-permute-start.4 = (bf16[256,256]{1,0:T(8,128)(2,1)S(1)}, bf16[256,256]{1,0:T(8,128)(2,1)S(1)}, u32[]{:S(2)}, u32[]{:S(2)}) collective-permute-start(bf16[256,256]{1,0:T(8,128)(2,1)S(1)} %constant_dynamic-update-slice_fusion.refs_0_), channel_id=1, source_target_pairs={{0,1},{1,0},{2,3},{3,2},{4,5},{5,4},{6,7},{7,6},{8,9},{9,8},{10,11... | collective-permute-start | bytes 393224 | tf_op jit(solution)/shard_map/ppermute | solution.py:184
  11.3 15.7 %collective-permute-start.3 = (bf16[256,256]{1,0:T(8,128)(2,1)S(1)}, bf16[256,256]{1,0:T(8,128)(2,1)S(1)}, u32[]{:S(2)}, u32[]{:S(2)}) collective-permute-start(bf16[256,256]{1,0:T(8,128)(2,1)S(1)} %constant_dynamic-update-slice_fusion.refs_0_), channel_id=1, source_target_pairs={{6,0},{7,1},{0,2},{1,3},{2,4},{3,5},{4,6},{5,7},{14,8},{15,9},{8,1... | collective-permute-start | bytes 393224 | tf_op jit(solution)/shard_map/ppermute | solution.py:182
  13.3 13.7 %collective-permute-start.2 = (bf16[256,256]{1,0:T(8,128)(2,1)S(1)}, bf16[256,256]{1,0:T(8,128)(2,1)S(1)}, u32[]{:S(2)}, u32[]{:S(2)}) collective-permute-start(bf16[256,256]{1,0:T(8,128)(2,1)S(1)} %constant_dynamic-update-slice_fusion.refs_0_), channel_id=1, source_target_pairs={{4,0},{5,1},{6,2},{7,3},{0,4},{1,5},{2,6},{3,7},{12,8},{13,9},{14,... | collective-permute-start | bytes 393224 | tf_op jit(solution)/shard_map/ppermute | solution.py:182
  16.9 10.1 %collective-permute-start.1 = (bf16[256,256]{1,0:T(8,128)(2,1)S(1)}, bf16[256,256]{1,0:T(8,128)(2,1)S(1)}, u32[]{:S(2)}, u32[]{:S(2)}) collective-permute-start(bf16[256,256]{1,0:T(8,128)(2,1)S(1)} %constant_dynamic-update-slice_fusion.refs_0_), channel_id=1, source_target_pairs={{2,0},{3,1},{4,2},{5,3},{6,4},{7,5},{0,6},{1,7},{10,8},{11,9},{12,... | collective-permute-start | bytes 393224 | tf_op jit(solution)/shard_map/ppermute | solution.py:182
  19.2 0.7 copy-start
  19.9 9.1 %copy-start.1 = (bf16[8,256]{1,0:T(8,128)(2,1)S(1)}, bf16[8,256]{1,0:T(8,128)(2,1)}, u32[]{:S(2)}) copy-start(bf16[8,256]{1,0:T(8,128)(2,1)} %refs_12_.1) | copy-start | bytes 12292
  27.1 1.4 %collective-permute-start.5 = (bf16[256,256]{1,0:T(8,128)(2,1)S(1)}, bf16[256,256]{1,0:T(8,128)(2,1)S(1)}, u32[]{:S(2)}, u32[]{:S(2)}) collective-permute-start(bf16[256,256]{1,0:T(8,128)(2,1)S(1)} %collective-permute-done.1.refs_5_), channel_id=1, source_target_pairs={{0,1},{1,0},{2,3},{3,2},{4,5},{5,4},{6,7},{7,6},{8,9},{9,8},{10,11... | collective-permute-start | bytes 393224 | tf_op jit(solution)/shard_map/ppermute | solution.py:188
  27.2 1.5 %collective-permute-start.6 = (bf16[256,256]{1,0:T(8,128)(2,1)S(1)}, bf16[256,256]{1,0:T(8,128)(2,1)S(1)}, u32[]{:S(2)}, u32[]{:S(2)}) collective-permute-start(bf16[256,256]{1,0:T(8,128)(2,1)S(1)} %collective-permute-done.2.refs_7_), channel_id=1, source_target_pairs={{0,1},{1,0},{2,3},{3,2},{4,5},{5,4},{6,7},{7,6},{8,9},{9,8},{10,11... | collective-permute-start | bytes 393224 | tf_op jit(solution)/shard_map/ppermute | solution.py:188
  27.7 1.3 %collective-permute-start.7 = (bf16[256,256]{1,0:T(8,128)(2,1)S(1)}, bf16[256,256]{1,0:T(8,128)(2,1)S(1)}, u32[]{:S(2)}, u32[]{:S(2)}) collective-permute-start(bf16[256,256]{1,0:T(8,128)(2,1)S(1)} %collective-permute-done.3.refs_9_), channel_id=1, source_target_pairs={{0,1},{1,0},{2,3},{3,2},{4,5},{5,4},{6,7},{7,6},{8,9},{9,8},{10,11... | collective-permute-start | bytes 393224 | tf_op jit(solution)/shard_map/ppermute | solution.py:188
  45.5 17.4 %collective-permute-start.8 = (f32[2,4,128,256]{3,2,1,0:T(8,128)S(1)}, f32[2,4,128,256]{3,2,1,0:T(8,128)S(1)}, u32[]{:S(2)}, u32[]{:S(2)}) collective-permute-start(f32[2,4,128,256]{3,2,1,0:T(8,128)S(1)} %get-tuple-element.23), channel_id=1, source_target_pairs={{0,1},{1,0},{2,3},{3,2},{4,5},{5,4},{6,7},{7,6},{8,9},{9,8},{10,11... | collective-permute-start | bytes 3145736 | tf_op jit(solution)/shard_map/ppermute | solution.py:191
  61.7 1.3 %collective-permute-start.9 = (f32[8,256]{1,0:T(8,128)S(1)}, f32[8,256]{1,0:T(8,128)S(1)}, u32[]{:S(2)}, u32[]{:S(2)}) collective-permute-start(f32[8,256]{1,0:T(8,128)S(1)} %slice_add_fusion.1), channel_id=1, source_target_pairs={{0,1},{1,0},{2,3},{3,2},{4,5},{5,4},{6,7},{7,6},{8,9},{9,8},{10,11... | collective-permute-start | bytes 24584 | tf_op jit(solution)/shard_map/ppermute | solution.py:194
  64.0 14.1 %all-to-all-start.2 = ((bf16[8,144,256]{2,1,0:T(8,128)(2,1)}), bf16[8,144,256]{2,1,0:T(8,128)(2,1)S(1)}, u32[]{:S(2)}, u32[]{:S(2)}) async-start(bf16[8,144,256]{2,1,0:T(8,128)(2,1)} %pad_maximum_fusion), calls=%async_computation.2 | async-start | bytes 1179648 | tf_op jit(solution)/shard_map/all_to_all | solution.py:197

commit v3 on v2

v3 whole, which is shorter than its diff:
```python
import functools

import jax
import jax.numpy as jnp
from jax import lax
from jax.experimental import pallas as pl
from jax.experimental.pallas import tpu as pltpu
from jax.sharding import PartitionSpec as P

F32 = jnp.float32
BF16 = jnp.bfloat16
K, R = 8, 256
SHARD = 128
NB, NJ = 64, 512
XL, Z, CORE = 2, 4, 2
PEERS = 8

SPACE = range(XL * Z * CORE)
SAME_CORE = [[2 * g + c for g in range(XL * Z)] for c in range(CORE)]
TO_CORE = [(p, p ^ 1) for p in SPACE]
TO_XL = [(p, p ^ 8) for p in SPACE]


def from_z(d):
    return [((p & 9) | ((((p >> 1) + d) % 4) << 1), p) for p in SPACE]


def dot_last(x, y):
    return lax.dot_general(x, y, (((1,), (1,)), ((), ())), preferred_element_type=F32)


def add_up(x):
    return jnp.sum(x.astype(F32), axis=0)


def dot(x, y):
    return jnp.dot(x, y, preferred_element_type=F32)


def split(x):
    high = x.astype(BF16)
    return high, (x - high.astype(F32)).astype(BF16)


GROUP = 4 * SHARD
VMEM_LIMIT = 44 << 20


def body(last, place, t0, t1, t2, t3, *refs):
    steps = 3 if last else 1
    pieces, refs = refs[: 2 * steps], refs[2 * steps :]
    b_ref, c_ref, refs = refs[0], refs[1], refs[2:]
    if last:
        gb_in, gc_in, refs = refs[0], refs[1], refs[4:]
    same_ref, other_ref, *outs, w_ref, a_ref = refs
    step = pl.program_id(0)
    for s in range(steps):

        @pl.when(step == s)
        def _():
            a_ref[: 2 * SHARD] = pieces[2 * s][...]
            a_ref[2 * SHARD :] = pieces[2 * s + 1][...]

    rows = a_ref[...]
    wide = rows.astype(F32)
    rows_t = rows.T
    b = b_ref[...]
    c_half = c_ref[...]
    grad = jnp.zeros((GROUP, R), F32)
    for k in range(K):
        ck = c_half[k : k + 1, :]
        half = dot_last((wide * ck).astype(BF16), b)
        t = jnp.concatenate([r[k, 0] for r in (t0, t1, t2, t3)], axis=0).astype(F32)
        d2 = ((jnp.tanh(half) + 1.0) - (t + t)).astype(BF16)
        grad = grad + dot(d2, b) * ck
        part = dot(rows_t, d2)
        w_ref[k] = jnp.where(step > 0, w_ref[k], 0.0) + part if last else part

    xl = place[0] >> 3
    for dx in range(2):
        at = lax.bitwise_xor(xl, dx)
        same_ref[at, 0] = grad[dx * SHARD : (dx + 1) * SHARD]
        other_ref[at, 0] = grad[(2 + dx) * SHARD : (3 + dx) * SHARD]

    @pl.when(step == steps - 1)
    def _():
        total = gb_in[...] if last else jnp.zeros((R, NJ), F32)
        lane = lax.broadcasted_iota(jnp.int32, (R, 128), 1)
        sums = jnp.zeros((R, 128), F32)
        bt = b_ref[...].T.astype(F32)
        c_t = jnp.concatenate([c_half, jnp.zeros((128 - K, R), F32)], axis=0).T
        for k in range(K):
            wk = w_ref[k]
            total = total + wk * c_t[:, k : k + 1]
            s = jnp.sum(wk * bt, axis=1, keepdims=True) * 0.5
            sums = jnp.where(lane == k, s, sums)
        if not last:
            outs[0][...] = total
            outs[1][...] = sums
            return
        grad_b = total.T.astype(BF16)
        high, low = split((sums + gc_in[...]).T[:K])
        for peer in range(PEERS):
            outs[0][peer, :NB] = grad_b[peer * NB : (peer + 1) * NB]
            outs[0][peer, NB:] = jnp.concatenate([high, low], axis=0)


def local(place, target, pieces, b_full, c_half, *before):
    last = bool(before)
    steps, shift = (3, 1) if last else (1, 0)

    def tile(q):
        dc, dx = q // 2, q % 2

        def index(s, place):
            p = place[0]
            z = (lax.shift_right_logical(p, 1) + s + shift) & 3
            return 0, ((p & 8) ^ (8 * dx)) + z * 2 + ((p & 1) ^ dc), 0, 0

        return pl.BlockSpec((K, 1, SHARD, NJ), index)

    def whole(*shape):
        return pl.BlockSpec(shape, lambda s, place: (0,) * len(shape))

    anywhere = pl.BlockSpec(memory_space=pl.ANY)
    out = pl.BlockSpec(
        (XL, 1, SHARD, R), lambda s, place: (0, (lax.shift_right_logical(place[0], 1) + s + shift) & 3, 0, 0)
    )
    n = 2 * steps
    if last:
        after, carried = [((PEERS, NB + 2 * K, R), BF16)], [whole(R, NJ), whole(R, 128), anywhere, anywhere]
    else:
        after, carried = [((R, NJ), F32), ((R, 128), F32)], []
    return pl.pallas_call(
        functools.partial(body, last),
        grid_spec=pltpu.PrefetchScalarGridSpec(
            num_scalar_prefetch=1,
            grid=(steps,),
            in_specs=[tile(q) for q in range(4)] + [whole(2 * SHARD, R)] * n + [whole(NJ, R), whole(K, R)] + carried,
            out_specs=[out, out] + [whole(*shape) for shape, _ in after],
            scratch_shapes=[
                pltpu.VMEM((K, R, NJ), F32),
                pltpu.VMEM((GROUP, R), BF16),
            ],
        ),
        out_shape=[jax.ShapeDtypeStruct((XL, Z, SHARD, R), F32)] * 2
        + [jax.ShapeDtypeStruct(shape, dtype) for shape, dtype in after],
        input_output_aliases={n + 9: 0, n + 10: 1} if last else {},
        compiler_params=pltpu.CompilerParams(vmem_limit_bytes=VMEM_LIMIT),
        cost_estimate=pl.CostEstimate(
            flops=3_230_000_000 * steps, bytes_accessed=5_500_000 * steps, transcendentals=2_100_000 * steps
        ),
        name="rest" if last else "begin",
    )(place, target, target, target, target, *pieces, b_full, c_half, *before)


def on_device(target, a_factor, b_factor, c_factor):
    place = lax.axis_index("space").astype(jnp.int32).reshape(1)
    b_full = lax.all_to_all(jnp.broadcast_to(b_factor[None], (PEERS, NB, R)), "samples", 0, 0).reshape(NJ, R)
    c_half = c_factor.astype(F32) * 0.5
    a_x = lax.ppermute(a_factor, "space", TO_XL)
    pair = jnp.concatenate([a_factor, a_x], axis=0)
    mine = [lax.ppermute(pair, "space", from_z(d)) if d else pair for d in range(Z)]
    target = target.reshape(K, 16, SHARD, NJ)
    same, other, gb, gc = local(place, target, [pair, lax.ppermute(pair, "space", TO_CORE)], b_full, c_half)
    *mine, gc = lax.optimization_barrier((*mine[1:], gc))
    pieces = []
    for m in mine:
        pieces += [m, lax.ppermute(m, "space", TO_CORE)]
    same, other, first = local(place, target, pieces, b_full, c_half, gb, gc, same, other)

    arrived = lax.ppermute(other, "space", TO_CORE)
    first = add_up(lax.all_to_all(first, "samples", 0, 0))
    grad_b, c_sum = first[:NB], first[NB : NB + K] + first[NB + K :]
    high, low = split(c_sum + lax.ppermute(c_sum, "space", TO_CORE))
    tail = jnp.broadcast_to(jnp.concatenate([high, low], axis=0)[None], (PEERS, 2 * K, R))
    second = (same + arrived).astype(BF16).reshape(PEERS, SHARD, R)
    second = lax.all_to_all(jnp.concatenate([second, tail], axis=1), "space", 0, 0, axis_index_groups=SAME_CORE)
    second = add_up(second)
    return second[:SHARD], grad_b, second[SHARD : SHARD + K] + second[SHARD + K :]


def solution(mesh):
    return jax.shard_map(
        on_device,
        mesh=mesh,
        in_specs=(
            P(None, "samples", "space"),
            P(("samples", "space"), None),
            P(("space", "samples"), None),
            P(),
        ),
        out_specs=(P(("samples", "space"), None), P(("space", "samples"), None), P()),
        check_vma=False,
    )
```

time: 79.9 us -> 76.9 us (0.962)
  Pallas kernels: 23.6 us -> 20.6 us
    pallas_call x2, Pallas kernels: 23.6 us -> 20.6 us  [local(): pl.pallas_call(functools.partial(body, last), grid_spec=pltpu.PrefetchSca...]
  transfers between devices with their start and end apart: 12 -> 12, of which waited for: 6 -> 6; matrix products, arithmetic and copies ran while one was open for 4% -> 5% of each run, Pallas kernels for 9% -> 8%
where the time goes in v3:
time: 76.9 us; the launch traced here: 76.4 us
  Pallas kernels  20.6 us (27%)
  starting transfers between devices  19.4 us (25%)
  blocking collectives  16.5 us (21%)
  waiting for transfers between devices  13 us (17%)
  local copies, waits for them, and re-layouts  3.63 us (5%)
  other arithmetic  2.49 us (3%)
    pallas_call x2, Pallas kernels, local(): pl.pallas_call(functools.partial(body, last), grid_spec=pltpu.PrefetchSca...  20.6 us
    all_to_all x1, blocking collectives, on_device(): first = add_up(lax.all_to_all(first, 'samples', 0, 0))  16.5 us
    all_to_all x1, waiting for transfers between devices, on_device(): lax.all_to_all(jnp.concatenate([second, tail], axis=1), 'space', 0, 0, ax...  9.93 us
    all_to_all x1, starting transfers between devices, on_device(): lax.all_to_all(jnp.broadcast_to(b_factor[None], (PEERS, NB, R)), 'samples...  6.64 us
    ppermute x3, starting transfers between devices, on_device(): lax.ppermute(pair, 'space', from_z(d))  6.51 us
    all_to_all x1, starting transfers between devices, on_device(): lax.all_to_all(jnp.concatenate([second, tail], axis=1), 'space', 0, 0, ax...  3.54 us
    ppermute x1, starting transfers between devices, on_device(): a_x = lax.ppermute(a_factor, 'space', TO_XL)  1.65 us
  transfers between devices with their start and end apart: 12, of which 6 were waited for; matrix products, arithmetic and copies ran while one was open for 5% of the time, Pallas kernels for 8%

profile of v3, /device:TPU:0, one launch (start us, length us, event | category | flops | bytes accessed | tf_op | source)
XLA Modules:
  0.0 76.4 jit_solution(16364608402432376363)
XLA Ops:
  0.6 1.7 %collective-permute-start = (bf16[128,256]{1,0:T(8,128)(2,1)}, bf16[128,256]{1,0:T(8,128)(2,1)S(1)}, u32[]{:S(2)}, u32[]{:S(2)}) collective-permute-start(bf16[128,256]{1,0:T(8,128)(2,1)} %param.5), channel_id=1, source_target_pairs={{0,8},{1,9},{2,10},{3,11},{4,12},{5,13},{6,14},{7,15},{8,0},{9,1},... | collective-permute-start | bytes 196616 | tf_op jit(solution)/shard_map/ppermute | solution.py:161
  2.3 1.5 %broadcast_in_dim.4 = bf16[8,64,256]{2,1,0:T(8,128)(2,1)} broadcast(bf16[64,256]{1,0:T(8,128)(2,1)} %param.6), dimensions={1,2} | broadcast | bytes 294912 | tf_op jit(solution)/shard_map/broadcast_in_dim | solution.py:159
  3.8 6.6 %all-to-all-start = ((bf16[8,64,256]{2,1,0:T(8,128)(2,1)}), bf16[8,64,256]{2,1,0:T(8,128)(2,1)S(1)}, u32[]{:S(2)}, u32[]{:S(2)}) async-start(bf16[8,64,256]{2,1,0:T(8,128)(2,1)} %broadcast_in_dim.4), calls=%async_computation | async-start | bytes 524288 | tf_op jit(solution)/shard_map/all_to_all | solution.py:159
  10.4 0.8 %constant_dynamic-update-slice_fusion.1 = bf16[256,256]{1,0:T(8,128)(2,1)S(1)} fusion(bf16[128,256]{1,0:T(8,128)(2,1)} %param.5), kind=kLoop, calls=%fused_computation.10 | loop fusion | bytes 131072
  11.2 0.0 collective-permute-done
  11.3 0.1 collective-permute-start.4
  11.4 0.7 convert_multiply_fusion.refs_3_.refs_7_
  12.0 1.9 %collective-permute-start.3 = (bf16[256,256]{1,0:T(8,128)(2,1)S(1)}, bf16[256,256]{1,0:T(8,128)(2,1)S(1)}, u32[]{:S(2)}, u32[]{:S(2)}) collective-permute-start(bf16[256,256]{1,0:T(8,128)(2,1)S(1)} %constant_dynamic-update-slice_fusion.refs_0_), channel_id=1, source_target_pairs={{6,0},{7,1},{0,2},{1,3},{2,4},{3,5},{4,6},{5,7},{14,8},{15,9},{8,1... | collective-permute-start | bytes 393224 | tf_op jit(solution)/shard_map/ppermute | solution.py:163
  14.0 3.6 %collective-permute-start.2 = (bf16[256,256]{1,0:T(8,128)(2,1)S(1)}, bf16[256,256]{1,0:T(8,128)(2,1)S(1)}, u32[]{:S(2)}, u32[]{:S(2)}) collective-permute-start(bf16[256,256]{1,0:T(8,128)(2,1)S(1)} %constant_dynamic-update-slice_fusion.refs_0_), channel_id=1, source_target_pairs={{4,0},{5,1},{6,2},{7,3},{0,4},{1,5},{2,6},{3,7},{12,8},{13,9},{14,... | collective-permute-start | bytes 393224 | tf_op jit(solution)/shard_map/ppermute | solution.py:163
  17.5 1.0 %collective-permute-start.1 = (bf16[256,256]{1,0:T(8,128)(2,1)S(1)}, bf16[256,256]{1,0:T(8,128)(2,1)S(1)}, u32[]{:S(2)}, u32[]{:S(2)}) collective-permute-start(bf16[256,256]{1,0:T(8,128)(2,1)S(1)} %constant_dynamic-update-slice_fusion.refs_0_), channel_id=1, source_target_pairs={{2,0},{3,1},{4,2},{5,3},{6,4},{7,5},{0,6},{1,7},{10,8},{11,9},{12,... | collective-permute-start | bytes 393224 | tf_op jit(solution)/shard_map/ppermute | solution.py:163
  18.6 0.0 collective-permute-done.4.refs_1_
  18.6 0.6 all-to-all-done
  19.2 6.0 %begin.1 = (f32[2,4,128,256]{3,2,1,0:T(8,128)S(1)}, f32[2,4,128,256]{3,2,1,0:T(8,128)S(1)}, f32[256,512]{1,0:T(8,128)S(1)}, f32[256,128]{1,0:T(8,128)S(1)}) custom-call(s32[1]{0:T(128)} %bitcast.place, bf16[8,16,128,512]{3,2,1,0:T(8,128)(2,1)} %bitcast.6, bf16[8,16,128,512]{3,2,1,0:T(8,128)(2,1)} %bitcast.7, bf16[8,16,128,512]{3,2,1,0:T(8,128)(2,1)} %bitcast.8, ...), custom_call_target="tpu_custom_call" | custom-call | flops 3230000128 | bytes 5500000 | tf_op jit(solution)/shard_map/begin/pallas_call | solution.py:134
  25.2 0.0 collective-permute-done.3.refs_4_
  25.2 0.0 collective-permute-done.2.refs_2_
  25.2 0.0 collective-permute-done.1.refs_0_
  25.2 0.1 collective-permute-start.5
  25.3 0.5 collective-permute-start.6
  25.8 0.1 collective-permute-start.7
  25.9 0.7 collective-permute-done.5.refs_1_
  26.6 0.2 collective-permute-done.6.refs_3_
  26.8 0.3 collective-permute-done.7.refs_5_
  27.1 14.7 %rest.1 = (f32[2,4,128,256]{3,2,1,0:T(8,128)S(1)}, f32[2,4,128,256]{3,2,1,0:T(8,128)S(1)}, bf16[8,80,256]{2,1,0:T(8,128)(2,1)S(1)}) custom-call(s32[1]{0:T(128)} %bitcast.place, bf16[8,16,128,512]{3,2,1,0:T(8,128)(2,1)} %bitcast.10, bf16[8,16,128,512]{3,2,1,0:T(8,128)(2,1)} %bitcast.11, ...), custom_call_target="tpu_custom_call", output_to_operand_aliasing={{0}: (15, {}), {1}: (16, {})} | custom-call | flops 9690000384 | bytes 16500000 | tf_op jit(solution)/shard_map/rest/pallas_call | solution.py:134
  41.8 0.3 collective-permute-start.8
  42.1 16.5 %all_to_all.15 = bf16[8,80,256]{2,1,0:T(8,128)(2,1)S(1)} all-to-all(bf16[8,80,256]{2,1,0:T(8,128)(2,1)S(1)} %get-tuple-element.24), channel_id=1, replica_groups=mesh['samples'=8,'space'=16] {'samples'}, dimensions={0} | all-to-all | bytes 655360 | tf_op jit(solution)/shard_map/all_to_all | solution.py:173
  58.6 0.1 collective-permute-start.9
  58.7 1.2 %collective-permute-done.9 = f32[8,256]{1,0:T(8,128)S(1)} collective-permute-done((f32[8,256]{1,0:T(8,128)S(1)}, f32[8,256]{1,0:T(8,128)S(1)}, u32[]{:S(2)}, u32[]{:S(2)}) %collective-permute-start.9) | collective-permute-done | bytes 8224 | tf_op jit(solution)/shard_map/ppermute | solution.py:175
  59.9 0.0 collective-permute-done.8
  59.9 0.2 add_convert_fusion
  60.1 0.8 %pad_maximum_fusion = bf16[8,144,256]{2,1,0:T(8,128)(2,1)} fusion(bf16[8,16,256]{2,1,0:T(8,128)(2,1)S(1)} %broadcast_in_dim.5, bf16[8,128,256]{2,1,0:T(8,128)(2,1)S(1)} %bitcast.14), kind=kLoop, calls=%fused_computation.3 | loop fusion | flops 1179648 | bytes 1179648 | tf_op jit(solution)/shard_map/concatenate | solution.py:178
  60.9 3.5 %all-to-all-start.2 = ((bf16[8,144,256]{2,1,0:T(8,128)(2,1)}), bf16[8,144,256]{2,1,0:T(8,128)(2,1)S(1)}, u32[]{:S(2)}, u32[]{:S(2)}) async-start(bf16[8,144,256]{2,1,0:T(8,128)(2,1)} %pad_maximum_fusion), calls=%async_computation.2 | async-start | bytes 1179648 | tf_op jit(solution)/shard_map/all_to_all | solution.py:178
  64.5 0.6 slice.27
  65.1 9.9 %all-to-all-done.2 = bf16[8,144,256]{2,1,0:T(8,128)(2,1)S(1)} async-done(((bf16[8,144,256]{2,1,0:T(8,128)(2,1)}), bf16[8,144,256]{2,1,0:T(8,128)(2,1)S(1)}, u32[]{:S(2)}, u32[]{:S(2)}) %all-to-all-start.2) | async-done | bytes 589856 | tf_op jit(solution)/shard_map/all_to_all | solution.py:178
  75.1 0.1 convert_reduce_fusion
  75.1 0.6 slice_add_fusion
  75.7 0.7 slice.26
  (6 shorter events, 0.1 us)
Async XLA Ops:
  0.6 10.6 %collective-permute-start = (bf16[128,256]{1,0:T(8,128)(2,1)}, bf16[128,256]{1,0:T(8,128)(2,1)S(1)}, u32[]{:S(2)}, u32[]{:S(2)}) collective-permute-start(bf16[128,256]{1,0:T(8,128)(2,1)} %param.5), channel_id=1, source_target_pairs={{0,8},{1,9},{2,10},{3,11},{4,12},{5,13},{6,14},{7,15},{8,0},{9,1},... | collective-permute-start | bytes 196616 | tf_op jit(solution)/shard_map/ppermute | solution.py:161
  3.8 15.4 %all-to-all-start = ((bf16[8,64,256]{2,1,0:T(8,128)(2,1)}), bf16[8,64,256]{2,1,0:T(8,128)(2,1)S(1)}, u32[]{:S(2)}, u32[]{:S(2)}) async-start(bf16[8,64,256]{2,1,0:T(8,128)(2,1)} %broadcast_in_dim.4), calls=%async_computation | async-start | bytes 524288 | tf_op jit(solution)/shard_map/all_to_all | solution.py:159
  11.3 7.3 %collective-permute-start.4 = (bf16[256,256]{1,0:T(8,128)(2,1)S(1)}, bf16[256,256]{1,0:T(8,128)(2,1)S(1)}, u32[]{:S(2)}, u32[]{:S(2)}) collective-permute-start(bf16[256,256]{1,0:T(8,128)(2,1)S(1)} %constant_dynamic-update-slice_fusion.refs_0_), channel_id=1, source_target_pairs={{0,1},{1,0},{2,3},{3,2},{4,5},{5,4},{6,7},{7,6},{8,9},{9,8},{10,11... | collective-permute-start | bytes 393224 | tf_op jit(solution)/shard_map/ppermute | solution.py:165
  12.0 13.1 %collective-permute-start.3 = (bf16[256,256]{1,0:T(8,128)(2,1)S(1)}, bf16[256,256]{1,0:T(8,128)(2,1)S(1)}, u32[]{:S(2)}, u32[]{:S(2)}) collective-permute-start(bf16[256,256]{1,0:T(8,128)(2,1)S(1)} %constant_dynamic-update-slice_fusion.refs_0_), channel_id=1, source_target_pairs={{6,0},{7,1},{0,2},{1,3},{2,4},{3,5},{4,6},{5,7},{14,8},{15,9},{8,1... | collective-permute-start | bytes 393224 | tf_op jit(solution)/shard_map/ppermute | solution.py:163
  14.0 11.2 %collective-permute-start.2 = (bf16[256,256]{1,0:T(8,128)(2,1)S(1)}, bf16[256,256]{1,0:T(8,128)(2,1)S(1)}, u32[]{:S(2)}, u32[]{:S(2)}) collective-permute-start(bf16[256,256]{1,0:T(8,128)(2,1)S(1)} %constant_dynamic-update-slice_fusion.refs_0_), channel_id=1, source_target_pairs={{4,0},{5,1},{6,2},{7,3},{0,4},{1,5},{2,6},{3,7},{12,8},{13,9},{14,... | collective-permute-start | bytes 393224 | tf_op jit(solution)/shard_map/ppermute | solution.py:163
  17.5 7.7 %collective-permute-start.1 = (bf16[256,256]{1,0:T(8,128)(2,1)S(1)}, bf16[256,256]{1,0:T(8,128)(2,1)S(1)}, u32[]{:S(2)}, u32[]{:S(2)}) collective-permute-start(bf16[256,256]{1,0:T(8,128)(2,1)S(1)} %constant_dynamic-update-slice_fusion.refs_0_), channel_id=1, source_target_pairs={{2,0},{3,1},{4,2},{5,3},{6,4},{7,5},{0,6},{1,7},{10,8},{11,9},{12,... | collective-permute-start | bytes 393224 | tf_op jit(solution)/shard_map/ppermute | solution.py:163
  25.2 1.4 %collective-permute-start.5 = (bf16[256,256]{1,0:T(8,128)(2,1)S(1)}, bf16[256,256]{1,0:T(8,128)(2,1)S(1)}, u32[]{:S(2)}, u32[]{:S(2)}) collective-permute-start(bf16[256,256]{1,0:T(8,128)(2,1)S(1)} %collective-permute-done.1.refs_0_), channel_id=1, source_target_pairs={{0,1},{1,0},{2,3},{3,2},{4,5},{5,4},{6,7},{7,6},{8,9},{9,8},{10,11... | collective-permute-start | bytes 393224 | tf_op jit(solution)/shard_map/ppermute | solution.py:169
  25.3 1.5 %collective-permute-start.6 = (bf16[256,256]{1,0:T(8,128)(2,1)S(1)}, bf16[256,256]{1,0:T(8,128)(2,1)S(1)}, u32[]{:S(2)}, u32[]{:S(2)}) collective-permute-start(bf16[256,256]{1,0:T(8,128)(2,1)S(1)} %collective-permute-done.2.refs_2_), channel_id=1, source_target_pairs={{0,1},{1,0},{2,3},{3,2},{4,5},{5,4},{6,7},{7,6},{8,9},{9,8},{10,11... | collective-permute-start | bytes 393224 | tf_op jit(solution)/shard_map/ppermute | solution.py:169
  25.8 1.3 %collective-permute-start.7 = (bf16[256,256]{1,0:T(8,128)(2,1)S(1)}, bf16[256,256]{1,0:T(8,128)(2,1)S(1)}, u32[]{:S(2)}, u32[]{:S(2)}) collective-permute-start(bf16[256,256]{1,0:T(8,128)(2,1)S(1)} %collective-permute-done.3.refs_4_), channel_id=1, source_target_pairs={{0,1},{1,0},{2,3},{3,2},{4,5},{5,4},{6,7},{7,6},{8,9},{9,8},{10,11... | collective-permute-start | bytes 393224 | tf_op jit(solution)/shard_map/ppermute | solution.py:169
  41.8 18.0 %collective-permute-start.8 = (f32[2,4,128,256]{3,2,1,0:T(8,128)S(1)}, f32[2,4,128,256]{3,2,1,0:T(8,128)S(1)}, u32[]{:S(2)}, u32[]{:S(2)}) collective-permute-start(f32[2,4,128,256]{3,2,1,0:T(8,128)S(1)} %get-tuple-element.23), channel_id=1, source_target_pairs={{0,1},{1,0},{2,3},{3,2},{4,5},{5,4},{6,7},{7,6},{8,9},{9,8},{10,11... | collective-permute-start | bytes 3145736 | tf_op jit(solution)/shard_map/ppermute | solution.py:172
  58.6 1.3 %collective-permute-start.9 = (f32[8,256]{1,0:T(8,128)S(1)}, f32[8,256]{1,0:T(8,128)S(1)}, u32[]{:S(2)}, u32[]{:S(2)}) collective-permute-start(f32[8,256]{1,0:T(8,128)S(1)} %slice_add_fusion.1), channel_id=1, source_target_pairs={{0,1},{1,0},{2,3},{3,2},{4,5},{5,4},{6,7},{7,6},{8,9},{9,8},{10,11... | collective-permute-start | bytes 24584 | tf_op jit(solution)/shard_map/ppermute | solution.py:175
  60.9 14.1 %all-to-all-start.2 = ((bf16[8,144,256]{2,1,0:T(8,128)(2,1)}), bf16[8,144,256]{2,1,0:T(8,128)(2,1)S(1)}, u32[]{:S(2)}, u32[]{:S(2)}) async-start(bf16[8,144,256]{2,1,0:T(8,128)(2,1)} %pad_maximum_fusion), calls=%async_computation.2 | async-start | bytes 1179648 | tf_op jit(solution)/shard_map/all_to_all | solution.py:178

commit v4 on v3

--- a/solution.py
+++ b/solution.py
@@ -16,7 +16,6 @@
 PEERS = 8
 
 SPACE = range(XL * Z * CORE)
-SAME_CORE = [[2 * g + c for g in range(XL * Z)] for c in range(CORE)]
 TO_CORE = [(p, p ^ 1) for p in SPACE]
 TO_XL = [(p, p ^ 8) for p in SPACE]
 
@@ -27,10 +26,6 @@
 
 def dot_last(x, y):
     return lax.dot_general(x, y, (((1,), (1,)), ((), ())), preferred_element_type=F32)
-
-
-def add_up(x):
-    return jnp.sum(x.astype(F32), axis=0)
 
 
 def dot(x, y):
@@ -51,8 +46,8 @@
     pieces, refs = refs[: 2 * steps], refs[2 * steps :]
     b_ref, c_ref, refs = refs[0], refs[1], refs[2:]
     if last:
-        gb_in, gc_in, refs = refs[0], refs[1], refs[4:]
-    same_ref, other_ref, *outs, w_ref, a_ref = refs
+        gb_in, gc_in, refs = refs[0], refs[1], refs[6:]
+    parts, outs, w_ref, a_ref = refs[:4], refs[4:-2], refs[-2], refs[-1]
     step = pl.program_id(0)
     for s in range(steps):
 
@@ -76,11 +71,8 @@
         part = dot(rows_t, d2)
         w_ref[k] = jnp.where(step > 0, w_ref[k], 0.0) + part if last else part
 
-    xl = place[0] >> 3
-    for dx in range(2):
-        at = lax.bitwise_xor(xl, dx)
-        same_ref[at, 0] = grad[dx * SHARD : (dx + 1) * SHARD]
-        other_ref[at, 0] = grad[(2 + dx) * SHARD : (3 + dx) * SHARD]
+    for slot in range(4):
+        parts[slot][0] = grad[slot * SHARD : (slot + 1) * SHARD]
 
     @pl.when(step == steps - 1)
     def _():
@@ -100,9 +92,9 @@
             return
         grad_b = total.T.astype(BF16)
         high, low = split((sums + gc_in[...]).T[:K])
-        for peer in range(PEERS):
-            outs[0][peer, :NB] = grad_b[peer * NB : (peer + 1) * NB]
-            outs[0][peer, NB:] = jnp.concatenate([high, low], axis=0)
+        outs[0][...] = grad_b
+        for peer in range(XL * Z * CORE):
+            outs[1][peer] = jnp.concatenate([high, low], axis=0)
 
 
 def local(place, target, pieces, b_full, c_half, *before):
@@ -123,12 +115,10 @@
         return pl.BlockSpec(shape, lambda s, place: (0,) * len(shape))
 
     anywhere = pl.BlockSpec(memory_space=pl.ANY)
-    out = pl.BlockSpec(
-        (XL, 1, SHARD, R), lambda s, place: (0, (lax.shift_right_logical(place[0], 1) + s + shift) & 3, 0, 0)
-    )
+    out = pl.BlockSpec((1, SHARD, R), lambda s, place: (s + shift, 0, 0))
     n = 2 * steps
     if last:
-        after, carried = [((PEERS, NB + 2 * K, R), BF16)], [whole(R, NJ), whole(R, 128), anywhere, anywhere]
+        after, carried = [((NJ, R), BF16), ((XL * Z * CORE, 2 * K, R), BF16)], [whole(R, NJ), whole(R, 128)] + [anywhere] * 4
     else:
         after, carried = [((R, NJ), F32), ((R, 128), F32)], []
     return pl.pallas_call(
@@ -137,21 +127,57 @@
             num_scalar_prefetch=1,
             grid=(steps,),
             in_specs=[tile(q) for q in range(4)] + [whole(2 * SHARD, R)] * n + [whole(NJ, R), whole(K, R)] + carried,
-            out_specs=[out, out] + [whole(*shape) for shape, _ in after],
+            out_specs=[out] * 4 + [whole(*shape) for shape, _ in after],
             scratch_shapes=[
                 pltpu.VMEM((K, R, NJ), F32),
                 pltpu.VMEM((GROUP, R), BF16),
             ],
         ),
-        out_shape=[jax.ShapeDtypeStruct((XL, Z, SHARD, R), F32)] * 2
+        out_shape=[jax.ShapeDtypeStruct((Z, SHARD, R), F32)] * 4
         + [jax.ShapeDtypeStruct(shape, dtype) for shape, dtype in after],
-        input_output_aliases={n + 9: 0, n + 10: 1} if last else {},
+        input_output_aliases={n + 9 + i: i for i in range(4)} if last else {},
         compiler_params=pltpu.CompilerParams(vmem_limit_bytes=VMEM_LIMIT),
         cost_estimate=pl.CostEstimate(
             flops=3_230_000_000 * steps, bytes_accessed=5_500_000 * steps, transcendentals=2_100_000 * steps
         ),
         name="rest" if last else "begin",
     )(place, target, target, target, target, *pieces, b_full, c_half, *before)
+
+
+def total(ref, first, rows):
+    out = ref[0, first : first + rows].astype(F32)
+    for peer in range(1, ref.shape[0]):
+        out = out + ref[peer, first : first + rows].astype(F32)
+    return out
+
+
+def small(body, name, *out_shape):
+    shapes = [jax.ShapeDtypeStruct(shape, dtype) for shape, dtype in out_shape]
+    return pl.pallas_call(body, out_shape=shapes, compiler_params=pltpu.CompilerParams(vmem_limit_bytes=8 << 20), name=name)
+
+
+def join(x_ref, y_ref, out_ref):
+    out_ref[...] = (x_ref[...] + y_ref[...]).astype(BF16)
+
+
+def pack(times_ref, gb_ref, out_ref):
+    high, low = split(total(times_ref, 0, K) + total(times_ref, K, K))
+    tail = jnp.concatenate([high, low], axis=0)
+    for peer in range(PEERS):
+        out_ref[peer, :NB] = gb_ref[peer * NB : (peer + 1) * NB]
+        out_ref[peer, NB:] = tail
+
+
+def spread(x_ref, y_ref, across_ref, own_ref, *out_refs):
+    own_ref[...] = x_ref[0] + y_ref[0] + across_ref[0].astype(F32)
+    for d, ref in enumerate(out_refs, 1):
+        ref[...] = (x_ref[d] + y_ref[d] + across_ref[d].astype(F32)).astype(BF16)
+
+
+def finish(first_ref, own_ref, g1, g2, g3, grad_a, grad_b, grad_c):
+    grad_a[...] = own_ref[...] + g1[...].astype(F32) + g2[...].astype(F32) + g3[...].astype(F32)
+    grad_b[...] = total(first_ref, 0, NB)
+    grad_c[...] = total(first_ref, NB, K) + total(first_ref, NB + K, K)
 
 
 def on_device(target, a_factor, b_factor, c_factor):
@@ -162,22 +188,26 @@
     pair = jnp.concatenate([a_factor, a_x], axis=0)
     mine = [lax.ppermute(pair, "space", from_z(d)) if d else pair for d in range(Z)]
     target = target.reshape(K, 16, SHARD, NJ)
-    same, other, gb, gc = local(place, target, [pair, lax.ppermute(pair, "space", TO_CORE)], b_full, c_half)
+    *parts, gb, gc = local(place, target, [pair, lax.ppermute(pair, "space", TO_CORE)], b_full, c_half)
     *mine, gc = lax.optimization_barrier((*mine[1:], gc))
     pieces = []
     for m in mine:
         pieces += [m, lax.ppermute(m, "space", TO_CORE)]
-    same, other, first = local(place, target, pieces, b_full, c_half, gb, gc, same, other)
-
-    arrived = lax.ppermute(other, "space", TO_CORE)
-    first = add_up(lax.all_to_all(first, "samples", 0, 0))
-    grad_b, c_sum = first[:NB], first[NB : NB + K] + first[NB + K :]
-    high, low = split(c_sum + lax.ppermute(c_sum, "space", TO_CORE))
-    tail = jnp.broadcast_to(jnp.concatenate([high, low], axis=0)[None], (PEERS, 2 * K, R))
-    second = (same + arrived).astype(BF16).reshape(PEERS, SHARD, R)
-    second = lax.all_to_all(jnp.concatenate([second, tail], axis=1), "space", 0, 0, axis_index_groups=SAME_CORE)
-    second = add_up(second)
-    return second[:SHARD], grad_b, second[SHARD : SHARD + K] + second[SHARD + K :]
+    own, far, own_core, far_core, first, times = local(place, target, pieces, b_full, c_half, gb, gc, *parts)
+
+    far_core = lax.ppermute(far_core, "space", TO_CORE)
+    own_core = lax.ppermute(own_core, "space", TO_CORE)
+    times = lax.all_to_all(times, "space", 0, 0)
+    (across,) = small(join, "join", ((Z, SHARD, R), BF16))(far, far_core)
+    across = lax.ppermute(across, "space", TO_XL)
+    times, across = lax.optimization_barrier((times, across))
+    (first,) = small(pack, "pack", ((PEERS, NB + 2 * K, R), BF16))(times, first)
+    first = lax.all_to_all(first, "samples", 0, 0)
+    piece = (SHARD, R)
+    own, *away = small(spread, "spread", (piece, F32), *[(piece, BF16)] * 3)(own, own_core, across)
+    away = [lax.ppermute(x, "space", from_z(-d)) for d, x in enumerate(away, 1)]
+    first, *away = lax.optimization_barrier((first, *away))
+    return tuple(small(finish, "finish", (piece, F32), ((NB, R), F32), ((K, R), F32))(first, own, *away))
 
 
 def solution(mesh):

time: 76.9 us -> 73 us (0.949)
  starting transfers between devices: 19.4 us -> 24.7 us
  waiting for transfers between devices: 13 us -> 8.82 us
  blocking collectives: 16.5 us -> 13.1 us
  other arithmetic: 2.49 us -> 0.69 us
  Pallas kernels: 20.6 us -> 22.1 us
  local copies, waits for them, and re-layouts: 3.63 us -> 2.32 us
    all_to_all x1, waiting for transfers between devices: 9.93 us -> 2.1 us  [on_device(): first = lax.all_to_all(first, 'samples', 0, 0)]
    ppermute x2 -> x6, starting transfers between devices: 0.35 us -> 4.78 us  [the longest x3 3.9 us: on_device(): away = [lax.ppermute(x, 'space', from_z(-d)) for d, x in enumerate(away, 1)]]
    ppermute x2 -> x6, waiting for transfers between devices: 1.16 us -> 4.82 us  [the longest x3 3.42 us: on_device(): away = [lax.ppermute(x, 'space', from_z(-d)) for d, x in enumerate(away, 1)]]
    all_to_all x1, blocking collectives: 16.5 us -> 13.1 us  [on_device(): times = lax.all_to_all(times, 'space', 0, 0)]
    pallas_call x0 -> x4, Pallas kernels: none -> 1.65 us  [the longest x1 0.78 us: on_device(): first, = small(pack, 'pack', ((PEERS, NB + 2 * K, R), BF16))(times, first)]
    slice x2 -> x0, local copies, waits for them, and re-layouts: 1.3 us -> none  [the longest x1 0.66 us: on_device(): second[:SHARD]]
    concatenate x2 -> x0, other arithmetic: 0.85 us -> none  [the longest x1 0.85 us: on_device(): jnp.concatenate([second, tail], axis=1)]
    all_to_all x1, starting transfers between devices: 3.54 us -> 4.35 us  [on_device(): first = lax.all_to_all(first, 'samples', 0, 0)]
  transfers between devices with their start and end apart: 12 -> 16, of which waited for: 6 -> 8; matrix products, arithmetic and copies ran while one was open for 5% -> 4% of each run, Pallas kernels for 8% -> 10%
where the time goes in v4:
time: 73 us; the launch traced here: 72.5 us
  starting transfers between devices  24.7 us (34%)
  Pallas kernels  22.1 us (30%)
  blocking collectives  13.1 us (18%)
  waiting for transfers between devices  8.82 us (12%)
  local copies, waits for them, and re-layouts  2.32 us (3%)
    pallas_call x2, Pallas kernels, local(): pl.pallas_call(functools.partial(body, last), grid_spec=pltpu.PrefetchSca...  20.5 us
    all_to_all x1, blocking collectives, on_device(): times = lax.all_to_all(times, 'space', 0, 0)  13.1 us
    all_to_all x1, starting transfers between devices, on_device(): lax.all_to_all(jnp.broadcast_to(b_factor[None], (PEERS, NB, R)), 'samples...  6.64 us
    ppermute x3, starting transfers between devices, on_device(): lax.ppermute(pair, 'space', from_z(d))  6.51 us
    all_to_all x1, starting transfers between devices, on_device(): first = lax.all_to_all(first, 'samples', 0, 0)  4.35 us
    ppermute x3, starting transfers between devices, on_device(): away = [lax.ppermute(x, 'space', from_z(-d)) for d, x in enumerate(away, 1)]  3.9 us
    ppermute x3, waiting for transfers between devices, on_device(): away = [lax.ppermute(x, 'space', from_z(-d)) for d, x in enumerate(away, 1)]  3.42 us
    all_to_all x1, waiting for transfers between devices, on_device(): first = lax.all_to_all(first, 'samples', 0, 0)  2.1 us
  transfers between devices with their start and end apart: 16, of which 8 were waited for; matrix products, arithmetic and copies ran while one was open for 4% of the time, Pallas kernels for 10%

profile of v4, /device:TPU:0, one launch (start us, length us, event | category | flops | bytes accessed | tf_op | source)
XLA Modules:
  0.0 72.5 jit_solution(14430499852556696923)
XLA Ops:
  0.6 1.7 %collective-permute-start = (bf16[128,256]{1,0:T(8,128)(2,1)}, bf16[128,256]{1,0:T(8,128)(2,1)S(1)}, u32[]{:S(2)}, u32[]{:S(2)}) collective-permute-start(bf16[128,256]{1,0:T(8,128)(2,1)} %param.5), channel_id=1, source_target_pairs={{0,8},{1,9},{2,10},{3,11},{4,12},{5,13},{6,14},{7,15},{8,0},{9,1},... | collective-permute-start | bytes 196616 | tf_op jit(solution)/shard_map/ppermute | solution.py:187
  2.3 1.5 %broadcast_in_dim.2 = bf16[8,64,256]{2,1,0:T(8,128)(2,1)} broadcast(bf16[64,256]{1,0:T(8,128)(2,1)} %param.6), dimensions={1,2} | broadcast | bytes 294912 | tf_op jit(solution)/shard_map/broadcast_in_dim | solution.py:185
  3.8 6.6 %all-to-all-start = ((bf16[8,64,256]{2,1,0:T(8,128)(2,1)}), bf16[8,64,256]{2,1,0:T(8,128)(2,1)S(1)}, u32[]{:S(2)}, u32[]{:S(2)}) async-start(bf16[8,64,256]{2,1,0:T(8,128)(2,1)} %broadcast_in_dim.2), calls=%async_computation | async-start | bytes 524288 | tf_op jit(solution)/shard_map/all_to_all | solution.py:185
  10.4 0.8 %constant_dynamic-update-slice_fusion.1 = bf16[256,256]{1,0:T(8,128)(2,1)S(1)} fusion(bf16[128,256]{1,0:T(8,128)(2,1)} %param.5), kind=kLoop, calls=%fused_computation.2 | loop fusion | bytes 131072
  11.2 0.0 collective-permute-done
  11.3 0.1 collective-permute-start.4
  11.3 0.7 convert_multiply_fusion.refs_3_.refs_7_
  12.0 1.9 %collective-permute-start.3 = (bf16[256,256]{1,0:T(8,128)(2,1)S(1)}, bf16[256,256]{1,0:T(8,128)(2,1)S(1)}, u32[]{:S(2)}, u32[]{:S(2)}) collective-permute-start(bf16[256,256]{1,0:T(8,128)(2,1)S(1)} %constant_dynamic-update-slice_fusion.refs_0_), channel_id=1, source_target_pairs={{6,0},{7,1},{0,2},{1,3},{2,4},{3,5},{4,6},{5,7},{14,8},{15,9},{8,1... | collective-permute-start | bytes 393224 | tf_op jit(solution)/shard_map/ppermute | solution.py:189
  14.0 3.6 %collective-permute-start.2 = (bf16[256,256]{1,0:T(8,128)(2,1)S(1)}, bf16[256,256]{1,0:T(8,128)(2,1)S(1)}, u32[]{:S(2)}, u32[]{:S(2)}) collective-permute-start(bf16[256,256]{1,0:T(8,128)(2,1)S(1)} %constant_dynamic-update-slice_fusion.refs_0_), channel_id=1, source_target_pairs={{4,0},{5,1},{6,2},{7,3},{0,4},{1,5},{2,6},{3,7},{12,8},{13,9},{14,... | collective-permute-start | bytes 393224 | tf_op jit(solution)/shard_map/ppermute | solution.py:189
  17.5 1.0 %collective-permute-start.1 = (bf16[256,256]{1,0:T(8,128)(2,1)S(1)}, bf16[256,256]{1,0:T(8,128)(2,1)S(1)}, u32[]{:S(2)}, u32[]{:S(2)}) collective-permute-start(bf16[256,256]{1,0:T(8,128)(2,1)S(1)} %constant_dynamic-update-slice_fusion.refs_0_), channel_id=1, source_target_pairs={{2,0},{3,1},{4,2},{5,3},{6,4},{7,5},{0,6},{1,7},{10,8},{11,9},{12,... | collective-permute-start | bytes 393224 | tf_op jit(solution)/shard_map/ppermute | solution.py:189
  18.5 0.0 collective-permute-done.4.refs_1_
  18.6 0.6 all-to-all-done
  19.2 6.0 %begin.1 = (f32[4,128,256]{2,1,0:T(8,128)S(1)}, f32[4,128,256]{2,1,0:T(8,128)S(1)}, f32[4,128,256]{2,1,0:T(8,128)S(1)}, f32[4,128,256]{2,1,0:T(8,128)S(1)}, f32[...) custom-call(s32[1]{0:T(128)} %bitcast.place, bf16[8,16,128,512]{3,2,1,0:T(8,128)(2,1)} %bitcast.5, ...), custom_call_target="tpu_custom_call" | custom-call | flops 3230000128 | bytes 5500000 | tf_op jit(solution)/shard_map/begin/pallas_call | solution.py:124
  25.2 0.0 collective-permute-done.3.refs_4_
  25.2 0.0 collective-permute-done.2.refs_2_
  25.2 0.0 collective-permute-done.1.refs_0_
  25.2 0.1 collective-permute-start.5
  25.3 0.5 collective-permute-start.6
  25.8 0.1 collective-permute-start.7
  25.9 0.7 %collective-permute-done.5.refs_1_ = bf16[256,256]{1,0:T(8,128)(2,1)S(1)} collective-permute-done((bf16[256,256]{1,0:T(8,128)(2,1)S(1)}, bf16[256,256]{1,0:T(8,128)(2,1)S(1)}, u32[]{:S(2)}, u32[]{:S(2)}) %collective-permute-start.5) | collective-permute-done | bytes 131104 | tf_op jit(solution)/shard_map/ppermute | solution.py:195
  26.6 0.2 collective-permute-done.6.refs_3_
  26.8 0.3 collective-permute-done.7.refs_5_
  27.1 14.5 %rest.1 = (f32[4,128,256]{2,1,0:T(8,128)S(1)}, f32[4,128,256]{2,1,0:T(8,128)S(1)}, f32[4,128,256]{2,1,0:T(8,128)S(1)}, f32[4,128,256]{2,1,0:T(8,128)S(1)}, bf16[...) custom-call(s32[1]{0:T(128)} %bitcast.place, ...), custom_call_target="tpu_custom_call", output_to_operand_aliasing={{0}: (15, {}), {1}: (16, {}), {2}: (17, {}), {3}: (18, {})} | custom-call | flops 9690000384 | bytes 16500000 | tf_op jit(solution)/shard_map/rest/pallas_call | solution.py:124
  41.6 0.3 collective-permute-start.8
  41.9 0.3 collective-permute-start.10
  42.2 1.4 %collective-permute-done.8.y_ref = f32[4,128,256]{2,1,0:T(8,128)S(1)} collective-permute-done((f32[4,128,256]{2,1,0:T(8,128)S(1)}, f32[4,128,256]{2,1,0:T(8,128)S(1)}, u32[]{:S(2)}, u32[]{:S(2)}) %collective-permute-start.8) | collective-permute-done | bytes 524320 | tf_op jit(solution)/shard_map/ppermute | solution.py:198
  43.6 0.1 join.1
  43.7 0.3 collective-permute-start.9
  44.0 13.1 %all_to_all.15.times_ref = bf16[16,16,256]{2,1,0:T(8,128)(2,1)S(1)} all-to-all(bf16[16,16,256]{2,1,0:T(8,128)(2,1)S(1)} %get-tuple-element.39), channel_id=1, replica_groups=mesh['samples'=8,'space'=16] {'space'}, dimensions={0} | all-to-all | bytes 262144 | tf_op jit(solution)/shard_map/all_to_all | solution.py:200
  57.2 0.0 collective-permute-done.9.across_ref
  57.2 0.8 %pack.1 = bf16[8,80,256]{2,1,0:T(8,128)(2,1)} custom-call(bf16[16,16,256]{2,1,0:T(8,128)(2,1)S(1)} %all_to_all.15.times_ref, bf16[512,256]{1,0:T(8,128)(2,1)S(1)} %get-tuple-element.43.gb_ref), custom_call_target="tpu_custom_call" | custom-call | tf_op jit(solution)/shard_map/pack/pallas_call | solution.py:204
  58.0 4.3 %all-to-all-start.2 = ((bf16[8,80,256]{2,1,0:T(8,128)(2,1)}), bf16[8,80,256]{2,1,0:T(8,128)(2,1)S(1)}, u32[]{:S(2)}, u32[]{:S(2)}) async-start(bf16[8,80,256]{2,1,0:T(8,128)(2,1)} %pack.1), calls=%async_computation.2 | async-start | bytes 655360 | tf_op jit(solution)/shard_map/all_to_all | solution.py:205
  62.3 0.0 collective-permute-done.10.y_ref
  62.3 0.1 spread.1
  62.4 0.2 collective-permute-start.11
  62.6 2.9 %collective-permute-start.12 = (bf16[128,256]{1,0:T(8,128)(2,1)S(1)}, bf16[128,256]{1,0:T(8,128)(2,1)S(1)}, u32[]{:S(2)}, u32[]{:S(2)}) collective-permute-start(bf16[128,256]{1,0:T(8,128)(2,1)S(1)} %get-tuple-element.48), channel_id=1, source_target_pairs={{4,0},{5,1},{6,2},{7,3},{0,4},{1,5},{2,6},{3,7},{12,8},{13,9},{14,... | collective-permute-start | bytes 196616 | tf_op jit(solution)/shard_map/ppermute | solution.py:208
  65.4 0.8 %collective-permute-start.13 = (bf16[128,256]{1,0:T(8,128)(2,1)S(1)}, bf16[128,256]{1,0:T(8,128)(2,1)S(1)}, u32[]{:S(2)}, u32[]{:S(2)}) collective-permute-start(bf16[128,256]{1,0:T(8,128)(2,1)S(1)} %get-tuple-element.49), channel_id=1, source_target_pairs={{2,0},{3,1},{4,2},{5,3},{6,4},{7,5},{0,6},{1,7},{10,8},{11,9},{12,... | collective-permute-start | bytes 196616 | tf_op jit(solution)/shard_map/ppermute | solution.py:208
  66.3 2.5 %collective-permute-done.11.g1 = bf16[128,256]{1,0:T(8,128)(2,1)S(1)} collective-permute-done((bf16[128,256]{1,0:T(8,128)(2,1)S(1)}, bf16[128,256]{1,0:T(8,128)(2,1)S(1)}, u32[]{:S(2)}, u32[]{:S(2)}) %collective-permute-start.11) | collective-permute-done | bytes 65568 | tf_op jit(solution)/shard_map/ppermute | solution.py:208
  68.8 0.0 collective-permute-done.12.g2
  68.8 0.9 %collective-permute-done.13.g3 = bf16[128,256]{1,0:T(8,128)(2,1)S(1)} collective-permute-done((bf16[128,256]{1,0:T(8,128)(2,1)S(1)}, bf16[128,256]{1,0:T(8,128)(2,1)S(1)}, u32[]{:S(2)}, u32[]{:S(2)}) %collective-permute-start.13) | collective-permute-done | bytes 65568 | tf_op jit(solution)/shard_map/ppermute | solution.py:208
  69.7 2.1 %all-to-all-done.2.first_ref = bf16[8,80,256]{2,1,0:T(8,128)(2,1)S(1)} async-done(((bf16[8,80,256]{2,1,0:T(8,128)(2,1)}), bf16[8,80,256]{2,1,0:T(8,128)(2,1)S(1)}, u32[]{:S(2)}, u32[]{:S(2)}) %all-to-all-start.2) | async-done | bytes 327712 | tf_op jit(solution)/shard_map/all_to_all | solution.py:205
  71.8 0.7 finish.1
  (1 shorter events, 0.0 us)
Async XLA Ops:
  0.6 10.6 %collective-permute-start = (bf16[128,256]{1,0:T(8,128)(2,1)}, bf16[128,256]{1,0:T(8,128)(2,1)S(1)}, u32[]{:S(2)}, u32[]{:S(2)}) collective-permute-start(bf16[128,256]{1,0:T(8,128)(2,1)} %param.5), channel_id=1, source_target_pairs={{0,8},{1,9},{2,10},{3,11},{4,12},{5,13},{6,14},{7,15},{8,0},{9,1},... | collective-permute-start | bytes 196616 | tf_op jit(solution)/shard_map/ppermute | solution.py:187
  3.8 15.4 %all-to-all-start = ((bf16[8,64,256]{2,1,0:T(8,128)(2,1)}), bf16[8,64,256]{2,1,0:T(8,128)(2,1)S(1)}, u32[]{:S(2)}, u32[]{:S(2)}) async-start(bf16[8,64,256]{2,1,0:T(8,128)(2,1)} %broadcast_in_dim.2), calls=%async_computation | async-start | bytes 524288 | tf_op jit(solution)/shard_map/all_to_all | solution.py:185
  11.3 7.3 %collective-permute-start.4 = (bf16[256,256]{1,0:T(8,128)(2,1)S(1)}, bf16[256,256]{1,0:T(8,128)(2,1)S(1)}, u32[]{:S(2)}, u32[]{:S(2)}) collective-permute-start(bf16[256,256]{1,0:T(8,128)(2,1)S(1)} %constant_dynamic-update-slice_fusion.refs_0_), channel_id=1, source_target_pairs={{0,1},{1,0},{2,3},{3,2},{4,5},{5,4},{6,7},{7,6},{8,9},{9,8},{10,11... | collective-permute-start | bytes 393224 | tf_op jit(solution)/shard_map/ppermute | solution.py:191
  12.0 13.1 %collective-permute-start.3 = (bf16[256,256]{1,0:T(8,128)(2,1)S(1)}, bf16[256,256]{1,0:T(8,128)(2,1)S(1)}, u32[]{:S(2)}, u32[]{:S(2)}) collective-permute-start(bf16[256,256]{1,0:T(8,128)(2,1)S(1)} %constant_dynamic-update-slice_fusion.refs_0_), channel_id=1, source_target_pairs={{6,0},{7,1},{0,2},{1,3},{2,4},{3,5},{4,6},{5,7},{14,8},{15,9},{8,1... | collective-permute-start | bytes 393224 | tf_op jit(solution)/shard_map/ppermute | solution.py:189
  14.0 11.2 %collective-permute-start.2 = (bf16[256,256]{1,0:T(8,128)(2,1)S(1)}, bf16[256,256]{1,0:T(8,128)(2,1)S(1)}, u32[]{:S(2)}, u32[]{:S(2)}) collective-permute-start(bf16[256,256]{1,0:T(8,128)(2,1)S(1)} %constant_dynamic-update-slice_fusion.refs_0_), channel_id=1, source_target_pairs={{4,0},{5,1},{6,2},{7,3},{0,4},{1,5},{2,6},{3,7},{12,8},{13,9},{14,... | collective-permute-start | bytes 393224 | tf_op jit(solution)/shard_map/ppermute | solution.py:189
  17.5 7.7 %collective-permute-start.1 = (bf16[256,256]{1,0:T(8,128)(2,1)S(1)}, bf16[256,256]{1,0:T(8,128)(2,1)S(1)}, u32[]{:S(2)}, u32[]{:S(2)}) collective-permute-start(bf16[256,256]{1,0:T(8,128)(2,1)S(1)} %constant_dynamic-update-slice_fusion.refs_0_), channel_id=1, source_target_pairs={{2,0},{3,1},{4,2},{5,3},{6,4},{7,5},{0,6},{1,7},{10,8},{11,9},{12,... | collective-permute-start | bytes 393224 | tf_op jit(solution)/shard_map/ppermute | solution.py:189
  25.2 1.4 %collective-permute-start.5 = (bf16[256,256]{1,0:T(8,128)(2,1)S(1)}, bf16[256,256]{1,0:T(8,128)(2,1)S(1)}, u32[]{:S(2)}, u32[]{:S(2)}) collective-permute-start(bf16[256,256]{1,0:T(8,128)(2,1)S(1)} %collective-permute-done.1.refs_0_), channel_id=1, source_target_pairs={{0,1},{1,0},{2,3},{3,2},{4,5},{5,4},{6,7},{7,6},{8,9},{9,8},{10,11... | collective-permute-start | bytes 393224 | tf_op jit(solution)/shard_map/ppermute | solution.py:195
  25.3 1.5 %collective-permute-start.6 = (bf16[256,256]{1,0:T(8,128)(2,1)S(1)}, bf16[256,256]{1,0:T(8,128)(2,1)S(1)}, u32[]{:S(2)}, u32[]{:S(2)}) collective-permute-start(bf16[256,256]{1,0:T(8,128)(2,1)S(1)} %collective-permute-done.2.refs_2_), channel_id=1, source_target_pairs={{0,1},{1,0},{2,3},{3,2},{4,5},{5,4},{6,7},{7,6},{8,9},{9,8},{10,11... | collective-permute-start | bytes 393224 | tf_op jit(solution)/shard_map/ppermute | solution.py:195
  25.8 1.3 %collective-permute-start.7 = (bf16[256,256]{1,0:T(8,128)(2,1)S(1)}, bf16[256,256]{1,0:T(8,128)(2,1)S(1)}, u32[]{:S(2)}, u32[]{:S(2)}) collective-permute-start(bf16[256,256]{1,0:T(8,128)(2,1)S(1)} %collective-permute-done.3.refs_4_), channel_id=1, source_target_pairs={{0,1},{1,0},{2,3},{3,2},{4,5},{5,4},{6,7},{7,6},{8,9},{9,8},{10,11... | collective-permute-start | bytes 393224 | tf_op jit(solution)/shard_map/ppermute | solution.py:195
  41.6 2.0 %collective-permute-start.8 = (f32[4,128,256]{2,1,0:T(8,128)S(1)}, f32[4,128,256]{2,1,0:T(8,128)S(1)}, u32[]{:S(2)}, u32[]{:S(2)}) collective-permute-start(f32[4,128,256]{2,1,0:T(8,128)S(1)} %get-tuple-element.41), channel_id=1, source_target_pairs={{0,1},{1,0},{2,3},{3,2},{4,5},{5,4},{6,7},{7,6},{8,9},{9,8},{10,11... | collective-permute-start | bytes 1572872 | tf_op jit(solution)/shard_map/ppermute | solution.py:198
  41.9 20.4 %collective-permute-start.10 = (f32[4,128,256]{2,1,0:T(8,128)S(1)}, f32[4,128,256]{2,1,0:T(8,128)S(1)}, u32[]{:S(2)}, u32[]{:S(2)}) collective-permute-start(f32[4,128,256]{2,1,0:T(8,128)S(1)} %get-tuple-element.45), channel_id=1, source_target_pairs={{0,1},{1,0},{2,3},{3,2},{4,5},{5,4},{6,7},{7,6},{8,9},{9,8},{10,11... | collective-permute-start | bytes 1572872 | tf_op jit(solution)/shard_map/ppermute | solution.py:199
  43.7 13.4 %collective-permute-start.9 = (bf16[4,128,256]{2,1,0:T(8,128)(2,1)S(1)}, bf16[4,128,256]{2,1,0:T(8,128)(2,1)S(1)}, u32[]{:S(2)}, u32[]{:S(2)}) collective-permute-start(bf16[4,128,256]{2,1,0:T(8,128)(2,1)S(1)} %join.1), channel_id=1, source_target_pairs={{0,8},{1,9},{2,10},{3,11},{4,12},{5,13},{6,14},{7,15},{8,0},{9,1},... | collective-permute-start | bytes 786440 | tf_op jit(solution)/shard_map/ppermute | solution.py:202
  58.0 13.8 %all-to-all-start.2 = ((bf16[8,80,256]{2,1,0:T(8,128)(2,1)}), bf16[8,80,256]{2,1,0:T(8,128)(2,1)S(1)}, u32[]{:S(2)}, u32[]{:S(2)}) async-start(bf16[8,80,256]{2,1,0:T(8,128)(2,1)} %pack.1), calls=%async_computation.2 | async-start | bytes 655360 | tf_op jit(solution)/shard_map/all_to_all | solution.py:205
  62.4 6.4 %collective-permute-start.11 = (bf16[128,256]{1,0:T(8,128)(2,1)S(1)}, bf16[128,256]{1,0:T(8,128)(2,1)S(1)}, u32[]{:S(2)}, u32[]{:S(2)}) collective-permute-start(bf16[128,256]{1,0:T(8,128)(2,1)S(1)} %get-tuple-element.47), channel_id=1, source_target_pairs={{6,0},{7,1},{0,2},{1,3},{2,4},{3,5},{4,6},{5,7},{14,8},{15,9},{8,1... | collective-permute-start | bytes 196616 | tf_op jit(solution)/shard_map/ppermute | solution.py:208
  62.6 6.2 %collective-permute-start.12 = (bf16[128,256]{1,0:T(8,128)(2,1)S(1)}, bf16[128,256]{1,0:T(8,128)(2,1)S(1)}, u32[]{:S(2)}, u32[]{:S(2)}) collective-permute-start(bf16[128,256]{1,0:T(8,128)(2,1)S(1)} %get-tuple-element.48), channel_id=1, source_target_pairs={{4,0},{5,1},{6,2},{7,3},{0,4},{1,5},{2,6},{3,7},{12,8},{13,9},{14,... | collective-permute-start | bytes 196616 | tf_op jit(solution)/shard_map/ppermute | solution.py:208
  65.4 4.3 %collective-permute-start.13 = (bf16[128,256]{1,0:T(8,128)(2,1)S(1)}, bf16[128,256]{1,0:T(8,128)(2,1)S(1)}, u32[]{:S(2)}, u32[]{:S(2)}) collective-permute-start(bf16[128,256]{1,0:T(8,128)(2,1)S(1)} %get-tuple-element.49), channel_id=1, source_target_pairs={{2,0},{3,1},{4,2},{5,3},{6,4},{7,5},{0,6},{1,7},{10,8},{11,9},{12,... | collective-permute-start | bytes 196616 | tf_op jit(solution)/shard_map/ppermute | solution.py:208

commit v5 on v4

--- a/solution.py
+++ b/solution.py
@@ -43,19 +43,14 @@
 
 def body(last, place, t0, t1, t2, t3, *refs):
     steps = 3 if last else 1
-    pieces, refs = refs[: 2 * steps], refs[2 * steps :]
+    mine, theirs, refs = refs[0], refs[1], refs[2:]
     b_ref, c_ref, refs = refs[0], refs[1], refs[2:]
     if last:
         gb_in, gc_in, refs = refs[0], refs[1], refs[6:]
     parts, outs, w_ref, a_ref = refs[:4], refs[4:-2], refs[-2], refs[-1]
     step = pl.program_id(0)
-    for s in range(steps):
-
-        @pl.when(step == s)
-        def _():
-            a_ref[: 2 * SHARD] = pieces[2 * s][...]
-            a_ref[2 * SHARD :] = pieces[2 * s + 1][...]
-
+    a_ref[: 2 * SHARD] = mine[step]
+    a_ref[2 * SHARD :] = theirs[step]
     rows = a_ref[...]
     wide = rows.astype(F32)
     rows_t = rows.T
@@ -116,7 +111,6 @@
 
     anywhere = pl.BlockSpec(memory_space=pl.ANY)
     out = pl.BlockSpec((1, SHARD, R), lambda s, place: (s + shift, 0, 0))
-    n = 2 * steps
     if last:
         after, carried = [((NJ, R), BF16), ((XL * Z * CORE, 2 * K, R), BF16)], [whole(R, NJ), whole(R, 128)] + [anywhere] * 4
     else:
@@ -126,7 +120,7 @@
         grid_spec=pltpu.PrefetchScalarGridSpec(
             num_scalar_prefetch=1,
             grid=(steps,),
-            in_specs=[tile(q) for q in range(4)] + [whole(2 * SHARD, R)] * n + [whole(NJ, R), whole(K, R)] + carried,
+            in_specs=[tile(q) for q in range(4)] + [whole(steps, 2 * SHARD, R)] * 2 + [whole(NJ, R), whole(K, R)] + carried,
             out_specs=[out] * 4 + [whole(*shape) for shape, _ in after],
             scratch_shapes=[
                 pltpu.VMEM((K, R, NJ), F32),
@@ -135,7 +129,7 @@
         ),
         out_shape=[jax.ShapeDtypeStruct((Z, SHARD, R), F32)] * 4
         + [jax.ShapeDtypeStruct(shape, dtype) for shape, dtype in after],
-        input_output_aliases={n + 9 + i: i for i in range(4)} if last else {},
+        input_output_aliases={11 + i: i for i in range(4)} if last else {},
         compiler_params=pltpu.CompilerParams(vmem_limit_bytes=VMEM_LIMIT),
         cost_estimate=pl.CostEstimate(
             flops=3_230_000_000 * steps, bytes_accessed=5_500_000 * steps, transcendentals=2_100_000 * steps
@@ -156,6 +150,16 @@
     return pl.pallas_call(body, out_shape=shapes, compiler_params=pltpu.CompilerParams(vmem_limit_bytes=8 << 20), name=name)
 
 
+def repeat(x_ref, out_ref):
+    for peer in range(PEERS):
+        out_ref[peer] = x_ref[...]
+
+
+def stack(*refs):
+    for i, ref in enumerate(refs[:-1]):
+        refs[-1][i] = ref[...]
+
+
 def join(x_ref, y_ref, out_ref):
     out_ref[...] = (x_ref[...] + y_ref[...]).astype(BF16)
 
@@ -182,25 +186,25 @@
 
 def on_device(target, a_factor, b_factor, c_factor):
     place = lax.axis_index("space").astype(jnp.int32).reshape(1)
-    b_full = lax.all_to_all(jnp.broadcast_to(b_factor[None], (PEERS, NB, R)), "samples", 0, 0).reshape(NJ, R)
+    (b_wide,) = small(repeat, "repeat", ((PEERS, NB, R), BF16))(b_factor)
+    b_full = lax.all_to_all(b_wide, "samples", 0, 0).reshape(NJ, R)
     c_half = c_factor.astype(F32) * 0.5
     a_x = lax.ppermute(a_factor, "space", TO_XL)
     pair = jnp.concatenate([a_factor, a_x], axis=0)
     mine = [lax.ppermute(pair, "space", from_z(d)) if d else pair for d in range(Z)]
     target = target.reshape(K, 16, SHARD, NJ)
-    *parts, gb, gc = local(place, target, [pair, lax.ppermute(pair, "space", TO_CORE)], b_full, c_half)
+    *parts, gb, gc = local(place, target, [pair[None], lax.ppermute(pair, "space", TO_CORE)[None]], b_full, c_half)
     *mine, gc = lax.optimization_barrier((*mine[1:], gc))
-    pieces = []
-    for m in mine:
-        pieces += [m, lax.ppermute(m, "space", TO_CORE)]
+    (mine,) = small(stack, "stack", ((Z - 1, 2 * SHARD, R), BF16))(*mine)
+    pieces = [mine, lax.ppermute(mine, "space", TO_CORE)]
     own, far, own_core, far_core, first, times = local(place, target, pieces, b_full, c_half, gb, gc, *parts)
 
     far_core = lax.ppermute(far_core, "space", TO_CORE)
     own_core = lax.ppermute(own_core, "space", TO_CORE)
     times = lax.all_to_all(times, "space", 0, 0)
+    times, far_core = lax.optimization_barrier((times, far_core))
     (across,) = small(join, "join", ((Z, SHARD, R), BF16))(far, far_core)
     across = lax.ppermute(across, "space", TO_XL)
-    times, across = lax.optimization_barrier((times, across))
     (first,) = small(pack, "pack", ((PEERS, NB + 2 * K, R), BF16))(times, first)
     first = lax.all_to_all(first, "samples", 0, 0)
     piece = (SHARD, R)

time: 73 us -> 71.4 us (0.978)
  blocking collectives: 13.1 us -> 11.9 us
    ppermute x3, waiting for transfers between devices: 3.42 us -> 0.61 us  [on_device(): away = [lax.ppermute(x, 'space', from_z(-d)) for d, x in enumerate(away, 1)]]
    ppermute x1, waiting for transfers between devices: 0.01 us -> 2.79 us  [on_device(): across = lax.ppermute(across, 'space', TO_XL)]
    broadcast_in_dim x1 -> x0, local copies, waits for them, and re-layouts: 1.47 us -> none  [on_device(): jnp.broadcast_to(b_factor[None], (PEERS, NB, R))]
    ppermute x1, waiting for transfers between devices: 1.4 us -> 0.01 us  [on_device(): far_core = lax.ppermute(far_core, 'space', TO_CORE)]
    all_to_all x1, blocking collectives: 13.1 us -> 11.9 us  [on_device(): times = lax.all_to_all(times, 'space', 0, 0)]
    unnamed x1 -> x3, local copies, waits for them, and re-layouts: 0.84 us -> 1.6 us
    pallas_call x0 -> x2, Pallas kernels: none -> 0.73 us  [the longest x1 0.71 us: on_device(): b_wide, = small(repeat, 'repeat', ((PEERS, NB, R), BF16))(b_factor)]
    ppermute x4 -> x2, waiting for transfers between devices: 1.26 us -> 1.71 us  [the longest x1 1.71 us: on_device(): pieces = [mine, lax.ppermute(mine, 'space', TO_CORE)]]
  transfers between devices with their start and end apart: 16 -> 14, of which waited for: 8 -> 5; matrix products, arithmetic and copies ran while one was open for 4% -> 2% of each run, Pallas kernels for 10% -> 11%
where the time goes in v5:
time: 71.4 us; the launch traced here: 70.9 us
  starting transfers between devices  24.7 us (35%)
  Pallas kernels  22.8 us (32%)
  blocking collectives  11.9 us (17%)
  waiting for transfers between devices  8.47 us (12%)
  local copies, waits for them, and re-layouts  1.61 us (2%)
  between operations  0.72 us (1%)
    pallas_call x2, Pallas kernels, local(): pl.pallas_call(functools.partial(body, last), grid_spec=pltpu.PrefetchSca...  20.4 us
    all_to_all x1, blocking collectives, on_device(): times = lax.all_to_all(times, 'space', 0, 0)  11.9 us
    all_to_all x1, starting transfers between devices, on_device(): b_full = lax.all_to_all(b_wide, 'samples', 0, 0).reshape(NJ, R)  6.64 us
    ppermute x3, starting transfers between devices, on_device(): lax.ppermute(pair, 'space', from_z(d))  6.51 us
    all_to_all x1, starting transfers between devices, on_device(): first = lax.all_to_all(first, 'samples', 0, 0)  4.7 us
    ppermute x3, starting transfers between devices, on_device(): away = [lax.ppermute(x, 'space', from_z(-d)) for d, x in enumerate(away, 1)]  3.84 us
    ppermute x1, waiting for transfers between devices, on_device(): across = lax.ppermute(across, 'space', TO_XL)  2.79 us
    all_to_all x1, waiting for transfers between devices, on_device(): first = lax.all_to_all(first, 'samples', 0, 0)  2.72 us
  transfers between devices with their start and end apart: 14, of which 5 were waited for; matrix products, arithmetic and copies ran while one was open for 2% of the time, Pallas kernels for 11%

profile of v5, /device:TPU:0, one launch (start us, length us, event | category | flops | bytes accessed | tf_op | source)
XLA Modules:
  0.0 70.9 jit_solution(11527017317630472325)
XLA Ops:
  0.6 1.7 %collective-permute-start = (bf16[128,256]{1,0:T(8,128)(2,1)}, bf16[128,256]{1,0:T(8,128)(2,1)S(1)}, u32[]{:S(2)}, u32[]{:S(2)}) collective-permute-start(bf16[128,256]{1,0:T(8,128)(2,1)} %param.5), channel_id=1, source_target_pairs={{0,8},{1,9},{2,10},{3,11},{4,12},{5,13},{6,14},{7,15},{8,0},{9,1},... | collective-permute-start | bytes 196616 | tf_op jit(solution)/shard_map/ppermute | solution.py:192
  2.3 0.0 copy-start
  2.3 0.8 %copy-done = bf16[64,256]{1,0:T(8,128)(2,1)S(1)} copy-done((bf16[64,256]{1,0:T(8,128)(2,1)S(1)}, bf16[64,256]{1,0:T(8,128)(2,1)}, u32[]{:S(2)}) %copy-start) | copy-done | bytes 32792
  3.0 0.7 repeat.1
  3.7 6.6 %all-to-all-start = ((bf16[8,64,256]{2,1,0:T(8,128)(2,1)}), bf16[8,64,256]{2,1,0:T(8,128)(2,1)S(1)}, u32[]{:S(2)}, u32[]{:S(2)}) async-start(bf16[8,64,256]{2,1,0:T(8,128)(2,1)} %repeat.1), calls=%async_computation | async-start | bytes 524288 | tf_op jit(solution)/shard_map/all_to_all | solution.py:190
  10.4 0.8 %constant_dynamic-update-slice_fusion.1 = bf16[256,256]{1,0:T(8,128)(2,1)S(1)} fusion(bf16[128,256]{1,0:T(8,128)(2,1)} %param.5), kind=kLoop, calls=%fused_computation.2 | loop fusion | bytes 131072
  11.2 0.0 collective-permute-done
  11.2 0.1 collective-permute-start.4
  11.3 0.7 convert_multiply_fusion.refs_3_
  12.0 1.9 %collective-permute-start.3 = (bf16[256,256]{1,0:T(8,128)(2,1)S(1)}, bf16[256,256]{1,0:T(8,128)(2,1)S(1)}, u32[]{:S(2)}, u32[]{:S(2)}) collective-permute-start(bf16[256,256]{1,0:T(8,128)(2,1)S(1)} %constant_dynamic-update-slice_fusion), channel_id=1, source_target_pairs={{6,0},{7,1},{0,2},{1,3},{2,4},{3,5},{4,6},{5,7},{14,8},{15,9},{8,1... | collective-permute-start | bytes 393224 | tf_op jit(solution)/shard_map/ppermute | solution.py:194
  13.9 3.6 %collective-permute-start.2 = (bf16[256,256]{1,0:T(8,128)(2,1)S(1)}, bf16[256,256]{1,0:T(8,128)(2,1)S(1)}, u32[]{:S(2)}, u32[]{:S(2)}) collective-permute-start(bf16[256,256]{1,0:T(8,128)(2,1)S(1)} %constant_dynamic-update-slice_fusion), channel_id=1, source_target_pairs={{4,0},{5,1},{6,2},{7,3},{0,4},{1,5},{2,6},{3,7},{12,8},{13,9},{14,... | collective-permute-start | bytes 393224 | tf_op jit(solution)/shard_map/ppermute | solution.py:194
  17.5 1.0 %collective-permute-start.1 = (bf16[256,256]{1,0:T(8,128)(2,1)S(1)}, bf16[256,256]{1,0:T(8,128)(2,1)S(1)}, u32[]{:S(2)}, u32[]{:S(2)}) collective-permute-start(bf16[256,256]{1,0:T(8,128)(2,1)S(1)} %constant_dynamic-update-slice_fusion), channel_id=1, source_target_pairs={{2,0},{3,1},{4,2},{5,3},{6,4},{7,5},{0,6},{1,7},{10,8},{11,9},{12,... | collective-permute-start | bytes 393224 | tf_op jit(solution)/shard_map/ppermute | solution.py:194
  18.5 0.0 collective-permute-done.4
  18.5 0.6 all-to-all-done
  19.2 6.0 %begin.1 = (f32[4,128,256]{2,1,0:T(8,128)S(1)}, f32[4,128,256]{2,1,0:T(8,128)S(1)}, f32[4,128,256]{2,1,0:T(8,128)S(1)}, f32[4,128,256]{2,1,0:T(8,128)S(1)}, f32[...) custom-call(s32[1]{0:T(128)} %bitcast.place, bf16[8,16,128,512]{3,2,1,0:T(8,128)(2,1)} %bitcast.9, ...), custom_call_target="tpu_custom_call" | custom-call | flops 3230000128 | bytes 5500000 | tf_op jit(solution)/shard_map/begin/pallas_call | solution.py:118
  25.2 0.0 collective-permute-done.3.refs_2_
  25.2 0.0 collective-permute-done.2.refs_1_
  25.2 0.0 collective-permute-done.1.refs_0_
  25.2 0.1 collective-permute-start.5
  25.3 1.7 %collective-permute-done.5.refs_1_ = bf16[3,256,256]{2,1,0:T(8,128)(2,1)S(1)} collective-permute-done((bf16[3,256,256]{2,1,0:T(8,128)(2,1)S(1)}, bf16[3,256,256]{2,1,0:T(8,128)(2,1)S(1)}, u32[]{:S(2)}, u32[]{:S(2)}) %collective-permute-start.5) | collective-permute-done | bytes 393248 | tf_op jit(solution)/shard_map/ppermute | solution.py:199
  27.0 14.4 %rest.1 = (f32[4,128,256]{2,1,0:T(8,128)S(1)}, f32[4,128,256]{2,1,0:T(8,128)S(1)}, f32[4,128,256]{2,1,0:T(8,128)S(1)}, f32[4,128,256]{2,1,0:T(8,128)S(1)}, bf16[...) custom-call(s32[1]{0:T(128)} %bitcast.place, ...), custom_call_target="tpu_custom_call", output_to_operand_aliasing={{0}: (11, {}), {1}: (12, {}), {2}: (13, {}), {3}: (14, {})} | custom-call | flops 9690000384 | bytes 16500000 | tf_op jit(solution)/shard_map/rest/pallas_call | solution.py:118
  41.4 0.2 collective-permute-start.6
  41.7 0.4 collective-permute-start.7
  42.0 11.9 %all_to_all.15.times_ref = bf16[16,16,256]{2,1,0:T(8,128)(2,1)S(1)} all-to-all(bf16[16,16,256]{2,1,0:T(8,128)(2,1)S(1)} %get-tuple-element.39), channel_id=1, replica_groups=mesh['samples'=8,'space'=16] {'space'}, dimensions={0} | all-to-all | bytes 262144 | tf_op jit(solution)/shard_map/all_to_all | solution.py:204
  53.9 0.0 collective-permute-done.6.y_ref
  53.9 0.1 join.1
  54.0 0.6 collective-permute-start.8
  54.7 0.8 %pack.1 = bf16[8,80,256]{2,1,0:T(8,128)(2,1)} custom-call(bf16[16,16,256]{2,1,0:T(8,128)(2,1)S(1)} %all_to_all.15.times_ref, bf16[512,256]{1,0:T(8,128)(2,1)S(1)} %get-tuple-element.42.gb_ref), custom_call_target="tpu_custom_call" | custom-call | tf_op jit(solution)/shard_map/pack/pallas_call | solution.py:208
  55.4 4.7 %all-to-all-start.2 = ((bf16[8,80,256]{2,1,0:T(8,128)(2,1)}), bf16[8,80,256]{2,1,0:T(8,128)(2,1)S(1)}, u32[]{:S(2)}, u32[]{:S(2)}) async-start(bf16[8,80,256]{2,1,0:T(8,128)(2,1)} %pack.1), calls=%async_computation.2 | async-start | bytes 655360 | tf_op jit(solution)/shard_map/all_to_all | solution.py:209
  60.1 0.0 collective-permute-done.7.y_ref
  60.1 2.8 %collective-permute-done.8.across_ref = bf16[4,128,256]{2,1,0:T(8,128)(2,1)S(1)} collective-permute-done((bf16[4,128,256]{2,1,0:T(8,128)(2,1)S(1)}, bf16[4,128,256]{2,1,0:T(8,128)(2,1)S(1)}, u32[]{:S(2)}, u32[]{:S(2)}) %collective-permute-start.8) | collective-permute-done | bytes 262176 | tf_op jit(solution)/shard_map/ppermute | solution.py:207
  62.9 0.1 spread.1
  63.0 0.5 collective-permute-start.9
  63.5 2.4 %collective-permute-start.10 = (bf16[128,256]{1,0:T(8,128)(2,1)S(1)}, bf16[128,256]{1,0:T(8,128)(2,1)S(1)}, u32[]{:S(2)}, u32[]{:S(2)}) collective-permute-start(bf16[128,256]{1,0:T(8,128)(2,1)S(1)} %get-tuple-element.48), channel_id=1, source_target_pairs={{4,0},{5,1},{6,2},{7,3},{0,4},{1,5},{2,6},{3,7},{12,8},{13,9},{14,... | collective-permute-start | bytes 196616 | tf_op jit(solution)/shard_map/ppermute | solution.py:212
  65.9 0.9 %collective-permute-start.11 = (bf16[128,256]{1,0:T(8,128)(2,1)S(1)}, bf16[128,256]{1,0:T(8,128)(2,1)S(1)}, u32[]{:S(2)}, u32[]{:S(2)}) collective-permute-start(bf16[128,256]{1,0:T(8,128)(2,1)S(1)} %get-tuple-element.49), channel_id=1, source_target_pairs={{2,0},{3,1},{4,2},{5,3},{6,4},{7,5},{0,6},{1,7},{10,8},{11,9},{12,... | collective-permute-start | bytes 196616 | tf_op jit(solution)/shard_map/ppermute | solution.py:212
  66.8 2.7 %all-to-all-done.2.first_ref = bf16[8,80,256]{2,1,0:T(8,128)(2,1)S(1)} async-done(((bf16[8,80,256]{2,1,0:T(8,128)(2,1)}), bf16[8,80,256]{2,1,0:T(8,128)(2,1)S(1)}, u32[]{:S(2)}, u32[]{:S(2)}) %all-to-all-start.2) | async-done | bytes 327712 | tf_op jit(solution)/shard_map/all_to_all | solution.py:209
  69.6 0.0 collective-permute-done.9.g1
  69.6 0.0 collective-permute-done.10.g2
  69.6 0.6 collective-permute-done.11.g3
  70.2 0.7 %finish.1 = (f32[128,256]{1,0:T(8,128)}, f32[64,256]{1,0:T(8,128)}, f32[8,256]{1,0:T(8,128)}) custom-call(bf16[8,80,256]{2,1,0:T(8,128)(2,1)S(1)} %all-to-all-done.2.first_ref, f32[128,256]{1,0:T(8,128)S(1)} %get-tuple-element.51.own_ref, bf16[128,256]{1,0:T(8,128)(2,1)S(1)} %collective-permute-done.9.g1, bf16[128,256]{1,0:T(8,128)(2,1)S(1)} %collective-permute-done.10.g2, ...), custom_call_target="tpu_custom_call" | custom-call | tf_op jit(solution)/shard_map/finish/pallas_call | solution.py:214
  (2 shorter events, 0.0 us)
Async XLA Ops:
  0.6 10.6 %collective-permute-start = (bf16[128,256]{1,0:T(8,128)(2,1)}, bf16[128,256]{1,0:T(8,128)(2,1)S(1)}, u32[]{:S(2)}, u32[]{:S(2)}) collective-permute-start(bf16[128,256]{1,0:T(8,128)(2,1)} %param.5), channel_id=1, source_target_pairs={{0,8},{1,9},{2,10},{3,11},{4,12},{5,13},{6,14},{7,15},{8,0},{9,1},... | collective-permute-start | bytes 196616 | tf_op jit(solution)/shard_map/ppermute | solution.py:192
  2.3 0.8 %copy-start = (bf16[64,256]{1,0:T(8,128)(2,1)S(1)}, bf16[64,256]{1,0:T(8,128)(2,1)}, u32[]{:S(2)}) copy-start(bf16[64,256]{1,0:T(8,128)(2,1)} %x_ref.1) | copy-start | bytes 98308
  3.7 15.4 %all-to-all-start = ((bf16[8,64,256]{2,1,0:T(8,128)(2,1)}), bf16[8,64,256]{2,1,0:T(8,128)(2,1)S(1)}, u32[]{:S(2)}, u32[]{:S(2)}) async-start(bf16[8,64,256]{2,1,0:T(8,128)(2,1)} %repeat.1), calls=%async_computation | async-start | bytes 524288 | tf_op jit(solution)/shard_map/all_to_all | solution.py:190
  11.2 7.3 %collective-permute-start.4 = (bf16[256,256]{1,0:T(8,128)(2,1)S(1)}, bf16[256,256]{1,0:T(8,128)(2,1)S(1)}, u32[]{:S(2)}, u32[]{:S(2)}) collective-permute-start(bf16[256,256]{1,0:T(8,128)(2,1)S(1)} %constant_dynamic-update-slice_fusion), channel_id=1, source_target_pairs={{0,1},{1,0},{2,3},{3,2},{4,5},{5,4},{6,7},{7,6},{8,9},{9,8},{10,11... | collective-permute-start | bytes 393224 | tf_op jit(solution)/shard_map/ppermute | solution.py:196
  12.0 13.1 %collective-permute-start.3 = (bf16[256,256]{1,0:T(8,128)(2,1)S(1)}, bf16[256,256]{1,0:T(8,128)(2,1)S(1)}, u32[]{:S(2)}, u32[]{:S(2)}) collective-permute-start(bf16[256,256]{1,0:T(8,128)(2,1)S(1)} %constant_dynamic-update-slice_fusion), channel_id=1, source_target_pairs={{6,0},{7,1},{0,2},{1,3},{2,4},{3,5},{4,6},{5,7},{14,8},{15,9},{8,1... | collective-permute-start | bytes 393224 | tf_op jit(solution)/shard_map/ppermute | solution.py:194
  13.9 11.2 %collective-permute-start.2 = (bf16[256,256]{1,0:T(8,128)(2,1)S(1)}, bf16[256,256]{1,0:T(8,128)(2,1)S(1)}, u32[]{:S(2)}, u32[]{:S(2)}) collective-permute-start(bf16[256,256]{1,0:T(8,128)(2,1)S(1)} %constant_dynamic-update-slice_fusion), channel_id=1, source_target_pairs={{4,0},{5,1},{6,2},{7,3},{0,4},{1,5},{2,6},{3,7},{12,8},{13,9},{14,... | collective-permute-start | bytes 393224 | tf_op jit(solution)/shard_map/ppermute | solution.py:194
  17.5 7.7 %collective-permute-start.1 = (bf16[256,256]{1,0:T(8,128)(2,1)S(1)}, bf16[256,256]{1,0:T(8,128)(2,1)S(1)}, u32[]{:S(2)}, u32[]{:S(2)}) collective-permute-start(bf16[256,256]{1,0:T(8,128)(2,1)S(1)} %constant_dynamic-update-slice_fusion), channel_id=1, source_target_pairs={{2,0},{3,1},{4,2},{5,3},{6,4},{7,5},{0,6},{1,7},{10,8},{11,9},{12,... | collective-permute-start | bytes 393224 | tf_op jit(solution)/shard_map/ppermute | solution.py:194
  25.2 1.8 %collective-permute-start.5 = (bf16[3,256,256]{2,1,0:T(8,128)(2,1)S(1)}, bf16[3,256,256]{2,1,0:T(8,128)(2,1)S(1)}, u32[]{:S(2)}, u32[]{:S(2)}) collective-permute-start(bf16[3,256,256]{2,1,0:T(8,128)(2,1)S(1)} %stack.1.refs_0_), channel_id=1, source_target_pairs={{0,1},{1,0},{2,3},{3,2},{4,5},{5,4},{6,7},{7,6},{8,9},{9,8},{10,11... | collective-permute-start | bytes 1179656 | tf_op jit(solution)/shard_map/ppermute | solution.py:199
  41.4 12.5 %collective-permute-start.6 = (f32[4,128,256]{2,1,0:T(8,128)S(1)}, f32[4,128,256]{2,1,0:T(8,128)S(1)}, u32[]{:S(2)}, u32[]{:S(2)}) collective-permute-start(f32[4,128,256]{2,1,0:T(8,128)S(1)} %get-tuple-element.40), channel_id=1, source_target_pairs={{0,1},{1,0},{2,3},{3,2},{4,5},{5,4},{6,7},{7,6},{8,9},{9,8},{10,11... | collective-permute-start | bytes 1572872 | tf_op jit(solution)/shard_map/ppermute | solution.py:202
  41.7 18.5 %collective-permute-start.7 = (f32[4,128,256]{2,1,0:T(8,128)S(1)}, f32[4,128,256]{2,1,0:T(8,128)S(1)}, u32[]{:S(2)}, u32[]{:S(2)}) collective-permute-start(f32[4,128,256]{2,1,0:T(8,128)S(1)} %get-tuple-element.44), channel_id=1, source_target_pairs={{0,1},{1,0},{2,3},{3,2},{4,5},{5,4},{6,7},{7,6},{8,9},{9,8},{10,11... | collective-permute-start | bytes 1572872 | tf_op jit(solution)/shard_map/ppermute | solution.py:203
  54.0 8.9 %collective-permute-start.8 = (bf16[4,128,256]{2,1,0:T(8,128)(2,1)S(1)}, bf16[4,128,256]{2,1,0:T(8,128)(2,1)S(1)}, u32[]{:S(2)}, u32[]{:S(2)}) collective-permute-start(bf16[4,128,256]{2,1,0:T(8,128)(2,1)S(1)} %join.1), channel_id=1, source_target_pairs={{0,8},{1,9},{2,10},{3,11},{4,12},{5,13},{6,14},{7,15},{8,0},{9,1},... | collective-permute-start | bytes 786440 | tf_op jit(solution)/shard_map/ppermute | solution.py:207
  55.4 14.1 %all-to-all-start.2 = ((bf16[8,80,256]{2,1,0:T(8,128)(2,1)}), bf16[8,80,256]{2,1,0:T(8,128)(2,1)S(1)}, u32[]{:S(2)}, u32[]{:S(2)}) async-start(bf16[8,80,256]{2,1,0:T(8,128)(2,1)} %pack.1), calls=%async_computation.2 | async-start | bytes 655360 | tf_op jit(solution)/shard_map/all_to_all | solution.py:209
  63.0 6.6 %collective-permute-start.9 = (bf16[128,256]{1,0:T(8,128)(2,1)S(1)}, bf16[128,256]{1,0:T(8,128)(2,1)S(1)}, u32[]{:S(2)}, u32[]{:S(2)}) collective-permute-start(bf16[128,256]{1,0:T(8,128)(2,1)S(1)} %get-tuple-element.47), channel_id=1, source_target_pairs={{6,0},{7,1},{0,2},{1,3},{2,4},{3,5},{4,6},{5,7},{14,8},{15,9},{8,1... | collective-permute-start | bytes 196616 | tf_op jit(solution)/shard_map/ppermute | solution.py:212
  63.5 6.1 %collective-permute-start.10 = (bf16[128,256]{1,0:T(8,128)(2,1)S(1)}, bf16[128,256]{1,0:T(8,128)(2,1)S(1)}, u32[]{:S(2)}, u32[]{:S(2)}) collective-permute-start(bf16[128,256]{1,0:T(8,128)(2,1)S(1)} %get-tuple-element.48), channel_id=1, source_target_pairs={{4,0},{5,1},{6,2},{7,3},{0,4},{1,5},{2,6},{3,7},{12,8},{13,9},{14,... | collective-permute-start | bytes 196616 | tf_op jit(solution)/shard_map/ppermute | solution.py:212
  65.9 4.3 %collective-permute-start.11 = (bf16[128,256]{1,0:T(8,128)(2,1)S(1)}, bf16[128,256]{1,0:T(8,128)(2,1)S(1)}, u32[]{:S(2)}, u32[]{:S(2)}) collective-permute-start(bf16[128,256]{1,0:T(8,128)(2,1)S(1)} %get-tuple-element.49), channel_id=1, source_target_pairs={{2,0},{3,1},{4,2},{5,3},{6,4},{7,5},{0,6},{1,7},{10,8},{11,9},{12,... | collective-permute-start | bytes 196616 | tf_op jit(solution)/shard_map/ppermute | solution.py:212

commit v6 on v5

--- a/solution.py
+++ b/solution.py
@@ -14,6 +14,7 @@
 NB, NJ = 64, 512
 XL, Z, CORE = 2, 4, 2
 PEERS = 8
+AWAY = 2, 1, 3
 
 SPACE = range(XL * Z * CORE)
 TO_CORE = [(p, p ^ 1) for p in SPACE]
@@ -145,9 +146,9 @@
     return out
 
 
-def small(body, name, *out_shape):
+def small(body, name, *out_shape, room=8):
     shapes = [jax.ShapeDtypeStruct(shape, dtype) for shape, dtype in out_shape]
-    return pl.pallas_call(body, out_shape=shapes, compiler_params=pltpu.CompilerParams(vmem_limit_bytes=8 << 20), name=name)
+    return pl.pallas_call(body, out_shape=shapes, compiler_params=pltpu.CompilerParams(vmem_limit_bytes=room << 20), name=name)
 
 
 def repeat(x_ref, out_ref):
@@ -174,7 +175,7 @@
 
 def spread(x_ref, y_ref, across_ref, own_ref, *out_refs):
     own_ref[...] = x_ref[0] + y_ref[0] + across_ref[0].astype(F32)
-    for d, ref in enumerate(out_refs, 1):
+    for d, ref in zip(AWAY, out_refs):
         ref[...] = (x_ref[d] + y_ref[d] + across_ref[d].astype(F32)).astype(BF16)
 
 
@@ -186,7 +187,7 @@
 
 def on_device(target, a_factor, b_factor, c_factor):
     place = lax.axis_index("space").astype(jnp.int32).reshape(1)
-    (b_wide,) = small(repeat, "repeat", ((PEERS, NB, R), BF16))(b_factor)
+    (b_wide,) = small(repeat, "repeat", ((PEERS, NB, R), BF16), room=60)(b_factor)
     b_full = lax.all_to_all(b_wide, "samples", 0, 0).reshape(NJ, R)
     c_half = c_factor.astype(F32) * 0.5
     a_x = lax.ppermute(a_factor, "space", TO_XL)
@@ -209,7 +210,7 @@
     first = lax.all_to_all(first, "samples", 0, 0)
     piece = (SHARD, R)
     own, *away = small(spread, "spread", (piece, F32), *[(piece, BF16)] * 3)(own, own_core, across)
-    away = [lax.ppermute(x, "space", from_z(-d)) for d, x in enumerate(away, 1)]
+    away = [lax.ppermute(x, "space", from_z(-d)) for d, x in zip(AWAY, away)]
     first, *away = lax.optimization_barrier((first, *away))
     return tuple(small(finish, "finish", (piece, F32), ((NB, R), F32), ((K, R), F32))(first, own, *away))
 

time: 71.4 us -> 70.9 us (level)
  waiting for transfers between devices: 8.47 us -> 7.44 us
  local copies, waits for them, and re-layouts: 1.61 us -> 0.85 us
    pallas_call x1, Pallas kernels: 0.71 us -> 1.48 us  [on_device(): b_wide, = small(repeat, 'repeat', ((PEERS, NB, R), BF16), room=60)(b_factor)]
    unnamed x3 -> x1, local copies, waits for them, and re-layouts: 1.6 us -> 0.84 us
  transfers between devices with their start and end apart: 14 -> 14, of which waited for: 5 -> 5; matrix products, arithmetic and copies ran while one was open for 2% -> 2% of each run, Pallas kernels for 11% -> 12%
where the time goes in v6:
time: 70.9 us; the launch traced here: 70.4 us
  starting transfers between devices  25.3 us (36%)
  Pallas kernels  23.5 us (33%)
  blocking collectives  11.9 us (17%)
  waiting for transfers between devices  7.44 us (10%)
  local copies, waits for them, and re-layouts  0.85 us (1%)
  between operations  0.72 us (1%)
    pallas_call x2, Pallas kernels, local(): pl.pallas_call(functools.partial(body, last), grid_spec=pltpu.PrefetchSca...  20.4 us
    all_to_all x1, blocking collectives, on_device(): times = lax.all_to_all(times, 'space', 0, 0)  11.9 us
    all_to_all x1, starting transfers between devices, on_device(): b_full = lax.all_to_all(b_wide, 'samples', 0, 0).reshape(NJ, R)  6.64 us
    ppermute x3, starting transfers between devices, on_device(): lax.ppermute(pair, 'space', from_z(d))  6.51 us
    all_to_all x1, starting transfers between devices, on_device(): first = lax.all_to_all(first, 'samples', 0, 0)  4.68 us
    ppermute x3, starting transfers between devices, on_device(): away = [lax.ppermute(x, 'space', from_z(-d)) for d, x in zip(AWAY, away)]  4.43 us
    ppermute x1, waiting for transfers between devices, on_device(): across = lax.ppermute(across, 'space', TO_XL)  2.84 us
    all_to_all x1, waiting for transfers between devices, on_device(): first = lax.all_to_all(first, 'samples', 0, 0)  2.08 us
  transfers between devices with their start and end apart: 14, of which 5 were waited for; matrix products, arithmetic and copies ran while one was open for 2% of the time, Pallas kernels for 12%

profile of v6, /device:TPU:0, one launch (start us, length us, event | category | flops | bytes accessed | tf_op | source)
XLA Modules:
  0.0 70.4 jit_solution(17809481033802707119)
XLA Ops:
  0.6 1.7 %collective-permute-start = (bf16[128,256]{1,0:T(8,128)(2,1)}, bf16[128,256]{1,0:T(8,128)(2,1)S(1)}, u32[]{:S(2)}, u32[]{:S(2)}) collective-permute-start(bf16[128,256]{1,0:T(8,128)(2,1)} %param.5), channel_id=1, source_target_pairs={{0,8},{1,9},{2,10},{3,11},{4,12},{5,13},{6,14},{7,15},{8,0},{9,1},... | collective-permute-start | bytes 196616 | tf_op jit(solution)/shard_map/ppermute | solution.py:193
  2.3 1.5 %repeat.1 = bf16[8,64,256]{2,1,0:T(8,128)(2,1)} custom-call(bf16[64,256]{1,0:T(8,128)(2,1)} %x_ref.1), custom_call_target="tpu_custom_call" | custom-call | tf_op jit(solution)/shard_map/repeat/pallas_call | solution.py:190
  3.8 6.6 %all-to-all-start = ((bf16[8,64,256]{2,1,0:T(8,128)(2,1)}), bf16[8,64,256]{2,1,0:T(8,128)(2,1)S(1)}, u32[]{:S(2)}, u32[]{:S(2)}) async-start(bf16[8,64,256]{2,1,0:T(8,128)(2,1)} %repeat.1), calls=%async_computation | async-start | bytes 524288 | tf_op jit(solution)/shard_map/all_to_all | solution.py:191
  10.4 0.8 %constant_dynamic-update-slice_fusion.1 = bf16[256,256]{1,0:T(8,128)(2,1)S(1)} fusion(bf16[128,256]{1,0:T(8,128)(2,1)} %param.5), kind=kLoop, calls=%fused_computation.2 | loop fusion | bytes 131072
  11.2 0.0 collective-permute-done
  11.3 0.1 collective-permute-start.4
  11.4 0.7 convert_multiply_fusion.refs_3_
  12.0 1.9 %collective-permute-start.3 = (bf16[256,256]{1,0:T(8,128)(2,1)S(1)}, bf16[256,256]{1,0:T(8,128)(2,1)S(1)}, u32[]{:S(2)}, u32[]{:S(2)}) collective-permute-start(bf16[256,256]{1,0:T(8,128)(2,1)S(1)} %constant_dynamic-update-slice_fusion), channel_id=1, source_target_pairs={{6,0},{7,1},{0,2},{1,3},{2,4},{3,5},{4,6},{5,7},{14,8},{15,9},{8,1... | collective-permute-start | bytes 393224 | tf_op jit(solution)/shard_map/ppermute | solution.py:195
  14.0 3.6 %collective-permute-start.2 = (bf16[256,256]{1,0:T(8,128)(2,1)S(1)}, bf16[256,256]{1,0:T(8,128)(2,1)S(1)}, u32[]{:S(2)}, u32[]{:S(2)}) collective-permute-start(bf16[256,256]{1,0:T(8,128)(2,1)S(1)} %constant_dynamic-update-slice_fusion), channel_id=1, source_target_pairs={{4,0},{5,1},{6,2},{7,3},{0,4},{1,5},{2,6},{3,7},{12,8},{13,9},{14,... | collective-permute-start | bytes 393224 | tf_op jit(solution)/shard_map/ppermute | solution.py:195
  17.5 1.0 %collective-permute-start.1 = (bf16[256,256]{1,0:T(8,128)(2,1)S(1)}, bf16[256,256]{1,0:T(8,128)(2,1)S(1)}, u32[]{:S(2)}, u32[]{:S(2)}) collective-permute-start(bf16[256,256]{1,0:T(8,128)(2,1)S(1)} %constant_dynamic-update-slice_fusion), channel_id=1, source_target_pairs={{2,0},{3,1},{4,2},{5,3},{6,4},{7,5},{0,6},{1,7},{10,8},{11,9},{12,... | collective-permute-start | bytes 393224 | tf_op jit(solution)/shard_map/ppermute | solution.py:195
  18.6 0.0 collective-permute-done.4
  18.6 0.6 all-to-all-done
  19.2 6.0 %begin.1 = (f32[4,128,256]{2,1,0:T(8,128)S(1)}, f32[4,128,256]{2,1,0:T(8,128)S(1)}, f32[4,128,256]{2,1,0:T(8,128)S(1)}, f32[4,128,256]{2,1,0:T(8,128)S(1)}, f32[...) custom-call(s32[1]{0:T(128)} %bitcast.place, bf16[8,16,128,512]{3,2,1,0:T(8,128)(2,1)} %bitcast.9, ...), custom_call_target="tpu_custom_call" | custom-call | flops 3230000128 | bytes 5500000 | tf_op jit(solution)/shard_map/begin/pallas_call | solution.py:119
  25.2 0.0 collective-permute-done.3.refs_2_
  25.2 0.0 collective-permute-done.2.refs_1_
  25.2 0.0 collective-permute-done.1.refs_0_
  25.3 0.1 collective-permute-start.5
  25.3 1.7 %collective-permute-done.5.refs_1_ = bf16[3,256,256]{2,1,0:T(8,128)(2,1)S(1)} collective-permute-done((bf16[3,256,256]{2,1,0:T(8,128)(2,1)S(1)}, bf16[3,256,256]{2,1,0:T(8,128)(2,1)S(1)}, u32[]{:S(2)}, u32[]{:S(2)}) %collective-permute-start.5) | collective-permute-done | bytes 393248 | tf_op jit(solution)/shard_map/ppermute | solution.py:200
  27.1 14.4 %rest.1 = (f32[4,128,256]{2,1,0:T(8,128)S(1)}, f32[4,128,256]{2,1,0:T(8,128)S(1)}, f32[4,128,256]{2,1,0:T(8,128)S(1)}, f32[4,128,256]{2,1,0:T(8,128)S(1)}, bf16[...) custom-call(s32[1]{0:T(128)} %bitcast.place, ...), custom_call_target="tpu_custom_call", output_to_operand_aliasing={{0}: (11, {}), {1}: (12, {}), {2}: (13, {}), {3}: (14, {})} | custom-call | flops 9690000384 | bytes 16500000 | tf_op jit(solution)/shard_map/rest/pallas_call | solution.py:119
  41.4 0.2 collective-permute-start.6
  41.7 0.4 collective-permute-start.7
  42.0 11.9 %all_to_all.15.times_ref = bf16[16,16,256]{2,1,0:T(8,128)(2,1)S(1)} all-to-all(bf16[16,16,256]{2,1,0:T(8,128)(2,1)S(1)} %get-tuple-element.39), channel_id=1, replica_groups=mesh['samples'=8,'space'=16] {'space'}, dimensions={0} | all-to-all | bytes 262144 | tf_op jit(solution)/shard_map/all_to_all | solution.py:205
  53.9 0.0 collective-permute-done.6.y_ref
  54.0 0.6 collective-permute-start.8
  54.6 0.8 %pack.1 = bf16[8,80,256]{2,1,0:T(8,128)(2,1)} custom-call(bf16[16,16,256]{2,1,0:T(8,128)(2,1)S(1)} %all_to_all.15.times_ref, bf16[512,256]{1,0:T(8,128)(2,1)S(1)} %get-tuple-element.42.gb_ref), custom_call_target="tpu_custom_call" | custom-call | tf_op jit(solution)/shard_map/pack/pallas_call | solution.py:209
  55.4 4.7 %all-to-all-start.2 = ((bf16[8,80,256]{2,1,0:T(8,128)(2,1)}), bf16[8,80,256]{2,1,0:T(8,128)(2,1)S(1)}, u32[]{:S(2)}, u32[]{:S(2)}) async-start(bf16[8,80,256]{2,1,0:T(8,128)(2,1)} %pack.1), calls=%async_computation.2 | async-start | bytes 655360 | tf_op jit(solution)/shard_map/all_to_all | solution.py:210
  60.1 0.0 collective-permute-done.7.y_ref
  60.1 2.8 %collective-permute-done.8.across_ref = bf16[4,128,256]{2,1,0:T(8,128)(2,1)S(1)} collective-permute-done((bf16[4,128,256]{2,1,0:T(8,128)(2,1)S(1)}, bf16[4,128,256]{2,1,0:T(8,128)(2,1)S(1)}, u32[]{:S(2)}, u32[]{:S(2)}) %collective-permute-start.8) | collective-permute-done | bytes 262176 | tf_op jit(solution)/shard_map/ppermute | solution.py:208
  62.9 0.1 spread.1
  63.0 1.2 %collective-permute-start.9 = (bf16[128,256]{1,0:T(8,128)(2,1)S(1)}, bf16[128,256]{1,0:T(8,128)(2,1)S(1)}, u32[]{:S(2)}, u32[]{:S(2)}) collective-permute-start(bf16[128,256]{1,0:T(8,128)(2,1)S(1)} %get-tuple-element.47), channel_id=1, source_target_pairs={{4,0},{5,1},{6,2},{7,3},{0,4},{1,5},{2,6},{3,7},{12,8},{13,9},{14,... | collective-permute-start | bytes 196616 | tf_op jit(solution)/shard_map/ppermute | solution.py:213
  64.2 1.1 %collective-permute-start.10 = (bf16[128,256]{1,0:T(8,128)(2,1)S(1)}, bf16[128,256]{1,0:T(8,128)(2,1)S(1)}, u32[]{:S(2)}, u32[]{:S(2)}) collective-permute-start(bf16[128,256]{1,0:T(8,128)(2,1)S(1)} %get-tuple-element.48), channel_id=1, source_target_pairs={{6,0},{7,1},{0,2},{1,3},{2,4},{3,5},{4,6},{5,7},{14,8},{15,9},{8,1... | collective-permute-start | bytes 196616 | tf_op jit(solution)/shard_map/ppermute | solution.py:213
  65.3 2.1 %collective-permute-start.11 = (bf16[128,256]{1,0:T(8,128)(2,1)S(1)}, bf16[128,256]{1,0:T(8,128)(2,1)S(1)}, u32[]{:S(2)}, u32[]{:S(2)}) collective-permute-start(bf16[128,256]{1,0:T(8,128)(2,1)S(1)} %get-tuple-element.49), channel_id=1, source_target_pairs={{2,0},{3,1},{4,2},{5,3},{6,4},{7,5},{0,6},{1,7},{10,8},{11,9},{12,... | collective-permute-start | bytes 196616 | tf_op jit(solution)/shard_map/ppermute | solution.py:213
  67.4 2.1 %all-to-all-done.2.first_ref = bf16[8,80,256]{2,1,0:T(8,128)(2,1)S(1)} async-done(((bf16[8,80,256]{2,1,0:T(8,128)(2,1)}), bf16[8,80,256]{2,1,0:T(8,128)(2,1)S(1)}, u32[]{:S(2)}, u32[]{:S(2)}) %all-to-all-start.2) | async-done | bytes 327712 | tf_op jit(solution)/shard_map/all_to_all | solution.py:210
  69.5 0.0 collective-permute-done.9.g1
  69.5 0.2 collective-permute-done.10.g2
  69.7 0.0 collective-permute-done.11.g3
  69.7 0.7 %finish.1 = (f32[128,256]{1,0:T(8,128)}, f32[64,256]{1,0:T(8,128)}, f32[8,256]{1,0:T(8,128)}) custom-call(bf16[8,80,256]{2,1,0:T(8,128)(2,1)S(1)} %all-to-all-done.2.first_ref, f32[128,256]{1,0:T(8,128)S(1)} %get-tuple-element.51.own_ref, bf16[128,256]{1,0:T(8,128)(2,1)S(1)} %collective-permute-done.9.g1, bf16[128,256]{1,0:T(8,128)(2,1)S(1)} %collective-permute-done.10.g2, ...), custom_call_target="tpu_custom_call" | custom-call | tf_op jit(solution)/shard_map/finish/pallas_call | solution.py:215
  (3 shorter events, 0.1 us)
Async XLA Ops:
  0.6 10.6 %collective-permute-start = (bf16[128,256]{1,0:T(8,128)(2,1)}, bf16[128,256]{1,0:T(8,128)(2,1)S(1)}, u32[]{:S(2)}, u32[]{:S(2)}) collective-permute-start(bf16[128,256]{1,0:T(8,128)(2,1)} %param.5), channel_id=1, source_target_pairs={{0,8},{1,9},{2,10},{3,11},{4,12},{5,13},{6,14},{7,15},{8,0},{9,1},... | collective-permute-start | bytes 196616 | tf_op jit(solution)/shard_map/ppermute | solution.py:193
  3.8 15.4 %all-to-all-start = ((bf16[8,64,256]{2,1,0:T(8,128)(2,1)}), bf16[8,64,256]{2,1,0:T(8,128)(2,1)S(1)}, u32[]{:S(2)}, u32[]{:S(2)}) async-start(bf16[8,64,256]{2,1,0:T(8,128)(2,1)} %repeat.1), calls=%async_computation | async-start | bytes 524288 | tf_op jit(solution)/shard_map/all_to_all | solution.py:191
  11.3 7.3 %collective-permute-start.4 = (bf16[256,256]{1,0:T(8,128)(2,1)S(1)}, bf16[256,256]{1,0:T(8,128)(2,1)S(1)}, u32[]{:S(2)}, u32[]{:S(2)}) collective-permute-start(bf16[256,256]{1,0:T(8,128)(2,1)S(1)} %constant_dynamic-update-slice_fusion), channel_id=1, source_target_pairs={{0,1},{1,0},{2,3},{3,2},{4,5},{5,4},{6,7},{7,6},{8,9},{9,8},{10,11... | collective-permute-start | bytes 393224 | tf_op jit(solution)/shard_map/ppermute | solution.py:197
  12.0 13.1 %collective-permute-start.3 = (bf16[256,256]{1,0:T(8,128)(2,1)S(1)}, bf16[256,256]{1,0:T(8,128)(2,1)S(1)}, u32[]{:S(2)}, u32[]{:S(2)}) collective-permute-start(bf16[256,256]{1,0:T(8,128)(2,1)S(1)} %constant_dynamic-update-slice_fusion), channel_id=1, source_target_pairs={{6,0},{7,1},{0,2},{1,3},{2,4},{3,5},{4,6},{5,7},{14,8},{15,9},{8,1... | collective-permute-start | bytes 393224 | tf_op jit(solution)/shard_map/ppermute | solution.py:195
  14.0 11.2 %collective-permute-start.2 = (bf16[256,256]{1,0:T(8,128)(2,1)S(1)}, bf16[256,256]{1,0:T(8,128)(2,1)S(1)}, u32[]{:S(2)}, u32[]{:S(2)}) collective-permute-start(bf16[256,256]{1,0:T(8,128)(2,1)S(1)} %constant_dynamic-update-slice_fusion), channel_id=1, source_target_pairs={{4,0},{5,1},{6,2},{7,3},{0,4},{1,5},{2,6},{3,7},{12,8},{13,9},{14,... | collective-permute-start | bytes 393224 | tf_op jit(solution)/shard_map/ppermute | solution.py:195
  17.5 7.7 %collective-permute-start.1 = (bf16[256,256]{1,0:T(8,128)(2,1)S(1)}, bf16[256,256]{1,0:T(8,128)(2,1)S(1)}, u32[]{:S(2)}, u32[]{:S(2)}) collective-permute-start(bf16[256,256]{1,0:T(8,128)(2,1)S(1)} %constant_dynamic-update-slice_fusion), channel_id=1, source_target_pairs={{2,0},{3,1},{4,2},{5,3},{6,4},{7,5},{0,6},{1,7},{10,8},{11,9},{12,... | collective-permute-start | bytes 393224 | tf_op jit(solution)/shard_map/ppermute | solution.py:195
  25.3 1.8 %collective-permute-start.5 = (bf16[3,256,256]{2,1,0:T(8,128)(2,1)S(1)}, bf16[3,256,256]{2,1,0:T(8,128)(2,1)S(1)}, u32[]{:S(2)}, u32[]{:S(2)}) collective-permute-start(bf16[3,256,256]{2,1,0:T(8,128)(2,1)S(1)} %stack.1.refs_0_), channel_id=1, source_target_pairs={{0,1},{1,0},{2,3},{3,2},{4,5},{5,4},{6,7},{7,6},{8,9},{9,8},{10,11... | collective-permute-start | bytes 1179656 | tf_op jit(solution)/shard_map/ppermute | solution.py:200
  41.4 12.5 %collective-permute-start.6 = (f32[4,128,256]{2,1,0:T(8,128)S(1)}, f32[4,128,256]{2,1,0:T(8,128)S(1)}, u32[]{:S(2)}, u32[]{:S(2)}) collective-permute-start(f32[4,128,256]{2,1,0:T(8,128)S(1)} %get-tuple-element.40), channel_id=1, source_target_pairs={{0,1},{1,0},{2,3},{3,2},{4,5},{5,4},{6,7},{7,6},{8,9},{9,8},{10,11... | collective-permute-start | bytes 1572872 | tf_op jit(solution)/shard_map/ppermute | solution.py:203
  41.7 18.4 %collective-permute-start.7 = (f32[4,128,256]{2,1,0:T(8,128)S(1)}, f32[4,128,256]{2,1,0:T(8,128)S(1)}, u32[]{:S(2)}, u32[]{:S(2)}) collective-permute-start(f32[4,128,256]{2,1,0:T(8,128)S(1)} %get-tuple-element.44), channel_id=1, source_target_pairs={{0,1},{1,0},{2,3},{3,2},{4,5},{5,4},{6,7},{7,6},{8,9},{9,8},{10,11... | collective-permute-start | bytes 1572872 | tf_op jit(solution)/shard_map/ppermute | solution.py:204
  54.0 8.9 %collective-permute-start.8 = (bf16[4,128,256]{2,1,0:T(8,128)(2,1)S(1)}, bf16[4,128,256]{2,1,0:T(8,128)(2,1)S(1)}, u32[]{:S(2)}, u32[]{:S(2)}) collective-permute-start(bf16[4,128,256]{2,1,0:T(8,128)(2,1)S(1)} %join.1), channel_id=1, source_target_pairs={{0,8},{1,9},{2,10},{3,11},{4,12},{5,13},{6,14},{7,15},{8,0},{9,1},... | collective-permute-start | bytes 786440 | tf_op jit(solution)/shard_map/ppermute | solution.py:208
  55.4 14.1 %all-to-all-start.2 = ((bf16[8,80,256]{2,1,0:T(8,128)(2,1)}), bf16[8,80,256]{2,1,0:T(8,128)(2,1)S(1)}, u32[]{:S(2)}, u32[]{:S(2)}) async-start(bf16[8,80,256]{2,1,0:T(8,128)(2,1)} %pack.1), calls=%async_computation.2 | async-start | bytes 655360 | tf_op jit(solution)/shard_map/all_to_all | solution.py:210
  63.0 6.5 %collective-permute-start.9 = (bf16[128,256]{1,0:T(8,128)(2,1)S(1)}, bf16[128,256]{1,0:T(8,128)(2,1)S(1)}, u32[]{:S(2)}, u32[]{:S(2)}) collective-permute-start(bf16[128,256]{1,0:T(8,128)(2,1)S(1)} %get-tuple-element.47), channel_id=1, source_target_pairs={{4,0},{5,1},{6,2},{7,3},{0,4},{1,5},{2,6},{3,7},{12,8},{13,9},{14,... | collective-permute-start | bytes 196616 | tf_op jit(solution)/shard_map/ppermute | solution.py:213
  64.2 5.5 %collective-permute-start.10 = (bf16[128,256]{1,0:T(8,128)(2,1)S(1)}, bf16[128,256]{1,0:T(8,128)(2,1)S(1)}, u32[]{:S(2)}, u32[]{:S(2)}) collective-permute-start(bf16[128,256]{1,0:T(8,128)(2,1)S(1)} %get-tuple-element.48), channel_id=1, source_target_pairs={{6,0},{7,1},{0,2},{1,3},{2,4},{3,5},{4,6},{5,7},{14,8},{15,9},{8,1... | collective-permute-start | bytes 196616 | tf_op jit(solution)/shard_map/ppermute | solution.py:213
  65.3 4.4 %collective-permute-start.11 = (bf16[128,256]{1,0:T(8,128)(2,1)S(1)}, bf16[128,256]{1,0:T(8,128)(2,1)S(1)}, u32[]{:S(2)}, u32[]{:S(2)}) collective-permute-start(bf16[128,256]{1,0:T(8,128)(2,1)S(1)} %get-tuple-element.49), channel_id=1, source_target_pairs={{2,0},{3,1},{4,2},{5,3},{6,4},{7,5},{0,6},{1,7},{10,8},{11,9},{12,... | collective-permute-start | bytes 196616 | tf_op jit(solution)/shard_map/ppermute | solution.py:213

commit v7 on v6

--- a/solution.py
+++ b/solution.py
@@ -45,7 +45,7 @@
 def body(last, place, t0, t1, t2, t3, *refs):
     steps = 3 if last else 1
     mine, theirs, refs = refs[0], refs[1], refs[2:]
-    b_ref, c_ref, refs = refs[0], refs[1], refs[2:]
+    b_ref, refs = refs[0], refs[1:]
     if last:
         gb_in, gc_in, refs = refs[0], refs[1], refs[6:]
     parts, outs, w_ref, a_ref = refs[:4], refs[4:-2], refs[-2], refs[-1]
@@ -55,8 +55,8 @@
     rows = a_ref[...]
     wide = rows.astype(F32)
     rows_t = rows.T
-    b = b_ref[...]
-    c_half = c_ref[...]
+    b = jnp.concatenate([b_ref[peer, :NB] for peer in range(PEERS)], axis=0)
+    c_half = b_ref[0, NB : NB + K].astype(F32) * 0.5
     grad = jnp.zeros((GROUP, R), F32)
     for k in range(K):
         ck = c_half[k : k + 1, :]
@@ -75,7 +75,7 @@
         total = gb_in[...] if last else jnp.zeros((R, NJ), F32)
         lane = lax.broadcasted_iota(jnp.int32, (R, 128), 1)
         sums = jnp.zeros((R, 128), F32)
-        bt = b_ref[...].T.astype(F32)
+        bt = b.T.astype(F32)
         c_t = jnp.concatenate([c_half, jnp.zeros((128 - K, R), F32)], axis=0).T
         for k in range(K):
             wk = w_ref[k]
@@ -93,7 +93,7 @@
             outs[1][peer] = jnp.concatenate([high, low], axis=0)
 
 
-def local(place, target, pieces, b_full, c_half, *before):
+def local(place, target, pieces, b_full, *before):
     last = bool(before)
     steps, shift = (3, 1) if last else (1, 0)
 
@@ -121,7 +121,7 @@
         grid_spec=pltpu.PrefetchScalarGridSpec(
             num_scalar_prefetch=1,
             grid=(steps,),
-            in_specs=[tile(q) for q in range(4)] + [whole(steps, 2 * SHARD, R)] * 2 + [whole(NJ, R), whole(K, R)] + carried,
+            in_specs=[tile(q) for q in range(4)] + [whole(steps, 2 * SHARD, R)] * 2 + [whole(PEERS, NB + K, R)] + carried,
             out_specs=[out] * 4 + [whole(*shape) for shape, _ in after],
             scratch_shapes=[
                 pltpu.VMEM((K, R, NJ), F32),
@@ -130,13 +130,13 @@
         ),
         out_shape=[jax.ShapeDtypeStruct((Z, SHARD, R), F32)] * 4
         + [jax.ShapeDtypeStruct(shape, dtype) for shape, dtype in after],
-        input_output_aliases={11 + i: i for i in range(4)} if last else {},
+        input_output_aliases={10 + i: i for i in range(4)} if last else {},
         compiler_params=pltpu.CompilerParams(vmem_limit_bytes=VMEM_LIMIT),
         cost_estimate=pl.CostEstimate(
             flops=3_230_000_000 * steps, bytes_accessed=5_500_000 * steps, transcendentals=2_100_000 * steps
         ),
         name="rest" if last else "begin",
-    )(place, target, target, target, target, *pieces, b_full, c_half, *before)
+    )(place, target, target, target, target, *pieces, b_full, *before)
 
 
 def total(ref, first, rows):
@@ -151,9 +151,11 @@
     return pl.pallas_call(body, out_shape=shapes, compiler_params=pltpu.CompilerParams(vmem_limit_bytes=room << 20), name=name)
 
 
-def repeat(x_ref, out_ref):
+def repeat(b_ref, c_ref, out_ref):
+    c = c_ref[...]
     for peer in range(PEERS):
-        out_ref[peer] = x_ref[...]
+        out_ref[peer, :NB] = b_ref[...]
+        out_ref[peer, NB:] = c
 
 
 def stack(*refs):
@@ -187,18 +189,17 @@
 
 def on_device(target, a_factor, b_factor, c_factor):
     place = lax.axis_index("space").astype(jnp.int32).reshape(1)
-    (b_wide,) = small(repeat, "repeat", ((PEERS, NB, R), BF16), room=60)(b_factor)
-    b_full = lax.all_to_all(b_wide, "samples", 0, 0).reshape(NJ, R)
-    c_half = c_factor.astype(F32) * 0.5
+    (b_wide,) = small(repeat, "repeat", ((PEERS, NB + K, R), BF16), room=60)(b_factor, c_factor)
+    b_full = lax.all_to_all(b_wide, "samples", 0, 0)
     a_x = lax.ppermute(a_factor, "space", TO_XL)
     pair = jnp.concatenate([a_factor, a_x], axis=0)
     mine = [lax.ppermute(pair, "space", from_z(d)) if d else pair for d in range(Z)]
     target = target.reshape(K, 16, SHARD, NJ)
-    *parts, gb, gc = local(place, target, [pair[None], lax.ppermute(pair, "space", TO_CORE)[None]], b_full, c_half)
+    *parts, gb, gc = local(place, target, [pair[None], lax.ppermute(pair, "space", TO_CORE)[None]], b_full)
     *mine, gc = lax.optimization_barrier((*mine[1:], gc))
     (mine,) = small(stack, "stack", ((Z - 1, 2 * SHARD, R), BF16))(*mine)
     pieces = [mine, lax.ppermute(mine, "space", TO_CORE)]
-    own, far, own_core, far_core, first, times = local(place, target, pieces, b_full, c_half, gb, gc, *parts)
+    own, far, own_core, far_core, first, times = local(place, target, pieces, b_full, gb, gc, *parts)
 
     far_core = lax.ppermute(far_core, "space", TO_CORE)
     own_core = lax.ppermute(own_core, "space", TO_CORE)

time: 70.9 us -> 71.3 us (level)
  waiting for transfers between devices: 7.44 us -> 9.66 us
  starting transfers between devices: 25.3 us -> 24.2 us
    ppermute x1, waiting for transfers between devices: 2.84 us -> 4.05 us  [on_device(): across = lax.ppermute(across, 'space', TO_XL)]
    ppermute x3, waiting for transfers between devices: 0.16 us -> 1.25 us  [on_device(): away = [lax.ppermute(x, 'space', from_z(-d)) for d, x in zip(AWAY, away)]]
    all_to_all x1, waiting for transfers between devices: 2.08 us -> 1.22 us  [on_device(): first = lax.all_to_all(first, 'samples', 0, 0)]
    all_to_all x1, starting transfers between devices: 4.68 us -> 3.82 us  [on_device(): first = lax.all_to_all(first, 'samples', 0, 0)]
    all_to_all x1, waiting for transfers between devices: 0.63 us -> 1.43 us  [on_device(): b_full = lax.all_to_all(b_wide, 'samples', 0, 0)]
  transfers between devices with their start and end apart: 14 -> 14, of which waited for: 5 -> 6; matrix products, arithmetic and copies ran while one was open for 2% -> 1% of each run, Pallas kernels for 12% -> 12%
where the time goes in v7:
time: 71.3 us; the launch traced here: 70.8 us
  starting transfers between devices  24.2 us (34%)
  Pallas kernels  23.5 us (33%)
  blocking collectives  11.9 us (17%)
  waiting for transfers between devices  9.66 us (14%)
  local copies, waits for them, and re-layouts  0.85 us (1%)
  between operations  0.72 us (1%)
    pallas_call x2, Pallas kernels, local(): pl.pallas_call(functools.partial(body, last), grid_spec=pltpu.PrefetchSca...  20.4 us
    all_to_all x1, blocking collectives, on_device(): times = lax.all_to_all(times, 'space', 0, 0)  11.9 us
    all_to_all x1, starting transfers between devices, on_device(): b_full = lax.all_to_all(b_wide, 'samples', 0, 0)  6.64 us
    ppermute x3, starting transfers between devices, on_device(): lax.ppermute(pair, 'space', from_z(d))  6.58 us
    ppermute x3, starting transfers between devices, on_device(): away = [lax.ppermute(x, 'space', from_z(-d)) for d, x in zip(AWAY, away)]  4.09 us
    ppermute x1, waiting for transfers between devices, on_device(): across = lax.ppermute(across, 'space', TO_XL)  4.05 us
    all_to_all x1, starting transfers between devices, on_device(): first = lax.all_to_all(first, 'samples', 0, 0)  3.82 us
    ppermute x1, waiting for transfers between devices, on_device(): pieces = [mine, lax.ppermute(mine, 'space', TO_CORE)]  1.71 us
  transfers between devices with their start and end apart: 14, of which 6 were waited for; matrix products, arithmetic and copies ran while one was open for 1% of the time, Pallas kernels for 12%

profile of v7, /device:TPU:0, one launch (start us, length us, event | category | flops | bytes accessed | tf_op | source)
XLA Modules:
  0.0 70.8 jit_solution(5115298876986014138)
XLA Ops:
  0.6 1.7 %collective-permute-start = (bf16[128,256]{1,0:T(8,128)(2,1)}, bf16[128,256]{1,0:T(8,128)(2,1)S(1)}, u32[]{:S(2)}, u32[]{:S(2)}) collective-permute-start(bf16[128,256]{1,0:T(8,128)(2,1)} %param.5), channel_id=1, source_target_pairs={{0,8},{1,9},{2,10},{3,11},{4,12},{5,13},{6,14},{7,15},{8,0},{9,1},... | collective-permute-start | bytes 196616 | tf_op jit(solution)/shard_map/ppermute | solution.py:194
  2.3 1.5 %repeat.1 = bf16[8,72,256]{2,1,0:T(8,128)(2,1)} custom-call(bf16[64,256]{1,0:T(8,128)(2,1)} %b_ref.1, bf16[8,256]{1,0:T(8,128)(2,1)} %c_ref.1), custom_call_target="tpu_custom_call" | custom-call | tf_op jit(solution)/shard_map/repeat/pallas_call | solution.py:192
  3.8 6.6 %all-to-all-start = ((bf16[8,72,256]{2,1,0:T(8,128)(2,1)}), bf16[8,72,256]{2,1,0:T(8,128)(2,1)S(1)}, u32[]{:S(2)}, u32[]{:S(2)}) async-start(bf16[8,72,256]{2,1,0:T(8,128)(2,1)} %repeat.1), calls=%async_computation | async-start | bytes 589824 | tf_op jit(solution)/shard_map/all_to_all | solution.py:193
  10.4 0.8 %constant_dynamic-update-slice_fusion.1 = bf16[256,256]{1,0:T(8,128)(2,1)S(1)} fusion(bf16[128,256]{1,0:T(8,128)(2,1)} %param.5), kind=kLoop, calls=%fused_computation.1 | loop fusion | bytes 131072
  11.3 0.0 collective-permute-done
  11.3 0.1 collective-permute-start.4
  11.4 2.0 %collective-permute-start.3 = (bf16[256,256]{1,0:T(8,128)(2,1)S(1)}, bf16[256,256]{1,0:T(8,128)(2,1)S(1)}, u32[]{:S(2)}, u32[]{:S(2)}) collective-permute-start(bf16[256,256]{1,0:T(8,128)(2,1)S(1)} %constant_dynamic-update-slice_fusion), channel_id=1, source_target_pairs={{6,0},{7,1},{0,2},{1,3},{2,4},{3,5},{4,6},{5,7},{14,8},{15,9},{8,1... | collective-permute-start | bytes 393224 | tf_op jit(solution)/shard_map/ppermute | solution.py:196
  13.4 3.6 %collective-permute-start.2 = (bf16[256,256]{1,0:T(8,128)(2,1)S(1)}, bf16[256,256]{1,0:T(8,128)(2,1)S(1)}, u32[]{:S(2)}, u32[]{:S(2)}) collective-permute-start(bf16[256,256]{1,0:T(8,128)(2,1)S(1)} %constant_dynamic-update-slice_fusion), channel_id=1, source_target_pairs={{4,0},{5,1},{6,2},{7,3},{0,4},{1,5},{2,6},{3,7},{12,8},{13,9},{14,... | collective-permute-start | bytes 393224 | tf_op jit(solution)/shard_map/ppermute | solution.py:196
  16.9 1.0 %collective-permute-start.1 = (bf16[256,256]{1,0:T(8,128)(2,1)S(1)}, bf16[256,256]{1,0:T(8,128)(2,1)S(1)}, u32[]{:S(2)}, u32[]{:S(2)}) collective-permute-start(bf16[256,256]{1,0:T(8,128)(2,1)S(1)} %constant_dynamic-update-slice_fusion), channel_id=1, source_target_pairs={{2,0},{3,1},{4,2},{5,3},{6,4},{7,5},{0,6},{1,7},{10,8},{11,9},{12,... | collective-permute-start | bytes 393224 | tf_op jit(solution)/shard_map/ppermute | solution.py:196
  17.9 0.0 collective-permute-done.4
  17.9 1.4 %all-to-all-done.refs_2_ = bf16[8,72,256]{2,1,0:T(8,128)(2,1)S(1)} async-done(((bf16[8,72,256]{2,1,0:T(8,128)(2,1)}), bf16[8,72,256]{2,1,0:T(8,128)(2,1)S(1)}, u32[]{:S(2)}, u32[]{:S(2)}) %all-to-all-start) | async-done | bytes 294944 | tf_op jit(solution)/shard_map/all_to_all | solution.py:193
  19.4 6.0 %begin.1 = (f32[4,128,256]{2,1,0:T(8,128)S(1)}, f32[4,128,256]{2,1,0:T(8,128)S(1)}, f32[4,128,256]{2,1,0:T(8,128)S(1)}, f32[4,128,256]{2,1,0:T(8,128)S(1)}, f32[...) custom-call(s32[1]{0:T(128)} %bitcast.place, bf16[8,16,128,512]{3,2,1,0:T(8,128)(2,1)} %bitcast.6, ...), custom_call_target="tpu_custom_call" | custom-call | flops 3230000128 | bytes 5500000 | tf_op jit(solution)/shard_map/begin/pallas_call | solution.py:119
  25.4 0.0 collective-permute-done.3.refs_2_
  25.4 0.0 collective-permute-done.2.refs_1_
  25.4 0.0 collective-permute-done.1.refs_0_
  25.4 0.1 collective-permute-start.5
  25.5 1.7 %collective-permute-done.5.refs_1_ = bf16[3,256,256]{2,1,0:T(8,128)(2,1)S(1)} collective-permute-done((bf16[3,256,256]{2,1,0:T(8,128)(2,1)S(1)}, bf16[3,256,256]{2,1,0:T(8,128)(2,1)S(1)}, u32[]{:S(2)}, u32[]{:S(2)}) %collective-permute-start.5) | collective-permute-done | bytes 393248 | tf_op jit(solution)/shard_map/ppermute | solution.py:201
  27.2 14.4 %rest.1 = (f32[4,128,256]{2,1,0:T(8,128)S(1)}, f32[4,128,256]{2,1,0:T(8,128)S(1)}, f32[4,128,256]{2,1,0:T(8,128)S(1)}, f32[4,128,256]{2,1,0:T(8,128)S(1)}, bf16[...) custom-call(s32[1]{0:T(128)} %bitcast.place, ...), custom_call_target="tpu_custom_call", output_to_operand_aliasing={{0}: (10, {}), {1}: (11, {}), {2}: (12, {}), {3}: (13, {})} | custom-call | flops 9690000384 | bytes 16500000 | tf_op jit(solution)/shard_map/rest/pallas_call | solution.py:119
  41.6 0.2 collective-permute-start.6
  41.8 0.4 collective-permute-start.7
  42.2 11.9 %all_to_all.15.times_ref = bf16[16,16,256]{2,1,0:T(8,128)(2,1)S(1)} all-to-all(bf16[16,16,256]{2,1,0:T(8,128)(2,1)S(1)} %get-tuple-element.39), channel_id=1, replica_groups=mesh['samples'=8,'space'=16] {'space'}, dimensions={0} | all-to-all | bytes 262144 | tf_op jit(solution)/shard_map/all_to_all | solution.py:206
  54.1 0.0 collective-permute-done.6.y_ref
  54.2 0.6 collective-permute-start.8
  54.8 0.8 %pack.1 = bf16[8,80,256]{2,1,0:T(8,128)(2,1)} custom-call(bf16[16,16,256]{2,1,0:T(8,128)(2,1)S(1)} %all_to_all.15.times_ref, bf16[512,256]{1,0:T(8,128)(2,1)S(1)} %get-tuple-element.42.gb_ref), custom_call_target="tpu_custom_call" | custom-call | tf_op jit(solution)/shard_map/pack/pallas_call | solution.py:210
  55.6 3.8 %all-to-all-start.2 = ((bf16[8,80,256]{2,1,0:T(8,128)(2,1)}), bf16[8,80,256]{2,1,0:T(8,128)(2,1)S(1)}, u32[]{:S(2)}, u32[]{:S(2)}) async-start(bf16[8,80,256]{2,1,0:T(8,128)(2,1)} %pack.1), calls=%async_computation.2 | async-start | bytes 655360 | tf_op jit(solution)/shard_map/all_to_all | solution.py:211
  59.4 0.0 collective-permute-done.7.y_ref
  59.4 4.0 %collective-permute-done.8.across_ref = bf16[4,128,256]{2,1,0:T(8,128)(2,1)S(1)} collective-permute-done((bf16[4,128,256]{2,1,0:T(8,128)(2,1)S(1)}, bf16[4,128,256]{2,1,0:T(8,128)(2,1)S(1)}, u32[]{:S(2)}, u32[]{:S(2)}) %collective-permute-start.8) | collective-permute-done | bytes 262176 | tf_op jit(solution)/shard_map/ppermute | solution.py:209
  63.5 0.1 spread.1
  63.5 0.9 %collective-permute-start.9 = (bf16[128,256]{1,0:T(8,128)(2,1)S(1)}, bf16[128,256]{1,0:T(8,128)(2,1)S(1)}, u32[]{:S(2)}, u32[]{:S(2)}) collective-permute-start(bf16[128,256]{1,0:T(8,128)(2,1)S(1)} %get-tuple-element.47), channel_id=1, source_target_pairs={{4,0},{5,1},{6,2},{7,3},{0,4},{1,5},{2,6},{3,7},{12,8},{13,9},{14,... | collective-permute-start | bytes 196616 | tf_op jit(solution)/shard_map/ppermute | solution.py:214
  64.4 1.1 %collective-permute-start.10 = (bf16[128,256]{1,0:T(8,128)(2,1)S(1)}, bf16[128,256]{1,0:T(8,128)(2,1)S(1)}, u32[]{:S(2)}, u32[]{:S(2)}) collective-permute-start(bf16[128,256]{1,0:T(8,128)(2,1)S(1)} %get-tuple-element.48), channel_id=1, source_target_pairs={{6,0},{7,1},{0,2},{1,3},{2,4},{3,5},{4,6},{5,7},{14,8},{15,9},{8,1... | collective-permute-start | bytes 196616 | tf_op jit(solution)/shard_map/ppermute | solution.py:214
  65.5 2.1 %collective-permute-start.11 = (bf16[128,256]{1,0:T(8,128)(2,1)S(1)}, bf16[128,256]{1,0:T(8,128)(2,1)S(1)}, u32[]{:S(2)}, u32[]{:S(2)}) collective-permute-start(bf16[128,256]{1,0:T(8,128)(2,1)S(1)} %get-tuple-element.49), channel_id=1, source_target_pairs={{2,0},{3,1},{4,2},{5,3},{6,4},{7,5},{0,6},{1,7},{10,8},{11,9},{12,... | collective-permute-start | bytes 196616 | tf_op jit(solution)/shard_map/ppermute | solution.py:214
  67.6 1.2 %all-to-all-done.2.first_ref = bf16[8,80,256]{2,1,0:T(8,128)(2,1)S(1)} async-done(((bf16[8,80,256]{2,1,0:T(8,128)(2,1)}), bf16[8,80,256]{2,1,0:T(8,128)(2,1)S(1)}, u32[]{:S(2)}, u32[]{:S(2)}) %all-to-all-start.2) | async-done | bytes 327712 | tf_op jit(solution)/shard_map/all_to_all | solution.py:211
  68.8 0.6 collective-permute-done.9.g1
  69.4 0.7 collective-permute-done.10.g2
  70.1 0.0 collective-permute-done.11.g3
  70.1 0.7 %finish.1 = (f32[128,256]{1,0:T(8,128)}, f32[64,256]{1,0:T(8,128)}, f32[8,256]{1,0:T(8,128)}) custom-call(bf16[8,80,256]{2,1,0:T(8,128)(2,1)S(1)} %all-to-all-done.2.first_ref, f32[128,256]{1,0:T(8,128)S(1)} %get-tuple-element.51.own_ref, bf16[128,256]{1,0:T(8,128)(2,1)S(1)} %collective-permute-done.9.g1, bf16[128,256]{1,0:T(8,128)(2,1)S(1)} %collective-permute-done.10.g2, ...), custom_call_target="tpu_custom_call" | custom-call | tf_op jit(solution)/shard_map/finish/pallas_call | solution.py:216
  (3 shorter events, 0.1 us)
Async XLA Ops:
  0.6 10.6 %collective-permute-start = (bf16[128,256]{1,0:T(8,128)(2,1)}, bf16[128,256]{1,0:T(8,128)(2,1)S(1)}, u32[]{:S(2)}, u32[]{:S(2)}) collective-permute-start(bf16[128,256]{1,0:T(8,128)(2,1)} %param.5), channel_id=1, source_target_pairs={{0,8},{1,9},{2,10},{3,11},{4,12},{5,13},{6,14},{7,15},{8,0},{9,1},... | collective-permute-start | bytes 196616 | tf_op jit(solution)/shard_map/ppermute | solution.py:194
  3.8 15.6 %all-to-all-start = ((bf16[8,72,256]{2,1,0:T(8,128)(2,1)}), bf16[8,72,256]{2,1,0:T(8,128)(2,1)S(1)}, u32[]{:S(2)}, u32[]{:S(2)}) async-start(bf16[8,72,256]{2,1,0:T(8,128)(2,1)} %repeat.1), calls=%async_computation | async-start | bytes 589824 | tf_op jit(solution)/shard_map/all_to_all | solution.py:193
  11.3 6.7 %collective-permute-start.4 = (bf16[256,256]{1,0:T(8,128)(2,1)S(1)}, bf16[256,256]{1,0:T(8,128)(2,1)S(1)}, u32[]{:S(2)}, u32[]{:S(2)}) collective-permute-start(bf16[256,256]{1,0:T(8,128)(2,1)S(1)} %constant_dynamic-update-slice_fusion), channel_id=1, source_target_pairs={{0,1},{1,0},{2,3},{3,2},{4,5},{5,4},{6,7},{7,6},{8,9},{9,8},{10,11... | collective-permute-start | bytes 393224 | tf_op jit(solution)/shard_map/ppermute | solution.py:198
  11.4 14.0 %collective-permute-start.3 = (bf16[256,256]{1,0:T(8,128)(2,1)S(1)}, bf16[256,256]{1,0:T(8,128)(2,1)S(1)}, u32[]{:S(2)}, u32[]{:S(2)}) collective-permute-start(bf16[256,256]{1,0:T(8,128)(2,1)S(1)} %constant_dynamic-update-slice_fusion), channel_id=1, source_target_pairs={{6,0},{7,1},{0,2},{1,3},{2,4},{3,5},{4,6},{5,7},{14,8},{15,9},{8,1... | collective-permute-start | bytes 393224 | tf_op jit(solution)/shard_map/ppermute | solution.py:196
  13.4 12.0 %collective-permute-start.2 = (bf16[256,256]{1,0:T(8,128)(2,1)S(1)}, bf16[256,256]{1,0:T(8,128)(2,1)S(1)}, u32[]{:S(2)}, u32[]{:S(2)}) collective-permute-start(bf16[256,256]{1,0:T(8,128)(2,1)S(1)} %constant_dynamic-update-slice_fusion), channel_id=1, source_target_pairs={{4,0},{5,1},{6,2},{7,3},{0,4},{1,5},{2,6},{3,7},{12,8},{13,9},{14,... | collective-permute-start | bytes 393224 | tf_op jit(solution)/shard_map/ppermute | solution.py:196
  16.9 8.5 %collective-permute-start.1 = (bf16[256,256]{1,0:T(8,128)(2,1)S(1)}, bf16[256,256]{1,0:T(8,128)(2,1)S(1)}, u32[]{:S(2)}, u32[]{:S(2)}) collective-permute-start(bf16[256,256]{1,0:T(8,128)(2,1)S(1)} %constant_dynamic-update-slice_fusion), channel_id=1, source_target_pairs={{2,0},{3,1},{4,2},{5,3},{6,4},{7,5},{0,6},{1,7},{10,8},{11,9},{12,... | collective-permute-start | bytes 393224 | tf_op jit(solution)/shard_map/ppermute | solution.py:196
  25.4 1.8 %collective-permute-start.5 = (bf16[3,256,256]{2,1,0:T(8,128)(2,1)S(1)}, bf16[3,256,256]{2,1,0:T(8,128)(2,1)S(1)}, u32[]{:S(2)}, u32[]{:S(2)}) collective-permute-start(bf16[3,256,256]{2,1,0:T(8,128)(2,1)S(1)} %stack.1.refs_0_), channel_id=1, source_target_pairs={{0,1},{1,0},{2,3},{3,2},{4,5},{5,4},{6,7},{7,6},{8,9},{9,8},{10,11... | collective-permute-start | bytes 1179656 | tf_op jit(solution)/shard_map/ppermute | solution.py:201
  41.6 12.5 %collective-permute-start.6 = (f32[4,128,256]{2,1,0:T(8,128)S(1)}, f32[4,128,256]{2,1,0:T(8,128)S(1)}, u32[]{:S(2)}, u32[]{:S(2)}) collective-permute-start(f32[4,128,256]{2,1,0:T(8,128)S(1)} %get-tuple-element.40), channel_id=1, source_target_pairs={{0,1},{1,0},{2,3},{3,2},{4,5},{5,4},{6,7},{7,6},{8,9},{9,8},{10,11... | collective-permute-start | bytes 1572872 | tf_op jit(solution)/shard_map/ppermute | solution.py:204
  41.8 17.6 %collective-permute-start.7 = (f32[4,128,256]{2,1,0:T(8,128)S(1)}, f32[4,128,256]{2,1,0:T(8,128)S(1)}, u32[]{:S(2)}, u32[]{:S(2)}) collective-permute-start(f32[4,128,256]{2,1,0:T(8,128)S(1)} %get-tuple-element.44), channel_id=1, source_target_pairs={{0,1},{1,0},{2,3},{3,2},{4,5},{5,4},{6,7},{7,6},{8,9},{9,8},{10,11... | collective-permute-start | bytes 1572872 | tf_op jit(solution)/shard_map/ppermute | solution.py:205
  54.2 9.3 %collective-permute-start.8 = (bf16[4,128,256]{2,1,0:T(8,128)(2,1)S(1)}, bf16[4,128,256]{2,1,0:T(8,128)(2,1)S(1)}, u32[]{:S(2)}, u32[]{:S(2)}) collective-permute-start(bf16[4,128,256]{2,1,0:T(8,128)(2,1)S(1)} %join.1), channel_id=1, source_target_pairs={{0,8},{1,9},{2,10},{3,11},{4,12},{5,13},{6,14},{7,15},{8,0},{9,1},... | collective-permute-start | bytes 786440 | tf_op jit(solution)/shard_map/ppermute | solution.py:209
  55.6 13.2 %all-to-all-start.2 = ((bf16[8,80,256]{2,1,0:T(8,128)(2,1)}), bf16[8,80,256]{2,1,0:T(8,128)(2,1)S(1)}, u32[]{:S(2)}, u32[]{:S(2)}) async-start(bf16[8,80,256]{2,1,0:T(8,128)(2,1)} %pack.1), calls=%async_computation.2 | async-start | bytes 655360 | tf_op jit(solution)/shard_map/all_to_all | solution.py:211
  63.5 5.9 %collective-permute-start.9 = (bf16[128,256]{1,0:T(8,128)(2,1)S(1)}, bf16[128,256]{1,0:T(8,128)(2,1)S(1)}, u32[]{:S(2)}, u32[]{:S(2)}) collective-permute-start(bf16[128,256]{1,0:T(8,128)(2,1)S(1)} %get-tuple-element.47), channel_id=1, source_target_pairs={{4,0},{5,1},{6,2},{7,3},{0,4},{1,5},{2,6},{3,7},{12,8},{13,9},{14,... | collective-permute-start | bytes 196616 | tf_op jit(solution)/shard_map/ppermute | solution.py:214
  64.4 5.7 %collective-permute-start.10 = (bf16[128,256]{1,0:T(8,128)(2,1)S(1)}, bf16[128,256]{1,0:T(8,128)(2,1)S(1)}, u32[]{:S(2)}, u32[]{:S(2)}) collective-permute-start(bf16[128,256]{1,0:T(8,128)(2,1)S(1)} %get-tuple-element.48), channel_id=1, source_target_pairs={{6,0},{7,1},{0,2},{1,3},{2,4},{3,5},{4,6},{5,7},{14,8},{15,9},{8,1... | collective-permute-start | bytes 196616 | tf_op jit(solution)/shard_map/ppermute | solution.py:214
  65.5 4.6 %collective-permute-start.11 = (bf16[128,256]{1,0:T(8,128)(2,1)S(1)}, bf16[128,256]{1,0:T(8,128)(2,1)S(1)}, u32[]{:S(2)}, u32[]{:S(2)}) collective-permute-start(bf16[128,256]{1,0:T(8,128)(2,1)S(1)} %get-tuple-element.49), channel_id=1, source_target_pairs={{2,0},{3,1},{4,2},{5,3},{6,4},{7,5},{0,6},{1,7},{10,8},{11,9},{12,... | collective-permute-start | bytes 196616 | tf_op jit(solution)/shard_map/ppermute | solution.py:214

commit v8 on v6

--- a/solution.py
+++ b/solution.py
@@ -58,14 +58,18 @@
     b = b_ref[...]
     c_half = c_ref[...]
     grad = jnp.zeros((GROUP, R), F32)
+    def model(k):
+        return dot_last((wide * c_half[k : k + 1, :]).astype(BF16), b)
+
+    half = model(0)
     for k in range(K):
-        ck = c_half[k : k + 1, :]
-        half = dot_last((wide * ck).astype(BF16), b)
-        t = jnp.concatenate([r[k, 0] for r in (t0, t1, t2, t3)], axis=0).astype(F32)
+        t = (jnp.concatenate([r[k, 0] for r in (t0, t1, t2, t3)], axis=0)).astype(F32)
         d2 = ((jnp.tanh(half) + 1.0) - (t + t)).astype(BF16)
-        grad = grad + dot(d2, b) * ck
+        if k + 1 < K:
+            half = model(k + 1)
         part = dot(rows_t, d2)
         w_ref[k] = jnp.where(step > 0, w_ref[k], 0.0) + part if last else part
+        grad = grad + dot(d2, b) * c_half[k : k + 1, :]
 
     for slot in range(4):
         parts[slot][0] = grad[slot * SHARD : (slot + 1) * SHARD]

time: 70.9 us -> 70.9 us (level)
  no operation moved by 1% of the time
where the time goes in v8:
time: 70.9 us; the launch traced here: 70.4 us
  starting transfers between devices  25.4 us (36%)
  Pallas kernels  23.4 us (33%)
  blocking collectives  11.9 us (17%)
  waiting for transfers between devices  7.37 us (10%)
  local copies, waits for them, and re-layouts  0.85 us (1%)
  between operations  0.72 us (1%)
    pallas_call x2, Pallas kernels, local(): pl.pallas_call(functools.partial(body, last), grid_spec=pltpu.PrefetchSca...  20.3 us
    all_to_all x1, blocking collectives, on_device(): times = lax.all_to_all(times, 'space', 0, 0)  11.9 us
    all_to_all x1, starting transfers between devices, on_device(): b_full = lax.all_to_all(b_wide, 'samples', 0, 0).reshape(NJ, R)  6.64 us
    ppermute x3, starting transfers between devices, on_device(): lax.ppermute(pair, 'space', from_z(d))  6.51 us
    all_to_all x1, starting transfers between devices, on_device(): first = lax.all_to_all(first, 'samples', 0, 0)  4.71 us
    ppermute x3, starting transfers between devices, on_device(): away = [lax.ppermute(x, 'space', from_z(-d)) for d, x in zip(AWAY, away)]  4.47 us
    ppermute x1, waiting for transfers between devices, on_device(): across = lax.ppermute(across, 'space', TO_XL)  2.77 us
    all_to_all x1, waiting for transfers between devices, on_device(): first = lax.all_to_all(first, 'samples', 0, 0)  2.11 us
  transfers between devices with their start and end apart: 14, of which 5 were waited for; matrix products, arithmetic and copies ran while one was open for 2% of the time, Pallas kernels for 12%

profile of v8, /device:TPU:0, one launch (start us, length us, event | category | flops | bytes accessed | tf_op | source)
XLA Modules:
  0.0 70.4 jit_solution(1362828919127475546)
XLA Ops:
  0.6 1.7 %collective-permute-start = (bf16[128,256]{1,0:T(8,128)(2,1)}, bf16[128,256]{1,0:T(8,128)(2,1)S(1)}, u32[]{:S(2)}, u32[]{:S(2)}) collective-permute-start(bf16[128,256]{1,0:T(8,128)(2,1)} %param.5), channel_id=1, source_target_pairs={{0,8},{1,9},{2,10},{3,11},{4,12},{5,13},{6,14},{7,15},{8,0},{9,1},... | collective-permute-start | bytes 196616 | tf_op jit(solution)/shard_map/ppermute | solution.py:197
  2.3 1.5 %repeat.1 = bf16[8,64,256]{2,1,0:T(8,128)(2,1)} custom-call(bf16[64,256]{1,0:T(8,128)(2,1)} %x_ref.1), custom_call_target="tpu_custom_call" | custom-call | tf_op jit(solution)/shard_map/repeat/pallas_call | solution.py:194
  3.8 6.6 %all-to-all-start = ((bf16[8,64,256]{2,1,0:T(8,128)(2,1)}), bf16[8,64,256]{2,1,0:T(8,128)(2,1)S(1)}, u32[]{:S(2)}, u32[]{:S(2)}) async-start(bf16[8,64,256]{2,1,0:T(8,128)(2,1)} %repeat.1), calls=%async_computation | async-start | bytes 524288 | tf_op jit(solution)/shard_map/all_to_all | solution.py:195
  10.4 0.8 %constant_dynamic-update-slice_fusion.1 = bf16[256,256]{1,0:T(8,128)(2,1)S(1)} fusion(bf16[128,256]{1,0:T(8,128)(2,1)} %param.5), kind=kLoop, calls=%fused_computation.2 | loop fusion | bytes 131072
  11.2 0.0 collective-permute-done
  11.3 0.1 collective-permute-start.4
  11.4 0.7 convert_multiply_fusion.refs_3_
  12.0 1.9 %collective-permute-start.3 = (bf16[256,256]{1,0:T(8,128)(2,1)S(1)}, bf16[256,256]{1,0:T(8,128)(2,1)S(1)}, u32[]{:S(2)}, u32[]{:S(2)}) collective-permute-start(bf16[256,256]{1,0:T(8,128)(2,1)S(1)} %constant_dynamic-update-slice_fusion), channel_id=1, source_target_pairs={{6,0},{7,1},{0,2},{1,3},{2,4},{3,5},{4,6},{5,7},{14,8},{15,9},{8,1... | collective-permute-start | bytes 393224 | tf_op jit(solution)/shard_map/ppermute | solution.py:199
  14.0 3.6 %collective-permute-start.2 = (bf16[256,256]{1,0:T(8,128)(2,1)S(1)}, bf16[256,256]{1,0:T(8,128)(2,1)S(1)}, u32[]{:S(2)}, u32[]{:S(2)}) collective-permute-start(bf16[256,256]{1,0:T(8,128)(2,1)S(1)} %constant_dynamic-update-slice_fusion), channel_id=1, source_target_pairs={{4,0},{5,1},{6,2},{7,3},{0,4},{1,5},{2,6},{3,7},{12,8},{13,9},{14,... | collective-permute-start | bytes 393224 | tf_op jit(solution)/shard_map/ppermute | solution.py:199
  17.5 1.0 %collective-permute-start.1 = (bf16[256,256]{1,0:T(8,128)(2,1)S(1)}, bf16[256,256]{1,0:T(8,128)(2,1)S(1)}, u32[]{:S(2)}, u32[]{:S(2)}) collective-permute-start(bf16[256,256]{1,0:T(8,128)(2,1)S(1)} %constant_dynamic-update-slice_fusion), channel_id=1, source_target_pairs={{2,0},{3,1},{4,2},{5,3},{6,4},{7,5},{0,6},{1,7},{10,8},{11,9},{12,... | collective-permute-start | bytes 393224 | tf_op jit(solution)/shard_map/ppermute | solution.py:199
  18.6 0.0 collective-permute-done.4
  18.6 0.6 all-to-all-done
  19.2 6.0 %begin.1 = (f32[4,128,256]{2,1,0:T(8,128)S(1)}, f32[4,128,256]{2,1,0:T(8,128)S(1)}, f32[4,128,256]{2,1,0:T(8,128)S(1)}, f32[4,128,256]{2,1,0:T(8,128)S(1)}, f32[...) custom-call(s32[1]{0:T(128)} %bitcast.place, bf16[8,16,128,512]{3,2,1,0:T(8,128)(2,1)} %bitcast.9, ...), custom_call_target="tpu_custom_call" | custom-call | flops 3230000128 | bytes 5500000 | tf_op jit(solution)/shard_map/begin/pallas_call | solution.py:123
  25.2 0.0 collective-permute-done.3.refs_2_
  25.2 0.0 collective-permute-done.2.refs_1_
  25.2 0.0 collective-permute-done.1.refs_0_
  25.2 0.1 collective-permute-start.5
  25.3 1.7 %collective-permute-done.5.refs_1_ = bf16[3,256,256]{2,1,0:T(8,128)(2,1)S(1)} collective-permute-done((bf16[3,256,256]{2,1,0:T(8,128)(2,1)S(1)}, bf16[3,256,256]{2,1,0:T(8,128)(2,1)S(1)}, u32[]{:S(2)}, u32[]{:S(2)}) %collective-permute-start.5) | collective-permute-done | bytes 393248 | tf_op jit(solution)/shard_map/ppermute | solution.py:204
  27.0 14.4 %rest.1 = (f32[4,128,256]{2,1,0:T(8,128)S(1)}, f32[4,128,256]{2,1,0:T(8,128)S(1)}, f32[4,128,256]{2,1,0:T(8,128)S(1)}, f32[4,128,256]{2,1,0:T(8,128)S(1)}, bf16[...) custom-call(s32[1]{0:T(128)} %bitcast.place, ...), custom_call_target="tpu_custom_call", output_to_operand_aliasing={{0}: (11, {}), {1}: (12, {}), {2}: (13, {}), {3}: (14, {})} | custom-call | flops 9690000384 | bytes 16500000 | tf_op jit(solution)/shard_map/rest/pallas_call | solution.py:123
  41.4 0.2 collective-permute-start.6
  41.6 0.4 collective-permute-start.7
  42.0 11.9 %all_to_all.15.times_ref = bf16[16,16,256]{2,1,0:T(8,128)(2,1)S(1)} all-to-all(bf16[16,16,256]{2,1,0:T(8,128)(2,1)S(1)} %get-tuple-element.39), channel_id=1, replica_groups=mesh['samples'=8,'space'=16] {'space'}, dimensions={0} | all-to-all | bytes 262144 | tf_op jit(solution)/shard_map/all_to_all | solution.py:209
  53.9 0.0 collective-permute-done.6.y_ref
  54.0 0.6 collective-permute-start.8
  54.6 0.8 %pack.1 = bf16[8,80,256]{2,1,0:T(8,128)(2,1)} custom-call(bf16[16,16,256]{2,1,0:T(8,128)(2,1)S(1)} %all_to_all.15.times_ref, bf16[512,256]{1,0:T(8,128)(2,1)S(1)} %get-tuple-element.42.gb_ref), custom_call_target="tpu_custom_call" | custom-call | tf_op jit(solution)/shard_map/pack/pallas_call | solution.py:213
  55.4 4.7 %all-to-all-start.2 = ((bf16[8,80,256]{2,1,0:T(8,128)(2,1)}), bf16[8,80,256]{2,1,0:T(8,128)(2,1)S(1)}, u32[]{:S(2)}, u32[]{:S(2)}) async-start(bf16[8,80,256]{2,1,0:T(8,128)(2,1)} %pack.1), calls=%async_computation.2 | async-start | bytes 655360 | tf_op jit(solution)/shard_map/all_to_all | solution.py:214
  60.1 0.0 collective-permute-done.7.y_ref
  60.1 2.8 %collective-permute-done.8.across_ref = bf16[4,128,256]{2,1,0:T(8,128)(2,1)S(1)} collective-permute-done((bf16[4,128,256]{2,1,0:T(8,128)(2,1)S(1)}, bf16[4,128,256]{2,1,0:T(8,128)(2,1)S(1)}, u32[]{:S(2)}, u32[]{:S(2)}) %collective-permute-start.8) | collective-permute-done | bytes 262176 | tf_op jit(solution)/shard_map/ppermute | solution.py:212
  62.9 0.1 spread.1
  62.9 1.2 %collective-permute-start.9 = (bf16[128,256]{1,0:T(8,128)(2,1)S(1)}, bf16[128,256]{1,0:T(8,128)(2,1)S(1)}, u32[]{:S(2)}, u32[]{:S(2)}) collective-permute-start(bf16[128,256]{1,0:T(8,128)(2,1)S(1)} %get-tuple-element.47), channel_id=1, source_target_pairs={{4,0},{5,1},{6,2},{7,3},{0,4},{1,5},{2,6},{3,7},{12,8},{13,9},{14,... | collective-permute-start | bytes 196616 | tf_op jit(solution)/shard_map/ppermute | solution.py:217
  64.2 1.1 %collective-permute-start.10 = (bf16[128,256]{1,0:T(8,128)(2,1)S(1)}, bf16[128,256]{1,0:T(8,128)(2,1)S(1)}, u32[]{:S(2)}, u32[]{:S(2)}) collective-permute-start(bf16[128,256]{1,0:T(8,128)(2,1)S(1)} %get-tuple-element.48), channel_id=1, source_target_pairs={{6,0},{7,1},{0,2},{1,3},{2,4},{3,5},{4,6},{5,7},{14,8},{15,9},{8,1... | collective-permute-start | bytes 196616 | tf_op jit(solution)/shard_map/ppermute | solution.py:217
  65.2 2.1 %collective-permute-start.11 = (bf16[128,256]{1,0:T(8,128)(2,1)S(1)}, bf16[128,256]{1,0:T(8,128)(2,1)S(1)}, u32[]{:S(2)}, u32[]{:S(2)}) collective-permute-start(bf16[128,256]{1,0:T(8,128)(2,1)S(1)} %get-tuple-element.49), channel_id=1, source_target_pairs={{2,0},{3,1},{4,2},{5,3},{6,4},{7,5},{0,6},{1,7},{10,8},{11,9},{12,... | collective-permute-start | bytes 196616 | tf_op jit(solution)/shard_map/ppermute | solution.py:217
  67.4 2.1 %all-to-all-done.2.first_ref = bf16[8,80,256]{2,1,0:T(8,128)(2,1)S(1)} async-done(((bf16[8,80,256]{2,1,0:T(8,128)(2,1)}), bf16[8,80,256]{2,1,0:T(8,128)(2,1)S(1)}, u32[]{:S(2)}, u32[]{:S(2)}) %all-to-all-start.2) | async-done | bytes 327712 | tf_op jit(solution)/shard_map/all_to_all | solution.py:214
  69.5 0.0 collective-permute-done.9.g1
  69.5 0.1 collective-permute-done.10.g2
  69.6 0.0 collective-permute-done.11.g3
  69.6 0.7 %finish.1 = (f32[128,256]{1,0:T(8,128)}, f32[64,256]{1,0:T(8,128)}, f32[8,256]{1,0:T(8,128)}) custom-call(bf16[8,80,256]{2,1,0:T(8,128)(2,1)S(1)} %all-to-all-done.2.first_ref, f32[128,256]{1,0:T(8,128)S(1)} %get-tuple-element.51.own_ref, bf16[128,256]{1,0:T(8,128)(2,1)S(1)} %collective-permute-done.9.g1, bf16[128,256]{1,0:T(8,128)(2,1)S(1)} %collective-permute-done.10.g2, ...), custom_call_target="tpu_custom_call" | custom-call | tf_op jit(solution)/shard_map/finish/pallas_call | solution.py:219
  (3 shorter events, 0.1 us)
Async XLA Ops:
  0.6 10.6 %collective-permute-start = (bf16[128,256]{1,0:T(8,128)(2,1)}, bf16[128,256]{1,0:T(8,128)(2,1)S(1)}, u32[]{:S(2)}, u32[]{:S(2)}) collective-permute-start(bf16[128,256]{1,0:T(8,128)(2,1)} %param.5), channel_id=1, source_target_pairs={{0,8},{1,9},{2,10},{3,11},{4,12},{5,13},{6,14},{7,15},{8,0},{9,1},... | collective-permute-start | bytes 196616 | tf_op jit(solution)/shard_map/ppermute | solution.py:197
  3.8 15.4 %all-to-all-start = ((bf16[8,64,256]{2,1,0:T(8,128)(2,1)}), bf16[8,64,256]{2,1,0:T(8,128)(2,1)S(1)}, u32[]{:S(2)}, u32[]{:S(2)}) async-start(bf16[8,64,256]{2,1,0:T(8,128)(2,1)} %repeat.1), calls=%async_computation | async-start | bytes 524288 | tf_op jit(solution)/shard_map/all_to_all | solution.py:195
  11.3 7.3 %collective-permute-start.4 = (bf16[256,256]{1,0:T(8,128)(2,1)S(1)}, bf16[256,256]{1,0:T(8,128)(2,1)S(1)}, u32[]{:S(2)}, u32[]{:S(2)}) collective-permute-start(bf16[256,256]{1,0:T(8,128)(2,1)S(1)} %constant_dynamic-update-slice_fusion), channel_id=1, source_target_pairs={{0,1},{1,0},{2,3},{3,2},{4,5},{5,4},{6,7},{7,6},{8,9},{9,8},{10,11... | collective-permute-start | bytes 393224 | tf_op jit(solution)/shard_map/ppermute | solution.py:201
  12.0 13.1 %collective-permute-start.3 = (bf16[256,256]{1,0:T(8,128)(2,1)S(1)}, bf16[256,256]{1,0:T(8,128)(2,1)S(1)}, u32[]{:S(2)}, u32[]{:S(2)}) collective-permute-start(bf16[256,256]{1,0:T(8,128)(2,1)S(1)} %constant_dynamic-update-slice_fusion), channel_id=1, source_target_pairs={{6,0},{7,1},{0,2},{1,3},{2,4},{3,5},{4,6},{5,7},{14,8},{15,9},{8,1... | collective-permute-start | bytes 393224 | tf_op jit(solution)/shard_map/ppermute | solution.py:199
  14.0 11.2 %collective-permute-start.2 = (bf16[256,256]{1,0:T(8,128)(2,1)S(1)}, bf16[256,256]{1,0:T(8,128)(2,1)S(1)}, u32[]{:S(2)}, u32[]{:S(2)}) collective-permute-start(bf16[256,256]{1,0:T(8,128)(2,1)S(1)} %constant_dynamic-update-slice_fusion), channel_id=1, source_target_pairs={{4,0},{5,1},{6,2},{7,3},{0,4},{1,5},{2,6},{3,7},{12,8},{13,9},{14,... | collective-permute-start | bytes 393224 | tf_op jit(solution)/shard_map/ppermute | solution.py:199
  17.5 7.6 %collective-permute-start.1 = (bf16[256,256]{1,0:T(8,128)(2,1)S(1)}, bf16[256,256]{1,0:T(8,128)(2,1)S(1)}, u32[]{:S(2)}, u32[]{:S(2)}) collective-permute-start(bf16[256,256]{1,0:T(8,128)(2,1)S(1)} %constant_dynamic-update-slice_fusion), channel_id=1, source_target_pairs={{2,0},{3,1},{4,2},{5,3},{6,4},{7,5},{0,6},{1,7},{10,8},{11,9},{12,... | collective-permute-start | bytes 393224 | tf_op jit(solution)/shard_map/ppermute | solution.py:199
  25.2 1.8 %collective-permute-start.5 = (bf16[3,256,256]{2,1,0:T(8,128)(2,1)S(1)}, bf16[3,256,256]{2,1,0:T(8,128)(2,1)S(1)}, u32[]{:S(2)}, u32[]{:S(2)}) collective-permute-start(bf16[3,256,256]{2,1,0:T(8,128)(2,1)S(1)} %stack.1.refs_0_), channel_id=1, source_target_pairs={{0,1},{1,0},{2,3},{3,2},{4,5},{5,4},{6,7},{7,6},{8,9},{9,8},{10,11... | collective-permute-start | bytes 1179656 | tf_op jit(solution)/shard_map/ppermute | solution.py:204
  41.4 12.5 %collective-permute-start.6 = (f32[4,128,256]{2,1,0:T(8,128)S(1)}, f32[4,128,256]{2,1,0:T(8,128)S(1)}, u32[]{:S(2)}, u32[]{:S(2)}) collective-permute-start(f32[4,128,256]{2,1,0:T(8,128)S(1)} %get-tuple-element.40), channel_id=1, source_target_pairs={{0,1},{1,0},{2,3},{3,2},{4,5},{5,4},{6,7},{7,6},{8,9},{9,8},{10,11... | collective-permute-start | bytes 1572872 | tf_op jit(solution)/shard_map/ppermute | solution.py:207
  41.6 18.5 %collective-permute-start.7 = (f32[4,128,256]{2,1,0:T(8,128)S(1)}, f32[4,128,256]{2,1,0:T(8,128)S(1)}, u32[]{:S(2)}, u32[]{:S(2)}) collective-permute-start(f32[4,128,256]{2,1,0:T(8,128)S(1)} %get-tuple-element.44), channel_id=1, source_target_pairs={{0,1},{1,0},{2,3},{3,2},{4,5},{5,4},{6,7},{7,6},{8,9},{9,8},{10,11... | collective-permute-start | bytes 1572872 | tf_op jit(solution)/shard_map/ppermute | solution.py:208
  54.0 8.9 %collective-permute-start.8 = (bf16[4,128,256]{2,1,0:T(8,128)(2,1)S(1)}, bf16[4,128,256]{2,1,0:T(8,128)(2,1)S(1)}, u32[]{:S(2)}, u32[]{:S(2)}) collective-permute-start(bf16[4,128,256]{2,1,0:T(8,128)(2,1)S(1)} %join.1), channel_id=1, source_target_pairs={{0,8},{1,9},{2,10},{3,11},{4,12},{5,13},{6,14},{7,15},{8,0},{9,1},... | collective-permute-start | bytes 786440 | tf_op jit(solution)/shard_map/ppermute | solution.py:212
  55.4 14.1 %all-to-all-start.2 = ((bf16[8,80,256]{2,1,0:T(8,128)(2,1)}), bf16[8,80,256]{2,1,0:T(8,128)(2,1)S(1)}, u32[]{:S(2)}, u32[]{:S(2)}) async-start(bf16[8,80,256]{2,1,0:T(8,128)(2,1)} %pack.1), calls=%async_computation.2 | async-start | bytes 655360 | tf_op jit(solution)/shard_map/all_to_all | solution.py:214
  62.9 6.6 %collective-permute-start.9 = (bf16[128,256]{1,0:T(8,128)(2,1)S(1)}, bf16[128,256]{1,0:T(8,128)(2,1)S(1)}, u32[]{:S(2)}, u32[]{:S(2)}) collective-permute-start(bf16[128,256]{1,0:T(8,128)(2,1)S(1)} %get-tuple-element.47), channel_id=1, source_target_pairs={{4,0},{5,1},{6,2},{7,3},{0,4},{1,5},{2,6},{3,7},{12,8},{13,9},{14,... | collective-permute-start | bytes 196616 | tf_op jit(solution)/shard_map/ppermute | solution.py:217
  64.2 5.5 %collective-permute-start.10 = (bf16[128,256]{1,0:T(8,128)(2,1)S(1)}, bf16[128,256]{1,0:T(8,128)(2,1)S(1)}, u32[]{:S(2)}, u32[]{:S(2)}) collective-permute-start(bf16[128,256]{1,0:T(8,128)(2,1)S(1)} %get-tuple-element.48), channel_id=1, source_target_pairs={{6,0},{7,1},{0,2},{1,3},{2,4},{3,5},{4,6},{5,7},{14,8},{15,9},{8,1... | collective-permute-start | bytes 196616 | tf_op jit(solution)/shard_map/ppermute | solution.py:217
  65.2 4.4 %collective-permute-start.11 = (bf16[128,256]{1,0:T(8,128)(2,1)S(1)}, bf16[128,256]{1,0:T(8,128)(2,1)S(1)}, u32[]{:S(2)}, u32[]{:S(2)}) collective-permute-start(bf16[128,256]{1,0:T(8,128)(2,1)S(1)} %get-tuple-element.49), channel_id=1, source_target_pairs={{2,0},{3,1},{4,2},{5,3},{6,4},{7,5},{0,6},{1,7},{10,8},{11,9},{12,... | collective-permute-start | bytes 196616 | tf_op jit(solution)/shard_map/ppermute | solution.py:217
